TPU v7x, 32 devices: a whole 2x2x4 slice. The times are simulated.
32 devices in a mesh: dp: 2 (over x), fsdp: 16 (over z, y, core).
Axes of the slice: x: 2, y: 2, z: 4, core: 2. Of those that a mesh axis runs over, the one named last changes fastest.
Arguments:
- tokens: bfloat16 [32, 1024, 768], P(('dp', 'fsdp')), may hold values from -6 to 6
- segments: int32 [32, 1024], P(('dp', 'fsdp')), may hold values from -1 to 12, as said below
- thresholds: float32 [32], P(('dp', 'fsdp')), may hold values from 0.25 to 6
- qkv_weight: bfloat16 [768, 2304], P(('dp', 'fsdp')), may hold values from -0.21650635 to 0.21650635
- out_weight: bfloat16 [768, 768], P(('dp', 'fsdp')), may hold values from -0.4375 to 0.4375
- up_weight: bfloat16 [768, 3072], P(('dp', 'fsdp')), may hold values from -0.21875 to 0.21875
- down_weight: bfloat16 [3072, 768], P(('dp', 'fsdp')), may hold values from -0.109375 to 0.109375
- attn_gain: bfloat16 [768], P(('dp', 'fsdp')), may hold values from 0.5 to 1.5
- attn_shift: bfloat16 [768], P(('dp', 'fsdp')), may hold values from -1.1953125 to 1.1953125
- mlp_gain: bfloat16 [768], P(('dp', 'fsdp')), may hold values from 0.5 to 1.5
- mlp_shift: bfloat16 [768], P(('dp', 'fsdp')), may hold values from -1.1953125 to 1.1953125
- cotangent: bfloat16 [32, 1024, 768], P(('dp', 'fsdp')), may hold values from -6 to 6
Outputs:
- output: bfloat16 [32, 1024, 768], P(('dp', 'fsdp'))
- grad_tokens: float32 [32, 1024, 768], P(('dp', 'fsdp'))
- grad_qkv: float32 [768, 2304], P(('dp', 'fsdp'))
- grad_out: float32 [768, 768], P(('dp', 'fsdp'))
- grad_up: float32 [768, 3072], P(('dp', 'fsdp'))
- grad_down: float32 [3072, 768], P(('dp', 'fsdp'))
- grad_attn_gain: float32 [768], P(('dp', 'fsdp'))
- grad_attn_shift: float32 [768], P(('dp', 'fsdp'))
- grad_mlp_gain: float32 [768], P(('dp', 'fsdp'))
- grad_mlp_shift: float32 [768], P(('dp', 'fsdp'))
- fraction: float32 [], replicated
Inputs may be any that keep to these rules, and one draw needn't show every extreme that they name: `segments`: in each packed row the document numbers start at 0 and never fall; every document has 1 to 256 tokens and one document of exactly 256 tokens lies in every row; each row ends in 1 to 255 padding tokens marked -1.
All inputs are finite; a program needn't handle non-finite values.
Results may differ from a plain program's by a relative error of at most 0.011.
The roundings to bfloat16 on the way count: a program that leaves them out, or rounds other values in their place, can miss the bound.
Values may be sent and summed in bfloat16 or wider, within the bound.
No kernel may reach another device: no remote copies, remote signals or barrier semaphores. Data moves between devices by JAX's collectives and lax.ppermute only.
A program may use at most 256 MiB of HBM per device.

v0:
```python
import jax
import jax.numpy as jnp
from jax import lax
from jax.sharding import PartitionSpec as P

HEADS = 12
HD = 64


EPSILON = 1e-05
NEGATIVE = -1e30
SOFT_WIDTH = 0.25


def norm_forward(values, gain, shift):
    center = values - jnp.mean(values, axis=-1, keepdims=True)
    spread = jnp.mean(center * center, axis=-1, keepdims=True)
    inverse = lax.rsqrt(spread + EPSILON)
    unit = center * inverse
    return (unit * gain + shift, unit, inverse)


def norm_backward(grad_normed, unit, inverse, gain):
    grad_unit = grad_normed * gain
    grad_gain = jnp.sum(grad_normed * unit, axis=0)
    grad_shift = jnp.sum(grad_normed, axis=0)
    centered = grad_unit - jnp.mean(grad_unit, axis=-1, keepdims=True)
    grad_input = inverse * (centered - unit * jnp.mean(grad_unit * unit, axis=-1, keepdims=True))
    return (grad_input, grad_gain, grad_shift)


def pair_masks(seg_row):
    length = seg_row.shape[0]
    places = jnp.arange(length)
    same = seg_row[:, None] == seg_row[None, :]
    earlier = places[None, :] < places[:, None]
    key_live = seg_row[None, :] >= 0
    strict = same & earlier & key_live
    allowed = strict | (places[:, None] == places[None, :])
    return (allowed, strict)


def shifted_sum(select):
    running = jnp.cumsum(select, axis=0)
    return jnp.concatenate([jnp.zeros((1, select.shape[1]), jnp.float32), running[:-1]], axis=0)


def split_heads(project_row):
    length = project_row.shape[0]
    return project_row.reshape(length, 3, HEADS, HD).transpose(1, 2, 0, 3)


def head_scores(query_head, key_head):
    return jnp.dot(query_head, key_head.T, preferred_element_type=jnp.float32) * HD ** (-0.5)


def soft_forward(scores, selsum, allowed, value_head):
    logits = jnp.where(allowed, scores - selsum, NEGATIVE)
    top = jnp.max(logits, axis=-1, keepdims=True)
    expo = jnp.exp(logits - top)
    total = jnp.sum(expo, axis=-1, keepdims=True)
    probs = (expo / total).astype(jnp.bfloat16)
    mixed = jnp.dot(probs, value_head, preferred_element_type=jnp.float32).astype(jnp.bfloat16)
    return (mixed, top[:, 0] + jnp.log(total[:, 0]))


def attend_row(project_row, seg_row, limit):
    allowed, strict = pair_masks(seg_row)
    parts = split_heads(project_row)
    queries, keys_all, values_all = (parts[0], parts[1], parts[2])
    first = head_scores(queries[0], keys_all[0])
    selsum = shifted_sum(jnp.where(strict, jnp.maximum(first, 0.0), 0.0))
    mixed_first, lse_first = soft_forward(first, selsum, allowed, values_all[0])

    def attend_one_head(carry, item):
        query_head, key_head, value_head = item
        scores = head_scores(query_head, key_head)
        return (carry, soft_forward(scores, selsum, allowed, value_head))

    unused, (mixed_rest, lse_rest) = lax.scan(
        attend_one_head, None, (queries[1:], keys_all[1:], values_all[1:])
    )
    mixed_heads = jnp.concatenate([mixed_first[None], mixed_rest], axis=0)
    lse_heads = jnp.concatenate([lse_first[None], lse_rest], axis=0)
    length = seg_row.shape[0]
    mixed_row = mixed_heads.transpose(1, 0, 2).reshape(length, HEADS * HD)
    soft = jnp.sum(jnp.where(strict, jax.nn.sigmoid((selsum - limit) / SOFT_WIDTH), 0.0))
    pairs = jnp.sum(strict.astype(jnp.float32))
    return (mixed_row, lse_heads, soft, pairs)


def soft_back(scores, selsum, allowed, value_head, grad_head, lse_head):
    logits = jnp.where(allowed, scores - selsum, NEGATIVE)
    probs = jnp.exp(logits - lse_head[:, None])
    grad_probs = jnp.dot(grad_head, value_head.T, preferred_element_type=jnp.float32)
    inner = jnp.sum(probs * grad_probs, axis=-1, keepdims=True)
    grad_logits = probs * (grad_probs - inner)
    grad_value = jnp.dot(
        probs.astype(jnp.bfloat16).T, grad_head, preferred_element_type=jnp.float32
    )
    return (grad_logits, grad_value)


def query_key_grads(grad_scores, query_head, key_head):
    scale = HD ** (-0.5)
    grad_query = jnp.dot(grad_scores, key_head, preferred_element_type=jnp.float32) * scale
    grad_key = jnp.dot(grad_scores.T, query_head, preferred_element_type=jnp.float32) * scale
    return (grad_query, grad_key)


def row_back(project_row, grad_row, lse_row, seg_row):
    length = seg_row.shape[0]
    allowed, strict = pair_masks(seg_row)
    parts = split_heads(project_row)
    queries, keys_all, values_all = (parts[0], parts[1], parts[2])
    grad_heads = grad_row.reshape(length, HEADS, HD).transpose(1, 0, 2)
    first = head_scores(queries[0], keys_all[0])
    selsum = shifted_sum(jnp.where(strict, jnp.maximum(first, 0.0), 0.0))
    grad_first, grad_value_first = soft_back(
        first, selsum, allowed, values_all[0], grad_heads[0], lse_row[0]
    )

    def row_one_head(carry, item):
        query_head, key_head, value_head, grad_head, lse_head = item
        scores = head_scores(query_head, key_head)
        grad_logits, grad_value = soft_back(
            scores, selsum, allowed, value_head, grad_head, lse_head
        )
        grad_query, grad_key = query_key_grads(
            grad_logits.astype(jnp.bfloat16), query_head, key_head
        )
        return (carry - grad_logits, (grad_query, grad_key, grad_value))

    grad_selsum, (grad_queries, grad_keys, grad_values) = lax.scan(
        row_one_head,
        -grad_first,
        (queries[1:], keys_all[1:], values_all[1:], grad_heads[1:], lse_row[1:]),
    )
    later = jnp.cumsum(grad_selsum[::-1], axis=0)[::-1]
    grad_select = jnp.concatenate([later[1:], jnp.zeros((1, length), jnp.float32)], axis=0)
    grad_scores_first = (grad_first + jnp.where(strict & (first > 0.0), grad_select, 0.0)).astype(
        jnp.bfloat16
    )
    grad_query_first, grad_key_first = query_key_grads(grad_scores_first, queries[0], keys_all[0])
    all_queries = jnp.concatenate([grad_query_first[None], grad_queries], axis=0)
    all_keys = jnp.concatenate([grad_key_first[None], grad_keys], axis=0)
    all_values = jnp.concatenate([grad_value_first[None], grad_values], axis=0)
    stacked = jnp.stack([all_queries, all_keys, all_values])
    return stacked.transpose(2, 0, 1, 3).reshape(length, 3 * HEADS * HD).astype(jnp.bfloat16)


def body(
    tokens,
    segments,
    thresholds,
    qkv_weight,
    out_weight,
    up_weight,
    down_weight,
    attn_gain,
    attn_shift,
    mlp_gain,
    mlp_shift,
    cotangent,
):
    rows_here, length, width = tokens.shape
    qkv_full, out_full, gain_one, shift_one = (
        lax.all_gather(qkv_weight, ("dp", "fsdp"), axis=0, tiled=True),
        lax.all_gather(out_weight, ("dp", "fsdp"), axis=0, tiled=True),
        lax.all_gather(attn_gain, ("dp", "fsdp"), axis=0, tiled=True),
        lax.all_gather(attn_shift, ("dp", "fsdp"), axis=0, tiled=True),
    )
    flat = tokens.astype(jnp.float32).reshape(rows_here * length, width)
    normed_float, unit_one, inverse_one = norm_forward(
        flat, gain_one.astype(jnp.float32), shift_one.astype(jnp.float32)
    )
    normed = normed_float.astype(jnp.bfloat16)
    project = jnp.dot(normed, qkv_full, preferred_element_type=jnp.float32).astype(jnp.bfloat16)
    project_rows = project.reshape(rows_here, length, 3 * width)
    mixed, lse_all, soft, pairs = lax.map(
        lambda item: attend_row(item[0], item[1], item[2]), (project_rows, segments, thresholds)
    )
    mixed_flat = mixed.reshape(rows_here * length, width)
    middle = flat + jnp.dot(mixed_flat, out_full, preferred_element_type=jnp.float32)
    up_full, down_full, gain_two, shift_two = (
        lax.all_gather(up_weight, ("dp", "fsdp"), axis=0, tiled=True),
        lax.all_gather(down_weight, ("dp", "fsdp"), axis=0, tiled=True),
        lax.all_gather(mlp_gain, ("dp", "fsdp"), axis=0, tiled=True),
        lax.all_gather(mlp_shift, ("dp", "fsdp"), axis=0, tiled=True),
    )
    normed_two_float, unit_two, inverse_two = norm_forward(
        middle, gain_two.astype(jnp.float32), shift_two.astype(jnp.float32)
    )
    normed_two = normed_two_float.astype(jnp.bfloat16)
    hidden = jnp.dot(normed_two, up_full, preferred_element_type=jnp.float32)
    active = jax.nn.gelu(hidden, approximate=True).astype(jnp.bfloat16)
    result = middle + jnp.dot(active, down_full, preferred_element_type=jnp.float32)
    output = result.astype(jnp.bfloat16).reshape(rows_here, length, width)
    totals = lax.psum((jnp.sum(soft), jnp.sum(pairs)), ("dp", "fsdp"))
    fraction = totals[0] / totals[1]
    up_back, down_back, gain_back_two = (up_full, down_full, gain_two)
    live = segments >= 0
    grad_seed = jnp.where(live[:, :, None], cotangent, jnp.zeros_like(cotangent)).reshape(
        rows_here * length, width
    )
    grad_down = jnp.dot(active.T, grad_seed, preferred_element_type=jnp.float32)
    grad_active = jnp.dot(grad_seed, down_back.T, preferred_element_type=jnp.float32)
    unused_value, gelu_pull = jax.vjp(lambda values: jax.nn.gelu(values, approximate=True), hidden)
    grad_hidden = gelu_pull(grad_active)[0].astype(jnp.bfloat16)
    grad_up = jnp.dot(normed_two.T, grad_hidden, preferred_element_type=jnp.float32)
    grad_normed_two = jnp.dot(grad_hidden, up_back.T, preferred_element_type=jnp.float32)
    grad_middle_part, grad_gain_two, grad_shift_two = norm_backward(
        grad_normed_two, unit_two, inverse_two, gain_back_two.astype(jnp.float32)
    )
    grad_middle = grad_seed.astype(jnp.float32) + grad_middle_part
    mlp_grads = (
        lax.psum_scatter(grad_up, ("dp", "fsdp"), scatter_dimension=0, tiled=True),
        lax.psum_scatter(grad_down, ("dp", "fsdp"), scatter_dimension=0, tiled=True),
        lax.psum_scatter(grad_gain_two, ("dp", "fsdp"), scatter_dimension=0, tiled=True),
        lax.psum_scatter(grad_shift_two, ("dp", "fsdp"), scatter_dimension=0, tiled=True),
    )
    qkv_back, out_back, gain_back_one = (qkv_full, out_full, gain_one)
    grad_branch = grad_middle.astype(jnp.bfloat16)
    grad_out = jnp.dot(mixed_flat.T, grad_branch, preferred_element_type=jnp.float32)
    grad_mixed = jnp.dot(grad_branch, out_back.T, preferred_element_type=jnp.float32).astype(
        jnp.bfloat16
    )
    grad_project = lax.map(
        lambda item: row_back(item[0], item[1], item[2], item[3]),
        (project_rows, grad_mixed.reshape(rows_here, length, width), lse_all, segments),
    )
    grad_project = grad_project.reshape(rows_here * length, 3 * width)
    grad_qkv = jnp.dot(normed.T, grad_project, preferred_element_type=jnp.float32)
    grad_normed = jnp.dot(grad_project, qkv_back.T, preferred_element_type=jnp.float32)
    grad_input_part, grad_gain_one, grad_shift_one = norm_backward(
        grad_normed, unit_one, inverse_one, gain_back_one.astype(jnp.float32)
    )
    grad_tokens = (grad_middle + grad_input_part).reshape(rows_here, length, width)
    attn_grads = (
        lax.psum_scatter(grad_qkv, ("dp", "fsdp"), scatter_dimension=0, tiled=True),
        lax.psum_scatter(grad_out, ("dp", "fsdp"), scatter_dimension=0, tiled=True),
        lax.psum_scatter(grad_gain_one, ("dp", "fsdp"), scatter_dimension=0, tiled=True),
        lax.psum_scatter(grad_shift_one, ("dp", "fsdp"), scatter_dimension=0, tiled=True),
    )
    return (
        output,
        grad_tokens,
        attn_grads[0],
        attn_grads[1],
        mlp_grads[0],
        mlp_grads[1],
        attn_grads[2],
        attn_grads[3],
        mlp_grads[2],
        mlp_grads[3],
        fraction,
    )


def solution(mesh):
    in_specs = (
        P(("dp", "fsdp"), None, None),
        P(("dp", "fsdp"), None),
        P(("dp", "fsdp")),
        P(("dp", "fsdp"), None),
        P(("dp", "fsdp"), None),
        P(("dp", "fsdp"), None),
        P(("dp", "fsdp"), None),
        P(("dp", "fsdp")),
        P(("dp", "fsdp")),
        P(("dp", "fsdp")),
        P(("dp", "fsdp")),
        P(("dp", "fsdp"), None, None),
    )
    out_specs = (
        P(("dp", "fsdp"), None, None),
        P(("dp", "fsdp"), None, None),
        P(("dp", "fsdp"), None),
        P(("dp", "fsdp"), None),
        P(("dp", "fsdp"), None),
        P(("dp", "fsdp"), None),
        P(("dp", "fsdp")),
        P(("dp", "fsdp")),
        P(("dp", "fsdp")),
        P(("dp", "fsdp")),
        P(),
    )
    return jax.shard_map(body, mesh=mesh, in_specs=in_specs, out_specs=out_specs, check_vma=False)
```

profile of v0, /device:TPU:0, one launch (start us, length us, event | category | flops | bytes accessed | tf_op | source)
XLA Modules:
  0.0 1027.6 jit_solution(558365524413268066)
XLA Ops:
  14.8 42.3 %all-reduce.11 = (bf16[768]{0:T(1024)(128)(2,1)S(1)}, bf16[768]{0:T(1024)(128)(2,1)S(1)}, bf16[768]{0:T(1024)(128)(2,1)S(1)}, bf16[768]{0:T(1024)(128)(2,1)S(1)}) all-reduce(bf16[768]{0:T(1024)(128)(2,1)S(1)} %dynamic-update-slice.1, bf16[768]{0:T(1024)(128)(2,1)S(1)} %dynamic-update-slice, ...), channel_id=1, replica_groups=mesh['dp'=2,'fsdp'=16] {'dp','fsdp'}, use_global_device_ids=true, to_apply=%add.3 | all-reduce | flops 3072 | bytes 12288
  61.3 12.3 %all-gather.5.cloned.1.call-done = bf16[768,2304]{1,0:T(8,128)(2,1)} async-done(((bf16[24,2304]{1,0:T(8,128)(2,1)}), bf16[768,2304]{1,0:T(8,128)(2,1)}) %all-gather.5.cloned.1.call-update) | async-done | bytes 3538960 | tf_op jit(solution)/shard_map/all_gather | solution.py:168
  73.6 7.8 convolution_convert_fusion
  81.4 6.6 copy.74
  88.0 3.7 convolution_multiply_fusion.2
  91.8 4.4 slice_bitcast_fusion
  96.2 5.4 copy.75
  107.7 5.5 copy.77
  120.5 4.5 copy.78
  125.0 5.7 copy.127
  130.7 5.3 concatenate.28.clone
  139.2 4.0 copy.80
  143.2 3.9 copy.79
  147.1 63.6 %while.51 = (s32[]{:T(128)}, bf16[11,1024,64]{1,2,0:T(8,128)(2,1)}, f32[11,1024]{1,0:T(8,128)S(1)}, bf16[11,1024,64]{2,1,0:T(8,128)(2,1)}, bf16[11,1024,64]{2,1,...) while((s32[]{:T(128)}, bf16[11,1024,64]{1,2,0:T(8,128)(2,1)}, ...), condition=%wide.region_9.10_spmd.clone, body=%wide.region_6.9_spmd.clone.sunk | while | flops 284228608 | bytes 17747064 | solution.py:80
  147.1 3.5 fusion.176
  164.4 3.5 fusion.176
  170.2 3.5 fusion.176
  176.0 3.5 fusion.176
  181.7 3.5 fusion.176
  187.6 3.5 fusion.176
  193.4 3.5 fusion.176
  204.9 3.5 fusion.176
  210.7 9.0 convert_reduce_fusion.1
  224.3 3.8 fusion.133
  228.5 10.8 %fusion.130 = f32[1024,3072]{1,0:T(8,128)} fusion(bf16[768,3072]{1,0:T(8,128)(2,1)} %all-gather.9.cloned.1.call-done, f32[1024,768]{0,1:T(8,128)S(1)} %get-tuple-element.394, f32[768]{0:T(1024)S(1)} %convert_element_type.101, f32[768]{0:T(1024)S(1)} %convert_element_type.100, f32[1024]{0:T(1024)S(1)} %add_rsqrt_fusion, f32[1024]{0:T(1024)S(1)} %broadcast_multiply_fusion.4), kind=kOutput, calls=%fused_computation.193 | convolution fusion | flops 4835770368 | bytes 20461568 | tf_op jit(solution)/shard_map/dot_general | solution.py:195
  239.3 20.0 %all-gather.11.cloned.1.call-done = bf16[3072,768]{1,0:T(8,128)(2,1)} async-done(((bf16[96,768]{1,0:T(8,128)(2,1)}), bf16[3072,768]{1,0:T(8,128)(2,1)}) %all-gather.11.cloned.1.call-update) | async-done | bytes 4718608 | tf_op jit(solution)/shard_map/all_gather | solution.py:187
  259.3 16.8 %fusion.63 = bf16[1024,3072]{1,0:T(8,128)(2,1)S(1)} fusion(f32[1024,3072]{1,0:T(8,128)} %fusion.130, bf16[3072,768]{1,0:T(8,128)(2,1)} %all-gather.11.cloned.1.call-done, bf16[1,1024,768]{1,2,0:T(8,128)(2,1)} %copy.84, pred[1024]{0:T(1024)(128)(4,1)S(1)} %get-tuple-element.655), kind=kOutput, calls=%fused_computation.73 | convolution fusion | flops 4895539200 | bytes 25166848 | tf_op jit(solution)/shard_map/dot_general | solution.py:207
  276.2 7.3 fusion.135
  283.5 4.0 copy.85
  287.5 3.6 multiply_reduce_fusion.2
  296.9 4.8 convolution_convert_fusion.1
  301.7 4.2 copy.86
  305.9 3.8 slice.134
  316.8 5.4 copy.89
  322.2 180.5 %while.52 = (s32[]{:T(128)}, f32[1024,1024]{0,1:T(8,128)}, bf16[11,1024,64]{1,2,0:T(8,128)(2,1)}, bf16[11,1024,64]{1,2,0:T(8,128)(2,1)}, bf16[11,1024,64]{1,2,0:...) while((s32[]{:T(128)}, f32[1024,1024]{0,1:T(8,128)}, ...), condition=%wide.region_17.18_spmd.clone, body=%wide.region_15.17_spmd.clone.sunk | while | flops 689044480 | bytes 97028320 | solution.py:134
  324.7 4.2 multiply_reduce_fusion.8
  341.1 4.2 multiply_reduce_fusion.8
  357.5 4.2 multiply_reduce_fusion.8
  373.9 4.2 multiply_reduce_fusion.8
  390.3 4.2 multiply_reduce_fusion.8
  406.7 4.2 multiply_reduce_fusion.8
  423.1 4.2 multiply_reduce_fusion.8
  439.5 4.2 multiply_reduce_fusion.8
  455.9 4.2 multiply_reduce_fusion.8
  472.3 4.2 multiply_reduce_fusion.8
  488.7 4.2 multiply_reduce_fusion.8
  502.7 34.4 %rev.6 = f32[1024,1024]{0,1:T(8,128)} reverse(f32[1024,1024]{0,1:T(8,128)} %get-tuple-element.163), dimensions={0} | reverse | bytes 8388608 | tf_op jit(solution)/shard_map/while/body/eval_jaxpr/rev | solution.py:139
  537.1 5.3 copy.126
  542.3 5.6 copy.94
  555.1 4.5 copy.95
  559.7 33.6 %slice.123 = f32[1023,1024]{1,0:T(8,128)} reverse(f32[1023,1024]{1,0:T(8,128)} %bitcast.246), dimensions={0} | reverse | bytes 8380416 | tf_op jit(solution)/shard_map/while/body/eval_jaxpr/slice | solution.py:140
  598.0 6.2 add_convert_fusion
  610.5 6.3 fusion.98
  616.9 14.0 %fusion.101 = f32[3072,768]{1,0:T(8,128)} fusion(bf16[1,1024,768]{1,2,0:T(8,128)(2,1)} %copy.84, pred[1024]{0:T(1024)(128)(4,1)S(1)} %get-tuple-element.656, f32[1024,3072]{1,0:T(8,128)} %fusion.130), kind=kOutput, calls=%fused_computation.144 | convolution fusion | flops 4860936192 | bytes 23593984 | tf_op jit(solution)/shard_map/dot_general | solution.py:206
  631.6 11.0 %fusion.129 = f32[768,3072]{1,0:T(8,128)} fusion(bf16[1024,3072]{1,0:T(8,128)(2,1)} %copy-done.36, f32[1024,768]{0,1:T(8,128)S(1)} %get-tuple-element.394, f32[768]{0:T(1024)S(1)} %copy-done.24, f32[768]{0:T(1024)S(1)} %convert_element_type.100, f32[1024]{0:T(1024)S(1)} %add_rsqrt_fusion, f32[1024]{0:T(1024)S(1)} %broadcast_multiply_fusion.4), kind=kOutput, calls=%fused_computation.192 | convolution fusion | flops 4835770368 | bytes 18888704 | tf_op jit(solution)/shard_map/dot_general | solution.py:210
  642.7 11.6 %fusion.112 = bf16[1,1024,768]{1,2,0:T(8,128)(2,1)} fusion(f32[1024,768]{0,1:T(8,128)S(1)} %get-tuple-element.394, bf16[3072,768]{1,0:T(8,128)(2,1)} %all-gather.11.cloned.1.call-done, f32[1024,3072]{1,0:T(8,128)} %fusion.130), kind=kOutput, calls=%fused_computation.156 | convolution fusion | flops 4861722624 | bytes 22020096 | tf_op jit(solution)/shard_map/dot_general | solution.py:197
  656.9 9.0 fusion.134
  665.9 4.5 copy.96
  673.3 40.6 %all-reduce.10 = (f32[768]{0:T(1024)S(1)}, f32[768]{0:T(1024)S(1)}, f32[768]{0:T(1024)S(1)}, f32[768]{0:T(1024)S(1)}, f32[]{:T(128)}, /*index=5*/f32[]{:T(128)}) all-reduce(f32[768]{0:T(1024)S(1)} %get-tuple-element.320, f32[768]{0:T(1024)S(1)} %get-tuple-element.397, ...), channel_id=6, replica_groups=mesh['dp'=2,'fsdp'=16] {'dp','fsdp'}, use_global_device_ids=true, to_apply=%region_27.28.clone | all-reduce | flops 3074 | bytes 24592
  716.3 5.5 fusion.86
  721.8 3.5 copy.100
  726.6 9.1 reduce-scatter.5.cloned.1.call-done
  735.8 141.7 %reduce-scatter.11.cloned.1.call-done = f32[96,768]{1,0:T(8,128)} async-done(((f32[3072,768]{1,0:T(8,128)}), f32[96,768]{1,0:T(8,128)}) %reduce-scatter.11.cloned.1.call-update) | async-done | bytes 294928 | tf_op jit(solution)/shard_map/reduce_scatter | solution.py:218
  877.5 141.7 %reduce-scatter.9.cloned.1.call-done = f32[24,3072]{1,0:T(8,128)} async-done(((f32[768,3072]{1,0:T(8,128)}), f32[24,3072]{1,0:T(8,128)}) %reduce-scatter.9.cloned.1.call-update) | async-done | bytes 294928 | tf_op jit(solution)/shard_map/reduce_scatter | solution.py:217
  (330 shorter events, 241.2 us)
Async XLA Ops:
  7.2 52.5 %copy-start.18 = (bf16[1,1024,768]{2,1,0:T(8,128)(2,1)S(1)}, bf16[1,1024,768]{2,1,0:T(8,128)(2,1)}, u32[]{:S(2)}) copy-start(bf16[1,1024,768]{2,1,0:T(8,128)(2,1)} %param.27) | copy-start | bytes 4718596
  7.2 66.4 %all-gather.5.cloned.1.call-start = ((), (), s32[]{:S(2)}) async-start(), calls=%async_computation.4 | async-start | bytes 3649536 | tf_op jit(solution)/shard_map/all_gather | solution.py:168
  7.9 216.4 %all-gather.7.cloned.1.call-start = ((), (), s32[]{:S(2)}) async-start(), calls=%async_computation.5 | async-start | bytes 1216512 | tf_op jit(solution)/shard_map/all_gather | solution.py:169
  8.7 219.8 %all-gather.9.cloned.1.call-start = ((), (), s32[]{:S(2)}) async-start(), calls=%async_computation.6 | async-start | bytes 4866048 | tf_op jit(solution)/shard_map/all_gather | solution.py:186
  9.4 249.9 %all-gather.11.cloned.1.call-start = ((), (), s32[]{:S(2)}) async-start(), calls=%async_computation.7 | async-start | bytes 4866048 | tf_op jit(solution)/shard_map/all_gather | solution.py:187
  10.0 716.6 %reduce-scatter.7.cloned.1.call-start = ((), (), s32[]{:S(2)}) async-start(), calls=%async_computation.9 | async-start | bytes 2433024 | tf_op jit(solution)/shard_map/reduce_scatter | solution.py:241
  57.1 16.5 %copy-start.34 = (f32[768]{0:T(1024)}, f32[768]{0:T(1024)S(1)}, u32[]{:S(2)}) copy-start(f32[768]{0:T(1024)S(1)} %convert_element_type.95) | copy-start | bytes 9220
  57.1 16.5 %copy-start.28 = (f32[768]{0:T(1024)}, f32[768]{0:T(1024)S(1)}, u32[]{:S(2)}) copy-start(f32[768]{0:T(1024)S(1)} %convert_element_type.94) | copy-start | bytes 9220
  57.1 171.4 %copy-start.23 = (f32[768]{0:T(1024)}, f32[768]{0:T(1024)S(1)}, u32[]{:S(2)}) copy-start(f32[768]{0:T(1024)S(1)} %convert_element_type.101) | copy-start | bytes 9220
  58.9 22.5 %copy-start.5 = (bf16[1,1024,768]{1,2,0:T(8,128)(2,1)}, bf16[1,1024,768]{1,2,0:T(8,128)(2,1)S(1)}, u32[]{:S(2)}) copy-start(bf16[1,1024,768]{1,2,0:T(8,128)(2,1)S(1)} %copy.73) | copy-start | bytes 4718596
  59.2 22.2 %copy-start.26 = (f32[1024]{0:T(1024)}, f32[1024]{0:T(1024)S(1)}, u32[]{:S(2)}) copy-start(f32[1024]{0:T(1024)S(1)} %broadcast_multiply_fusion.5) | copy-start | bytes 12292
  59.6 21.7 %copy-start.30 = (f32[1024]{0:T(1024)}, f32[1024]{0:T(1024)S(1)}, u32[]{:S(2)}) copy-start(f32[1024]{0:T(1024)S(1)} %add_rsqrt_fusion.1) | copy-start | bytes 12292
  96.2 5.4 copy-start.25
  210.7 9.0 copy-start.14
  219.7 3.3 copy-start.2
  259.3 16.8 %copy-start.15 = (bf16[768,3072]{1,0:T(8,128)(2,1)S(1)}, bf16[768,3072]{1,0:T(8,128)(2,1)}, u32[]{:S(2)}) copy-start(bf16[768,3072]{1,0:T(8,128)(2,1)} %all-gather.9.cloned.1.call-done) | copy-start | bytes 14155780
  276.2 7.3 copy-start.36
  287.5 3.6 copy-start.9
  287.5 3.6 copy-start.13
  291.1 2.8 copy-start.19
  296.8 438.9 %reduce-scatter.5.cloned.1.call-start = ((), (), s32[]{:S(2)}) async-start(), calls=%async_computation.8 | async-start | bytes 7299072 | tf_op jit(solution)/shard_map/reduce_scatter | solution.py:240
  305.9 3.8 copy-start.3
  322.2 2.4 copy-start.17
  328.9 2.5 copy-start
  334.0 4.7 copy-start.1
  338.7 2.3 copy-start.17
  345.3 2.5 copy-start
  350.4 4.7 copy-start.1
  355.1 2.4 copy-start.17
  361.7 2.5 copy-start
  366.8 4.7 copy-start.1
  371.5 2.4 copy-start.17
  378.1 2.5 copy-start
  383.2 4.7 copy-start.1
  387.9 2.4 copy-start.17
  394.5 2.5 copy-start
  399.6 4.7 copy-start.1
  404.4 2.3 copy-start.17
  410.9 2.5 copy-start
  416.1 4.7 copy-start.1
  420.8 2.3 copy-start.17
  427.3 2.5 copy-start
  432.5 4.7 copy-start.1
  443.7 2.5 copy-start
  448.8 4.7 copy-start.1
  460.1 2.5 copy-start
  465.2 4.7 copy-start.1
  476.5 2.5 copy-start
  481.6 4.7 copy-start.1
  492.9 2.5 copy-start
  498.0 4.7 copy-start.1
  593.3 4.7 copy-start.4
  598.0 8.0 copy-start.21
  604.3 3.3 copy-start.20
  607.8 2.8 copy-start.6
  607.8 2.8 copy-start.27
  607.8 2.8 copy-start.29
  607.8 2.7 copy-start.31
  607.8 2.7 copy-start.35
  616.9 260.6 %reduce-scatter.11.cloned.1.call-start = ((), (), s32[]{:S(2)}) async-start(), calls=%async_computation.11 | async-start | bytes 9732096 | tf_op jit(solution)/shard_map/reduce_scatter | solution.py:218
  631.0 388.2 %reduce-scatter.9.cloned.1.call-start = ((), (), s32[]{:S(2)}) async-start(), calls=%async_computation.10 | async-start | bytes 9732096 | tf_op jit(solution)/shard_map/reduce_scatter | solution.py:217
  665.9 4.5 copy-start.7
  665.9 7.4 copy-start.32
  665.9 7.4 copy-start.33
  (11 other events, 22.2 us)
Sparse Core Ops, SparseCore 0:
  10.9 62.6 all-gather.4
  76.5 52.7 all-gather.6
  132.2 62.4 all-gather.8
  197.4 61.8 all-gather.10
  296.9 97.9 reduce-scatter.6
  617.0 118.7 reduce-scatter.4
  742.2 135.1 reduce-scatter.10
  883.9 135.1 reduce-scatter.8
where the time goes:
time: 1040 us; the launch traced here: 1030 us
  waiting for transfers between devices  328 us (32%)
  matrix products  322 us (31%)
  local copies, waits for them, and re-layouts  189 us (18%)
  other arithmetic  86.8 us (8%)
  blocking collectives  82.9 us (8%)
  between operations  18.2 us (2%)
    reduce_scatter x1, waiting for transfers between devices, body(): lax.psum_scatter(grad_down, ('dp', 'fsdp'), scatter_dimension=0, tiled=True)  142 us
    reduce_scatter x1, waiting for transfers between devices, body(): lax.psum_scatter(grad_up, ('dp', 'fsdp'), scatter_dimension=0, tiled=True)  142 us
    dot_general x23, matrix products, head_scores(): jnp.dot(query_head, key_head.T, preferred_element_type=jnp.float32)  88.4 us
    unnamed x2, blocking collectives  82.9 us
    unnamed x91, local copies, waits for them, and re-layouts  56.3 us
    rev x1, local copies, waits for them, and re-layouts, row_back(): later = jnp.cumsum(grad_selsum[::-1], axis=0)[::-1]  34.4 us
    slice x1, local copies, waits for them, and re-layouts, row_back(): later[1:]  33.6 us
    dot_general x12, matrix products, soft_back(): jnp.dot(probs.astype(jnp.bfloat16).T, grad_head, preferred_element_type=j...  31 us
  transfers between devices with their start and end apart: 8, of which 5 were waited for; matrix products, arithmetic and copies ran while one was open for 53% of the time, Pallas kernels for 0%

commit v1 on v0

v1 whole, which is shorter than its diff:
```python
import functools

import jax
import jax.numpy as jnp
from jax import lax
from jax.experimental import pallas as pl
from jax.experimental.pallas import tpu as pltpu
from jax.sharding import PartitionSpec as P

HEADS = 12
HD = 64


EPSILON = 1e-05
NEGATIVE = -1e30
SOFT_WIDTH = 0.25


def norm_forward(values, gain, shift):
    center = values - jnp.mean(values, axis=-1, keepdims=True)
    spread = jnp.mean(center * center, axis=-1, keepdims=True)
    inverse = lax.rsqrt(spread + EPSILON)
    unit = center * inverse
    return (unit * gain + shift, unit, inverse)


def norm_backward(grad_normed, unit, inverse, gain):
    grad_unit = grad_normed * gain
    grad_gain = jnp.sum(grad_normed * unit, axis=0)
    grad_shift = jnp.sum(grad_normed, axis=0)
    centered = grad_unit - jnp.mean(grad_unit, axis=-1, keepdims=True)
    grad_input = inverse * (centered - unit * jnp.mean(grad_unit * unit, axis=-1, keepdims=True))
    return (grad_input, grad_gain, grad_shift)


BLOCK = 128
SPAN = 384
NT = (((1,), (1,)), ((), ()))
TN = (((0,), (0,)), ((), ()))


def dot_nt(a, b):
    return lax.dot_general(a, b, NT, preferred_element_type=jnp.float32)


def dot_tn(a, b):
    return lax.dot_general(a, b, TN, preferred_element_type=jnp.float32)


def halves(pair):
    lane = lax.broadcasted_iota(jnp.int32, pair.shape, 1)
    zero = jnp.zeros_like(pair)
    return (jnp.where(lane < HD, pair, zero), jnp.where(lane < HD, zero, pair))


def attend_kernel(limit_ref, seg_ref, project_ref, mixed_ref, lse_ref, bias_ref, stat_ref, column_ref):
    block = pl.program_id(0)
    width = HEADS * HD
    here = pl.multiple_of(block * BLOCK, BLOCK)
    first_key = pl.multiple_of(jnp.maximum(block - 2, 0) * BLOCK, BLOCK)
    rows = pl.ds(here, BLOCK)
    span = pl.ds(first_key, SPAN)

    @pl.when(block == 0)
    def _():
        column_ref[...] = jnp.zeros_like(column_ref)
        stat_ref[...] = jnp.zeros_like(stat_ref)

    low_lane = lax.broadcasted_iota(jnp.int32, (BLOCK, BLOCK), 1)
    bias = None
    for pair in range(HEADS // 2):
        at = pair * 2 * HD
        lanes = slice(at, at + 2 * HD)
        queries = halves(project_ref[rows, lanes] * jnp.bfloat16(HD ** (-0.5)))
        key = project_ref[span, width + at : width + at + 2 * HD]
        value = project_ref[span, 2 * width + at : 2 * width + at + 2 * HD]
        both = dot_nt(key, jnp.concatenate(queries, axis=0))
        outs = []
        for side in range(2):
            head = 2 * pair + side
            scores = both[:, side * BLOCK : (side + 1) * BLOCK]
            if bias is None:
                seg_key = jnp.broadcast_to(seg_ref[:, span], (BLOCK, SPAN)).T
                key_at = first_key + lax.broadcasted_iota(jnp.int32, (SPAN, BLOCK), 0)
                query_at = here + lax.broadcasted_iota(jnp.int32, (SPAN, BLOCK), 1)
                strict = (key_at < query_at) & (seg_ref[:, rows] == seg_key) & (seg_key >= 0)
                allowed = strict | (key_at == query_at)
                select = jnp.where(strict, jnp.maximum(scores, 0.0), 0.0)
                at_row = lax.broadcasted_iota(jnp.int32, (BLOCK, 2 * BLOCK), 0)
                at_lane = lax.broadcasted_iota(jnp.int32, (BLOCK, 2 * BLOCK), 1)
                sums = jnp.dot(
                    select,
                    ((at_row < at_lane) | (at_lane >= BLOCK)).astype(jnp.float32),
                    precision=lax.Precision.HIGHEST,
                    preferred_element_type=jnp.float32,
                )
                before = column_ref[span, :]
                selsum = before + sums[:, :BLOCK]
                column_ref[span, :] = before + sums[:, BLOCK:]
                bias = jnp.where(allowed, -selsum, NEGATIVE)
                bias_ref[...] = bias
                offset = (selsum - limit_ref[0]) * (1.0 / SOFT_WIDTH)
                soft = jnp.where(strict, 1.0 / (1.0 + jnp.exp(-offset)), 0.0)
                stat_ref[0:1, :] += jnp.sum(soft, axis=0, keepdims=True)
                stat_ref[1:2, :] += jnp.sum(jnp.where(strict, 1.0, 0.0), axis=0, keepdims=True)
            logits = scores + bias
            top = jnp.max(logits, axis=0, keepdims=True)
            expo = jnp.exp(logits - top)
            total = jnp.sum(expo, axis=0, keepdims=True)
            probs = (expo * (1.0 / total)).astype(jnp.bfloat16)
            outs.append(dot_tn(probs, value))
            lse_ref[head : head + 1, :] = top + jnp.log(total)
        mixed_ref[:, lanes] = jnp.where(low_lane < HD, outs[0], outs[1]).astype(jnp.bfloat16)


def attend_row(project_row, seg_row, limit):
    length = seg_row.shape[0]
    width = HEADS * HD
    blocks = length // BLOCK
    return pl.pallas_call(
        attend_kernel,
        name="attend_forward",
        grid=(blocks,),
        in_specs=[
            pl.BlockSpec(memory_space=pltpu.SMEM),
            pl.BlockSpec((1, length), lambda i: (0, 0)),
            pl.BlockSpec((length, 3 * width), lambda i: (0, 0), pipeline_mode=pl.Buffered(1)),
        ],
        out_specs=[
            pl.BlockSpec((BLOCK, width), lambda i: (i, 0)),
            pl.BlockSpec((16, BLOCK), lambda i: (0, i)),
            pl.BlockSpec((None, SPAN, BLOCK), lambda i: (i, 0, 0)),
            pl.BlockSpec((8, BLOCK), lambda i: (0, 0)),
        ],
        out_shape=[
            jax.ShapeDtypeStruct((length, width), jnp.bfloat16),
            jax.ShapeDtypeStruct((16, length), jnp.float32),
            jax.ShapeDtypeStruct((blocks, SPAN, BLOCK), jnp.float32),
            jax.ShapeDtypeStruct((8, BLOCK), jnp.float32),
        ],
        scratch_shapes=[pltpu.VMEM((length, BLOCK), jnp.float32)],
        cost_estimate=pl.CostEstimate(
            flops=4 * length * SPAN * width, transcendentals=HEADS * length * SPAN, bytes_accessed=10 * length * width
        ),
    )(limit, seg_row[None], project_row)


def attend_back_kernel(
    project_ref, grad_ref, lse_ref, bias_ref, out_ref, key_ref, value_ref, column_ref, select_ref
):
    block = pl.num_programs(0) - 1 - pl.program_id(0)
    width = HEADS * HD
    here = pl.multiple_of(block * BLOCK, BLOCK)
    first_key = pl.multiple_of(jnp.maximum(block - 2, 0) * BLOCK, BLOCK)
    rows = pl.ds(here, BLOCK)
    span = pl.ds(first_key, SPAN)

    @pl.when(pl.program_id(0) == 0)
    def _():
        key_ref[...] = jnp.zeros_like(key_ref)
        value_ref[...] = jnp.zeros_like(value_ref)
        column_ref[...] = jnp.zeros_like(column_ref)

    bias = jnp.concatenate([bias_ref[...], bias_ref[...]], axis=1)
    for pair in reversed(range(HEADS // 2)):
        at = pair * 2 * HD
        lanes = slice(at, at + 2 * HD)
        queries = halves(project_ref[rows, lanes] * jnp.bfloat16(HD ** (-0.5)))
        queries = jnp.concatenate(queries, axis=0)
        key = project_ref[span, width + at : width + at + 2 * HD]
        value = project_ref[span, 2 * width + at : 2 * width + at + 2 * HD]
        grads = jnp.concatenate(halves(grad_ref[:, lanes]), axis=0)
        lse = jnp.concatenate(
            [lse_ref[2 * pair : 2 * pair + 1, :], lse_ref[2 * pair + 1 : 2 * pair + 2, :]], axis=1
        )
        scores = dot_nt(key, queries)
        probs = jnp.exp(scores + bias - lse)
        grad_probs = dot_nt(value, grads)
        inner = jnp.sum(probs * grad_probs, axis=0, keepdims=True)
        logits_grads = probs * (grad_probs - inner)
        both = logits_grads[:, :BLOCK] + logits_grads[:, BLOCK:]
        if pair == HEADS // 2 - 1:
            select_ref[...] = -both
        else:
            select_ref[...] -= both
        if pair == 0:
            grad_selsum = select_ref[...]
            at_row = lax.broadcasted_iota(jnp.int32, (BLOCK, 2 * BLOCK), 0)
            at_lane = lax.broadcasted_iota(jnp.int32, (BLOCK, 2 * BLOCK), 1)
            after = ((at_row > at_lane) | (at_lane >= BLOCK)).astype(jnp.float32)
            sums = jnp.dot(
                grad_selsum,
                after,
                precision=lax.Precision.HIGHEST,
                preferred_element_type=jnp.float32,
            )
            later = column_ref[span, :]
            grad_select = later + sums[:, :BLOCK]
            column_ref[span, :] = later + sums[:, BLOCK:]
            key_at = first_key + lax.broadcasted_iota(jnp.int32, (SPAN, BLOCK), 0)
            query_at = here + lax.broadcasted_iota(jnp.int32, (SPAN, BLOCK), 1)
            chosen = (bias[:, :BLOCK] > 0.5 * NEGATIVE) & (key_at != query_at)
            chosen = chosen & (scores[:, :BLOCK] > 0.0)
            grad_select = jnp.where(chosen, grad_select, 0.0)
            logits_grads = jnp.concatenate(
                [logits_grads[:, :BLOCK] + grad_select, logits_grads[:, BLOCK:]], axis=1
            )
        low_grads = logits_grads.astype(jnp.bfloat16)
        value_ref[span, lanes] += jnp.dot(
            probs.astype(jnp.bfloat16), grads, preferred_element_type=jnp.float32
        )
        key_ref[span, lanes] += jnp.dot(low_grads, queries, preferred_element_type=jnp.float32)
        query_grad = jnp.dot(key.T, low_grads, preferred_element_type=jnp.float32)
        query_grad = jnp.concatenate([query_grad[:HD, :BLOCK], query_grad[HD:, BLOCK:]], axis=0)
        out_ref[:, lanes] = (query_grad.T * HD ** (-0.5)).astype(jnp.bfloat16)
    out_ref[:, width : 2 * width] = key_ref[rows, :].astype(jnp.bfloat16)
    out_ref[:, 2 * width :] = value_ref[rows, :].astype(jnp.bfloat16)


def row_back(project_row, grad_row, lse_row, bias_row):
    length = project_row.shape[0]
    width = HEADS * HD
    blocks = length // BLOCK
    return pl.pallas_call(
        attend_back_kernel,
        name="attend_backward",
        grid=(blocks,),
        in_specs=[
            pl.BlockSpec((length, 3 * width), lambda i: (0, 0), pipeline_mode=pl.Buffered(1)),
            pl.BlockSpec((BLOCK, width), lambda i: (blocks - 1 - i, 0)),
            pl.BlockSpec((16, BLOCK), lambda i: (0, blocks - 1 - i)),
            pl.BlockSpec((None, SPAN, BLOCK), lambda i: (blocks - 1 - i, 0, 0)),
        ],
        out_specs=pl.BlockSpec((BLOCK, 3 * width), lambda i: (blocks - 1 - i, 0)),
        out_shape=jax.ShapeDtypeStruct((length, 3 * width), jnp.bfloat16),
        scratch_shapes=[
            pltpu.VMEM((length, width), jnp.float32),
            pltpu.VMEM((length, width), jnp.float32),
            pltpu.VMEM((length, BLOCK), jnp.float32),
            pltpu.VMEM((SPAN, BLOCK), jnp.float32),
        ],
        cost_estimate=pl.CostEstimate(
            flops=10 * length * SPAN * width, transcendentals=HEADS * length * SPAN, bytes_accessed=14 * length * width
        ),
    )(project_row, grad_row, lse_row, bias_row)


BOTH = ("dp", "fsdp")


def bit_count(sizes):
    return (sizes["dp"] * sizes["fsdp"]).bit_length() - 1


def my_bits(sizes):
    count = bit_count(sizes)
    number = lax.axis_index("dp") * sizes["fsdp"] + lax.axis_index("fsdp")
    return [(number >> (count - 1 - place)) & 1 for place in range(count)]


def exchange(value, sizes, places):
    count = bit_count(sizes)
    masks = [1 << (count - 1 - place) for place in places]
    return lax.ppermute(value, BOTH, [(i, i ^ masks[i & 1]) for i in range(2**count)])


def side_of(shape, axis):
    return lax.broadcasted_iota(jnp.int32, shape, axis)


def join(mine, other, at, bit):
    shape = mine.shape[:at] + (2,) + mine.shape[at:]
    return jnp.where(side_of(shape, at) == bit, jnp.expand_dims(mine, at), jnp.expand_dims(other, at))


def gather_far(shard, sizes):
    bits = my_bits(sizes)
    value = shard
    for place in range(1, len(bits) - 2):
        value = join(value, exchange(value, sizes, (place, place)), place - 1, bits[place])
    return value


def gather_near(value, sizes):
    bits = my_bits(sizes)
    near = len(bits) - 2
    other = exchange(value, sizes, (0, near))
    return join(value, other, 0, jnp.where(bits[-1] == 0, bits[0], bits[near]))


def gather_next(value, sizes):
    bits = my_bits(sizes)
    near = len(bits) - 2
    other = exchange(value, sizes, (near, 0))
    by_first = join(value, other, near, bits[near])
    by_near = join(jnp.moveaxis(value, 0, near - 1), jnp.moveaxis(other, 0, near - 1), 0, bits[0])
    return jnp.where(bits[-1] == 0, by_first, by_near)


def gather_core(value, sizes):
    bits = my_bits(sizes)
    last = len(bits) - 1
    value = join(value, exchange(value, sizes, (last, last)), last, bits[last])
    return value.reshape((-1,) + value.shape[last + 2 :])


def pick(value, at, bit):
    return lax.dynamic_index_in_dim(value, bit, at, keepdims=False)


def add_exchange(mine, sent, sizes, places, kind):
    return mine.astype(jnp.float32) + exchange(sent.astype(kind), sizes, places).astype(jnp.float32)


def scatter_core(partial, sizes, kind=jnp.bfloat16):
    bits = my_bits(sizes)
    last = len(bits) - 1
    shape = (2,) * len(bits) + (partial.shape[0] >> len(bits),) + partial.shape[1:]
    view = partial.reshape(shape)
    return add_exchange(
        pick(view, last, bits[last]), pick(view, last, 1 - bits[last]), sizes, (last, last), kind
    )


def scatter_near(value, sizes, kind=jnp.bfloat16):
    bits = my_bits(sizes)
    near = len(bits) - 2
    even = bits[-1] == 0

    def cut(flip):
        by_near = pick(value, near, bits[near] ^ flip)
        by_first = jnp.moveaxis(pick(value, 0, bits[0] ^ flip), near - 1, 0)
        return jnp.where(even, by_near, by_first)

    return add_exchange(cut(0), cut(1), sizes, (near, 0), kind)


def scatter_next(value, sizes, kind=jnp.bfloat16):
    bits = my_bits(sizes)
    near = len(bits) - 2
    side = jnp.where(bits[-1] == 0, bits[0], bits[near])
    return add_exchange(pick(value, 0, side), pick(value, 0, 1 - side), sizes, (0, near), kind)


def scatter_far(value, sizes, kind=jnp.bfloat16):
    bits = my_bits(sizes)
    for place in reversed(range(1, len(bits) - 2)):
        value = add_exchange(
            pick(value, place - 1, bits[place]),
            pick(value, place - 1, 1 - bits[place]),
            sizes,
            (place, place),
            kind,
        )
    return value


def tie(*values):
    return lax.optimization_barrier(values)


def body(
    sizes,
    tokens,
    segments,
    thresholds,
    qkv_weight,
    out_weight,
    up_weight,
    down_weight,
    attn_gain,
    attn_shift,
    mlp_gain,
    mlp_shift,
    cotangent,
):
    rows_here, length, width = tokens.shape
    shards = sizes["dp"] * sizes["fsdp"]
    piece = width // shards
    small = jnp.stack([attn_gain, attn_shift, mlp_gain, mlp_shift], axis=1)
    small = jnp.pad(small, ((0, 0), (0, 128 - 4)))
    wide = up_weight.shape[1]
    second = lax.all_gather(
        jnp.concatenate([up_weight, out_weight], axis=1), BOTH, axis=0, tiled=True
    )
    up_full, out_full = (second[:, :wide], second[:, wide:])
    first = gather_far(jnp.concatenate([qkv_weight, small], axis=1), sizes)
    first, down_weight = tie(first, down_weight)
    down_full = gather_far(down_weight, sizes)
    first = gather_next(gather_near(first, sizes), sizes)
    first, down_full = tie(first, down_full)
    first = gather_core(first, sizes)
    down_full = gather_near(down_full, sizes)
    qkv_full = first[:, : 3 * width]
    small = first[:, 3 * width : 3 * width + 4].astype(jnp.float32).T
    gain_one, shift_one, gain_two, shift_two = (small[0], small[1], small[2], small[3])
    flat = tokens.astype(jnp.float32).reshape(rows_here * length, width)
    normed_float, unit_one, inverse_one = norm_forward(flat, gain_one, shift_one)
    normed = normed_float.astype(jnp.bfloat16)
    project = jnp.dot(normed, qkv_full, preferred_element_type=jnp.float32).astype(jnp.bfloat16)
    project, down_full = tie(project, down_full)
    down_full = gather_next(down_full, sizes)
    project_rows = project.reshape(rows_here, length, 3 * width)
    forward = [
        attend_row(project_rows[row], segments[row], thresholds[row : row + 1])
        for row in range(rows_here)
    ]
    mixed_flat = jnp.concatenate([item[0] for item in forward], axis=0)
    soft = sum(jnp.sum(item[3][0]) for item in forward)
    pairs = sum(jnp.sum(item[3][1]) for item in forward)
    middle = flat + jnp.dot(mixed_flat, out_full, preferred_element_type=jnp.float32)
    normed_two_float, unit_two, inverse_two = norm_forward(middle, gain_two, shift_two)
    normed_two, down_full = tie(normed_two_float.astype(jnp.bfloat16), down_full)
    down_full = gather_core(down_full, sizes)
    hidden = jnp.dot(normed_two, up_full, preferred_element_type=jnp.float32)
    active = jax.nn.gelu(hidden, approximate=True).astype(jnp.bfloat16)
    grad_seed = jnp.where(
        (segments >= 0)[:, :, None], cotangent, jnp.zeros_like(cotangent)
    ).reshape(rows_here * length, width)
    grad_down = jnp.dot(active.T, grad_seed, preferred_element_type=jnp.float32)
    down_full, grad_down = tie(down_full, grad_down)
    grad_down = lax.psum_scatter(
        grad_down.astype(jnp.bfloat16), BOTH, scatter_dimension=0, tiled=True
    ).astype(jnp.float32)
    grad_active = jnp.dot(grad_seed, down_full.T, preferred_element_type=jnp.float32)
    unused_value, gelu_pull = jax.vjp(lambda values: jax.nn.gelu(values, approximate=True), hidden)
    grad_hidden = gelu_pull(grad_active)[0].astype(jnp.bfloat16)
    grad_up = jnp.dot(normed_two.T, grad_hidden, preferred_element_type=jnp.float32)
    grad_hidden, grad_up = tie(grad_hidden, grad_up.astype(jnp.bfloat16))
    grad_up = scatter_core(grad_up, sizes)
    grad_normed_two = jnp.dot(grad_hidden, up_full.T, preferred_element_type=jnp.float32)
    grad_middle_part, grad_gain_two, grad_shift_two = norm_backward(
        grad_normed_two, unit_two, inverse_two, gain_two
    )
    grad_middle = grad_seed.astype(jnp.float32) + grad_middle_part
    grad_branch = grad_middle.astype(jnp.bfloat16)
    grad_out = jnp.dot(mixed_flat.T, grad_branch, preferred_element_type=jnp.float32)
    grad_branch, grad_out, grad_up = tie(grad_branch, grad_out.astype(jnp.bfloat16), grad_up)
    grad_up = scatter_near(grad_up, sizes)
    grad_out = scatter_core(grad_out, sizes)
    grad_mixed = jnp.dot(grad_branch, out_full.T, preferred_element_type=jnp.float32).astype(
        jnp.bfloat16
    )
    grad_mixed, grad_out = tie(grad_mixed.reshape(rows_here, length, width), grad_out)
    grad_out = scatter_near(grad_out, sizes)
    grad_project = jnp.concatenate(
        [
            row_back(project_rows[row], grad_mixed[row], forward[row][1], forward[row][2])
            for row in range(rows_here)
        ],
        axis=0,
    )
    grad_project, grad_up, grad_out = tie(grad_project, grad_up, grad_out)
    upper = scatter_next(jnp.concatenate([grad_up, grad_out], axis=-1), sizes)
    grad_qkv = jnp.dot(normed.T, grad_project, preferred_element_type=jnp.float32)
    grad_qkv, active = tie(grad_qkv.astype(jnp.bfloat16), active)
    grad_qkv = scatter_core(grad_qkv, sizes)
    result = middle + jnp.dot(active, down_full, preferred_element_type=jnp.float32)
    output = result.astype(jnp.bfloat16).reshape(rows_here, length, width)
    grad_project, grad_qkv, output = tie(grad_project, grad_qkv, output)
    upper = scatter_far(upper, sizes)
    grad_up, grad_out = (upper[:, :wide], upper[:, wide:])
    grad_qkv = scatter_far(scatter_next(scatter_near(grad_qkv, sizes), sizes), sizes)
    grad_normed = jnp.dot(grad_project, qkv_full.T, preferred_element_type=jnp.float32)
    grad_input_part, grad_gain_one, grad_shift_one = norm_backward(
        grad_normed, unit_one, inverse_one, gain_one
    )
    grad_tokens = (grad_middle + grad_input_part).reshape(rows_here, length, width)
    small = jnp.stack([grad_gain_one, grad_shift_one, grad_gain_two, grad_shift_two])
    small = small.reshape(4, shards, piece).transpose(1, 0, 2).reshape(shards, 4 * piece)
    totals = jnp.broadcast_to(jnp.stack([soft, pairs]), (shards, 2))
    small = jnp.concatenate([small, totals], axis=1)
    small = jnp.pad(small, ((0, 0), (0, 128 - small.shape[1])))
    small = scatter_near(scatter_core(small, sizes, jnp.float32), sizes, jnp.float32)
    small = scatter_far(scatter_next(small, sizes, jnp.float32), sizes, jnp.float32)[0]
    fraction = small[4 * piece] / small[4 * piece + 1]
    return (
        output,
        grad_tokens,
        grad_qkv,
        grad_out,
        grad_up,
        grad_down,
        small[:piece],
        small[piece : 2 * piece],
        small[2 * piece : 3 * piece],
        small[3 * piece : 4 * piece],
        fraction,
    )


def solution(mesh):
    in_specs = (
        P(("dp", "fsdp"), None, None),
        P(("dp", "fsdp"), None),
        P(("dp", "fsdp")),
        P(("dp", "fsdp"), None),
        P(("dp", "fsdp"), None),
        P(("dp", "fsdp"), None),
        P(("dp", "fsdp"), None),
        P(("dp", "fsdp")),
        P(("dp", "fsdp")),
        P(("dp", "fsdp")),
        P(("dp", "fsdp")),
        P(("dp", "fsdp"), None, None),
    )
    out_specs = (
        P(("dp", "fsdp"), None, None),
        P(("dp", "fsdp"), None, None),
        P(("dp", "fsdp"), None),
        P(("dp", "fsdp"), None),
        P(("dp", "fsdp"), None),
        P(("dp", "fsdp"), None),
        P(("dp", "fsdp")),
        P(("dp", "fsdp")),
        P(("dp", "fsdp")),
        P(("dp", "fsdp")),
        P(),
    )
    return jax.shard_map(
        functools.partial(body, dict(mesh.shape)), mesh=mesh, in_specs=in_specs, out_specs=out_specs, check_vma=False)
```

time: 1040 us -> 352 us (0.34)
  waiting for transfers between devices: 328 us -> 73.5 us
  matrix products: 322 us -> 85 us
  local copies, waits for them, and re-layouts: 189 us -> 35.7 us
  blocking collectives: 82.9 us -> 0 us
  Pallas kernels: 0 us -> 46.1 us
  starting transfers between devices: 0.31 us -> 34.5 us
  other arithmetic: 86.8 us -> 54.9 us
    reduce_scatter x4 -> x1, waiting for transfers between devices: 293 us -> 0.02 us  [body(): lax.psum_scatter(grad_down.astype(jnp.bfloat16), BOTH, scatter_dimension=...]
    dot_general x87 -> x4, matrix products: 254 us -> 34.4 us  [the longest x1 18.3 us: body(): jnp.dot(grad_seed, down_full.T, preferred_element_type=jnp.float32)]
    unnamed x2 -> x0, blocking collectives: 82.9 us -> none
    ppermute x0 -> x27, waiting for transfers between devices: none -> 73.4 us  [exchange(): lax.ppermute(value, BOTH, [(i, i ^ masks[i & 1]) for i in range(2 ** coun...]
    pallas_call x0 -> x2, Pallas kernels: none -> 46.1 us  [the longest x1 27.2 us: row_back(): pl.pallas_call(attend_back_kernel, name='attend_backward', grid=(blocks,)...]
    slice x3 -> x5, local copies, waits for them, and re-layouts: 41.9 us -> 3.35 us  [the longest x2 1.37 us: body(): grad_up, grad_out = (upper[:, :wide], upper[:, wide:])]
    unnamed x91 -> x78, local copies, waits for them, and re-layouts: 56.3 us -> 20.6 us
    ppermute x0 -> x27, starting transfers between devices: none -> 34.4 us  [exchange(): lax.ppermute(value, BOTH, [(i, i ^ masks[i & 1]) for i in range(2 ** coun...]
  transfers between devices with their start and end apart: 8 -> 29, of which waited for: 5 -> 12; matrix products, arithmetic and copies ran while one was open for 53% -> 36% of each run, Pallas kernels for 0% -> 13%
where the time goes in v1:
time: 352 us; the launch traced here: 348 us
  matrix products  85 us (24%)
  waiting for transfers between devices  73.5 us (21%)
  other arithmetic  54.9 us (16%)
  Pallas kernels  46.1 us (13%)
  local copies, waits for them, and re-layouts  35.7 us (10%)
  starting transfers between devices  34.5 us (10%)
  between operations  18.1 us (5%)
    ppermute x27, waiting for transfers between devices, exchange(): lax.ppermute(value, BOTH, [(i, i ^ masks[i & 1]) for i in range(2 ** coun...  73.4 us
    ppermute x27, starting transfers between devices, exchange(): lax.ppermute(value, BOTH, [(i, i ^ masks[i & 1]) for i in range(2 ** coun...  34.4 us
    pallas_call x1, Pallas kernels, row_back(): pl.pallas_call(attend_back_kernel, name='attend_backward', grid=(blocks,)...  27.2 us
    unnamed x78, local copies, waits for them, and re-layouts  20.6 us
    pallas_call x1, Pallas kernels, attend_row(): pl.pallas_call(attend_kernel, name='attend_forward', grid=(blocks,), in_s...  18.9 us
    dot_general x1, matrix products, body(): jnp.dot(grad_seed, down_full.T, preferred_element_type=jnp.float32)  18.3 us
    add x17, other arithmetic, add_exchange(): mine.astype(jnp.float32)  13.7 us
    dot_general x1, matrix products, body(): hidden = jnp.dot(normed_two, up_full, preferred_element_type=jnp.float32)  10.5 us
  transfers between devices with their start and end apart: 29, of which 12 were waited for; matrix products, arithmetic and copies ran while one was open for 36% of the time, Pallas kernels for 13%

profile of v1, /device:TPU:0, one launch (start us, length us, event | category | flops | bytes accessed | tf_op | source)
XLA Modules:
  0.0 347.8 jit_solution(17545991802426599068)
XLA Ops:
  7.2 1.6 pad_maximum_fusion
  10.6 4.1 %collective-permute-start = (bf16[24,2432]{1,0:T(8,128)(2,1)S(1)}, bf16[24,2432]{1,0:T(8,128)(2,1)S(1)}, u32[]{:S(2)}, u32[]{:S(2)}) collective-permute-start(bf16[24,2432]{1,0:T(8,128)(2,1)S(1)} %fusion.52), channel_id=1, source_target_pairs={{0,8},{1,9},{2,10},{3,11},{4,12},{5,13},{6,14},{7,15},{8,0},{9,1},... | collective-permute-start | bytes 350216 | tf_op jit(solution)/shard_map/ppermute | solution.py:264
  14.8 5.7 %collective-permute-done = bf16[24,2432]{1,0:T(8,128)(2,1)S(1)} collective-permute-done((bf16[24,2432]{1,0:T(8,128)(2,1)S(1)}, bf16[24,2432]{1,0:T(8,128)(2,1)S(1)}, u32[]{:S(2)}, u32[]{:S(2)}) %collective-permute-start) | collective-permute-done | bytes 116768 | tf_op jit(solution)/shard_map/ppermute | solution.py:264
  21.4 7.4 %collective-permute-done.1 = bf16[2,24,2432]{2,1,0:T(8,128)(2,1)S(1)} collective-permute-done((bf16[2,24,2432]{2,1,0:T(8,128)(2,1)S(1)}, bf16[2,24,2432]{2,1,0:T(8,128)(2,1)S(1)}, u32[]{:S(2)}, u32[]{:S(2)}) %collective-permute-start.1) | collective-permute-done | bytes 233504 | tf_op jit(solution)/shard_map/ppermute | solution.py:264
  29.1 1.4 collective-permute-start.2
  30.4 4.5 %collective-permute-start.4 = (bf16[96,768]{1,0:T(8,128)(2,1)}, bf16[96,768]{1,0:T(8,128)(2,1)S(1)}, u32[]{:S(2)}, u32[]{:S(2)}) collective-permute-start(bf16[96,768]{1,0:T(8,128)(2,1)} %param.18), channel_id=1, source_target_pairs={{0,8},{1,9},{2,10},{3,11},{4,12},{5,13},{6,14},{7,15},{8,0},{9,1},... | collective-permute-start | bytes 442376 | tf_op jit(solution)/shard_map/ppermute | solution.py:264
  35.0 6.2 %collective-permute-done.4 = bf16[96,768]{1,0:T(8,128)(2,1)S(1)} collective-permute-done((bf16[96,768]{1,0:T(8,128)(2,1)}, bf16[96,768]{1,0:T(8,128)(2,1)S(1)}, u32[]{:S(2)}, u32[]{:S(2)}) %collective-permute-start.4) | collective-permute-done | bytes 147488 | tf_op jit(solution)/shard_map/ppermute | solution.py:264
  44.2 13.2 %collective-permute-done.5 = bf16[2,96,768]{2,1,0:T(8,128)(2,1)S(1)} collective-permute-done((bf16[2,96,768]{2,1,0:T(8,128)(2,1)S(1)}, bf16[2,96,768]{2,1,0:T(8,128)(2,1)S(1)}, u32[]{:S(2)}, u32[]{:S(2)}) %collective-permute-start.5) | collective-permute-done | bytes 294944 | tf_op jit(solution)/shard_map/ppermute | solution.py:264
  58.7 2.2 select_select_fusion.1
  61.6 2.2 copy.80
  64.1 1.5 collective-permute-start.7
  66.1 16.8 %collective-permute-done.7 = bf16[2,2,96,768]{3,2,1,0:T(8,128)(2,1)S(1)} collective-permute-done((bf16[2,2,96,768]{3,2,1,0:T(8,128)(2,1)S(1)}, bf16[2,2,96,768]{3,2,1,0:T(8,128)(2,1)S(1)}, u32[]{:S(2)}, u32[]{:S(2)}) %collective-permute-start.7) | collective-permute-done | bytes 589856 | tf_op jit(solution)/shard_map/ppermute | solution.py:264
  83.1 3.0 bitcast_select_fusion.1
  87.0 5.8 %convolution_convert_fusion.project_ref = bf16[1024,2304]{1,0:T(8,128)(2,1)} fusion(bf16[768,2432]{1,0:T(8,128)(2,1)S(1)} %bitcast_select_fusion.1, bf16[1,1024,768]{1,2,0:T(8,128)(2,1)S(1)} %copy.80, f32[768]{0:T(1024)S(1)} %get-tuple-element.110, f32[768]{0:T(1024)S(1)} %get-tuple-element.111, f32[1024]{0:T(1024)S(1)} %add_rsqrt_fusion.1, ...), kind=kOutput, calls=%fused_computation.10 | convolution fusion | flops 3630956544 | bytes 9846784 | tf_op jit(solution)/shard_map/dot_general | solution.py:400
  92.8 1.5 collective-permute-start.8
  95.0 2.6 copy.84
  97.7 18.9 %attend_forward.1 = (bf16[1024,768]{1,0:T(8,128)(2,1)}, f32[16,1024]{1,0:T(8,128)}, f32[8,384,128]{2,1,0:T(8,128)}, f32[8,128]{1,0:T(8,128)}) custom-call(f32[1]{0:T(128)S(6)} %copy.134.limit_ref, s32[1,1024]{1,0:T(1,128)} %seg_ref.1, bf16[1024,2304]{1,0:T(8,128)(2,1)} %convolution_convert_fusion.project_ref), custom_call_target="tpu_custom_call" | custom-call | flops 1207959552 | bytes 7864320 | tf_op jit(solution)/shard_map/attend_forward/pallas_call | solution.py:120
  116.6 1.4 slice_reduce_fusion.5
  118.0 2.8 select_select_fusion
  120.8 3.7 %fusion.71 = (f32[1024]{0:T(1024)S(1)}, f32[1024,768]{0,1:T(8,128)S(1)}) fusion(bf16[1024,768]{1,0:T(8,128)(2,1)} %get-tuple-element.45, bf16[768,3840]{1,0:T(8,128)(2,1)} %all-gather.2.cloned.1.call-done, bf16[1,1024,768]{1,2,0:T(8,128)(2,1)} %copy-done.2), kind=kOutput, calls=%fused_computation.184 | convolution fusion | flops 1210317824 | bytes 7475200 | tf_op jit(solution)/shard_map/dot_general | solution.py:411
  125.5 2.2 copy-done.24
  127.7 10.5 %multiply_convert_fusion = (bf16[1024,3072]{1,0:T(8,128)(2,1)S(1)}, f32[1024,3072]{1,0:T(8,128)}) fusion(bf16[1024,768]{0,1:T(8,128)(2,1)S(1)} %add_convert_fusion.1, bf16[768,3840]{1,0:T(8,128)(2,1)S(1)} %copy-done.24), kind=kOutput, calls=%fused_computation.9 | convolution fusion | flops 4860149760 | bytes 25165824 | tf_op jit(solution)/shard_map/dot_general | solution.py:415
  138.3 2.6 copy-done.27
  140.9 6.8 %fusion.36 = bf16[3072,768]{1,0:T(8,128)(2,1)} fusion(bf16[1024,3072]{1,0:T(8,128)(2,1)S(1)} %get-tuple-element.61, bf16[1,1024,768]{1,2,0:T(8,128)(2,1)S(1)} %copy-done.8, pred[1024]{0:T(1024)(128)(4,1)S(1)} %compare_reduce_fusion), kind=kOutput, calls=%fused_computation.66 | convolution fusion | flops 4832624640 | bytes 12583936 | tf_op jit(solution)/shard_map/dot_general | solution.py:420
  147.7 3.1 bitcast_select_fusion
  150.8 18.3 %fusion.6 = bf16[1024,3072]{1,0:T(8,128)(2,1)} fusion(f32[1024,3072]{1,0:T(8,128)} %get-tuple-element.129, bf16[3072,768]{1,0:T(8,128)(2,1)S(1)} %bitcast_select_fusion, bf16[1,1024,768]{1,2,0:T(8,128)(2,1)S(1)} %copy-done.9, pred[1024]{0:T(1024)(128)(4,1)S(1)} %compare_reduce_fusion), kind=kOutput, calls=%fused_computation.8 | convolution fusion | flops 4895539200 | bytes 25166848 | tf_op jit(solution)/shard_map/dot_general | solution.py:425
  169.1 8.4 %convolution_convert_fusion.1 = bf16[768,3072]{1,0:T(8,128)(2,1)S(1)} fusion(bf16[1024,768]{0,1:T(8,128)(2,1)S(1)} %copy-done.22, bf16[1024,3072]{1,0:T(8,128)(2,1)} %fusion.6), kind=kOutput, calls=%fused_computation.11 | convolution fusion | flops 4834197504 | bytes 12582912 | tf_op jit(solution)/shard_map/dot_general | solution.py:428
  177.5 2.1 copy-done.15
  179.7 1.6 dynamic-slice_bitcast_fusion
  181.3 6.7 %fusion.72 = (f32[768]{0:T(1024)S(1)}, f32[1024,768]{1,0:T(8,128)}) fusion(bf16[1024,3072]{1,0:T(8,128)(2,1)S(1)} %copy-done.26, bf16[768,3840]{1,0:T(8,128)(2,1)S(1)} %bitcast.252), kind=kOutput, calls=%fused_computation.185 | convolution fusion | flops 4832623616 | bytes 14158848 | tf_op jit(solution)/shard_map/dot_general | solution.py:431
  188.0 3.5 %copy.87 = f32[1024,768]{0,1:T(8,128)} copy(f32[1024,768]{1,0:T(8,128)} %get-tuple-element.131) | data formatting | bytes 6291456 | tf_op jit(solution)/shard_map/dot_general | solution.py:431
  191.6 3.0 multiply_reduce_fusion
  196.3 1.4 convolution_convert_fusion.4
  198.5 2.5 convert_add_fusion
  201.6 1.8 fusion.31
  204.0 3.9 %fusion.38 = bf16[1,1024,768]{2,1,0:T(8,128)(2,1)} fusion(bf16[1024,768]{0,1:T(8,128)(2,1)S(1)} %fusion.69, bf16[768,3840]{1,0:T(8,128)(2,1)} %all-gather.2.cloned.1.call-done), kind=kOutput, calls=%fused_computation.70 | convolution fusion | flops 1208745984 | bytes 4325376 | tf_op jit(solution)/shard_map/dot_general | solution.py:441
  209.9 1.4 collective-permute-start.13
  211.3 1.4 pad_maximum_fusion.3
  212.9 27.2 %attend_backward.1 = bf16[1024,2304]{1,0:T(8,128)(2,1)} custom-call(bf16[1024,2304]{1,0:T(8,128)(2,1)} %convolution_convert_fusion.project_ref, bf16[1024,768]{1,0:T(8,128)(2,1)} %bitcast.239, f32[16,1024]{1,0:T(8,128)} %get-tuple-element.55.lse_ref, f32[8,384,128]{2,1,0:T(8,128)} %get-tuple-element.56.bias_ref), custom_call_target="tpu_custom_call" | custom-call | flops 3019898880 | bytes 11010048 | tf_op jit(solution)/shard_map/attend_backward/pallas_call | solution.py:224
  240.1 1.5 fusion.46
  241.6 3.6 %fusion.32 = f32[2,2,2,24,3072]{4,3,1,2,0:T(8,128)S(1)} fusion(bf16[2,2,2,24,3072]{4,3,1,2,0:T(8,128)(2,1)} %collective-permute-done.12, pred[]{:T(512)S(6)} %eq.75, f32[2,2,2,2,24,3072]{5,4,3,2,1,0:T(8,128)} %copy-done.5, s32[]{:T(128)S(6)} %select_n.254, s32[]{:T(128)S(6)} %select_n.255), kind=kLoop, calls=%fused_computation.55 | loop fusion | flops 1769472 | bytes 8257545 | tf_op jit(solution)/shard_map/add | solution.py:312
  246.6 4.5 %convolution_convert_fusion.2 = bf16[768,2304]{1,0:T(8,128)(2,1)S(1)} fusion(bf16[1024,2304]{1,0:T(8,128)(2,1)S(1)} %bitcast.229, bf16[1,1024,768]{1,2,0:T(8,128)(2,1)S(1)} %copy-done.3, f32[768]{0:T(1024)S(1)} %get-tuple-element.110, f32[768]{0:T(1024)S(1)} %get-tuple-element.111, f32[1024]{0:T(1024)S(1)} %add_rsqrt_fusion.1, ...), kind=kOutput, calls=%fused_computation.12 | convolution fusion | flops 3630366720 | bytes 9844736 | tf_op jit(solution)/shard_map/dot_general | solution.py:455
  251.3 5.7 %collective-permute-done.19 = bf16[2,2,24,3840]{3,2,0,1:T(8,128)(2,1)S(1)} collective-permute-done((bf16[2,2,24,3840]{3,2,0,1:T(8,128)(2,1)S(1)}, bf16[2,2,24,3840]{3,2,0,1:T(8,128)(2,1)S(1)}, u32[]{:S(2)}, u32[]{:S(2)}) %collective-permute-start.19) | collective-permute-done | bytes 737312 | tf_op jit(solution)/shard_map/ppermute | solution.py:264
  257.3 1.6 collective-permute-start.20
  258.8 9.5 %fusion.39 = bf16[1,1024,768]{1,2,0:T(8,128)(2,1)} fusion(f32[1024,768]{0,1:T(8,128)S(1)} %get-tuple-element.127, bf16[1024,3072]{1,0:T(8,128)(2,1)} %copy-done.27, bf16[3072,768]{1,0:T(8,128)(2,1)S(1)} %bitcast.231), kind=kOutput, calls=%fused_computation.71 | convolution fusion | flops 4833411072 | bytes 15728640 | tf_op jit(solution)/shard_map/dot_general | solution.py:458
  268.3 6.7 %collective-permute-done.20 = bf16[2,24,3840]{2,1,0:T(8,128)(2,1)S(1)} collective-permute-done((bf16[2,24,3840]{2,1,0:T(8,128)(2,1)S(1)}, bf16[2,24,3840]{2,1,0:T(8,128)(2,1)S(1)}, u32[]{:S(2)}, u32[]{:S(2)}) %collective-permute-start.20) | collective-permute-done | bytes 368672 | tf_op jit(solution)/shard_map/ppermute | solution.py:264
  275.9 2.0 collective-permute-start.21
  277.9 2.2 convert_add_fusion.1
  280.1 5.5 %fusion.73 = (f32[768]{0:T(1024)S(1)}, f32[1024,768]{1,0:T(8,128)}) fusion(bf16[1024,2304]{1,0:T(8,128)(2,1)S(1)} %bitcast.229, bf16[768,2432]{1,0:T(8,128)(2,1)S(1)} %copy-done.17), kind=kOutput, calls=%fused_computation.186 | convolution fusion | flops 3624664320 | bytes 11406336 | tf_op jit(solution)/shard_map/dot_general | solution.py:464
  285.7 3.7 %copy.97 = f32[1024,768]{0,1:T(8,128)} copy(f32[1024,768]{1,0:T(8,128)} %get-tuple-element.133) | data formatting | bytes 6291456 | tf_op jit(solution)/shard_map/dot_general | solution.py:464
  289.4 3.7 %fusion.26 = (f32[768]{0:T(1024)S(1)}, f32[1024]{0:T(1024)S(1)}, f32[1024]{0:T(1024)S(1)}) fusion(f32[1024,768]{0,1:T(8,128)} %copy.97, bf16[1,1024,768]{1,2,0:T(8,128)(2,1)} %copy-done.2, f32[1024]{0:T(1024)S(1)} %add_rsqrt_fusion.1, f32[1024]{0:T(1024)S(1)} %broadcast_multiply_fusion.5, f32[768]{0:T(1024)S(1)} %get-tuple-element.111), kind=kLoop, calls=%fused_computation.38 | loop fusion | flops 7075072 | bytes 4741120 | tf_op jit(solution)/shard_map/reduce_sum | solution.py:29
  296.2 2.3 fusion.33
  298.5 2.1 collective-permute-start.15
  300.7 3.6 %collective-permute-done.24 = f32[2,2,1,128]{3,1,0,2:T(2,128)S(1)} collective-permute-done((f32[2,2,1,128]{3,1,0,2:T(2,128)S(1)}, f32[2,2,1,128]{3,1,0,2:T(2,128)S(1)}, u32[]{:S(2)}, u32[]{:S(2)}) %collective-permute-start.24) | collective-permute-done | bytes 2080 | tf_op jit(solution)/shard_map/ppermute | solution.py:264
  304.3 3.2 collective-permute-start.25
  307.5 1.6 collective-permute-done.25
  309.0 1.5 collective-permute-start.26
  313.5 4.7 %fusion.25 = f32[1,1024,768]{1,2,0:T(8,128)} fusion(bf16[1,1024,768]{1,2,0:T(8,128)(2,1)S(1)} %copy-done.4, f32[1024,768]{0,1:T(8,128)S(1)} %copy-done.6, f32[1024]{0:T(1024)S(1)} %broadcast_multiply_fusion, f32[1024]{0:T(1024)S(1)} %broadcast_multiply_fusion.1, f32[768]{0:T(1024)S(1)} %get-tuple-element.111, f32[1024]{0:T(1024)S(1)} %add_rsqrt_fusion.1, ...), kind=kLoop, calls=%fused_computation.37 | loop fusion | flops 14942208 | bytes 15768576 | tf_op jit(solution)/shard_map/reshape | solution.py:468
  318.2 2.7 copy.107
  320.9 2.4 copy.108
  323.3 1.4 bitcast_add_fusion.1
  324.7 3.6 %collective-permute-start.17 = (bf16[2,24,2304]{2,1,0:T(8,128)(2,1)S(1)}, bf16[2,24,2304]{2,1,0:T(8,128)(2,1)S(1)}, u32[]{:S(2)}, u32[]{:S(2)}) collective-permute-start(bf16[2,24,2304]{2,1,0:T(8,128)(2,1)S(1)} %fusion.50), channel_id=1, source_target_pairs={{0,4},{1,5},{2,6},{3,7},{4,0},{5,1},{6,2},{7,3},{8,12},{9,13},{10,... | collective-permute-start | bytes 663560 | tf_op jit(solution)/shard_map/ppermute | solution.py:264
  328.9 4.2 %collective-permute-done.17 = bf16[2,24,2304]{2,1,0:T(8,128)(2,1)S(1)} collective-permute-done((bf16[2,24,2304]{2,1,0:T(8,128)(2,1)S(1)}, bf16[2,24,2304]{2,1,0:T(8,128)(2,1)S(1)}, u32[]{:S(2)}, u32[]{:S(2)}) %collective-permute-start.17) | collective-permute-done | bytes 221216 | tf_op jit(solution)/shard_map/ppermute | solution.py:264
  336.3 1.6 convert_element_type.196
  (189 shorter events, 29.6 us)
Async XLA Ops:
  7.2 113.6 %all-gather.2.cloned.1.call-start = ((), (), s32[]{:S(2)}) async-start(), calls=%async_computation.1 | async-start | bytes 6082560 | tf_op jit(solution)/shard_map/all_gather | solution.py:383
  8.9 327.4 %reduce-scatter.2.cloned.1.call-start = ((), (), s32[]{:S(2)}) async-start(), calls=%async_computation.2 | async-start | bytes 4866048 | tf_op jit(solution)/shard_map/reduce_scatter | solution.py:422
  10.6 9.8 %collective-permute-start = (bf16[24,2432]{1,0:T(8,128)(2,1)S(1)}, bf16[24,2432]{1,0:T(8,128)(2,1)S(1)}, u32[]{:S(2)}, u32[]{:S(2)}) collective-permute-start(bf16[24,2432]{1,0:T(8,128)(2,1)S(1)} %fusion.52), channel_id=1, source_target_pairs={{0,8},{1,9},{2,10},{3,11},{4,12},{5,13},{6,14},{7,15},{8,0},{9,1},... | collective-permute-start | bytes 350216 | tf_op jit(solution)/shard_map/ppermute | solution.py:264
  20.6 8.2 %collective-permute-start.1 = (bf16[2,24,2432]{2,1,0:T(8,128)(2,1)S(1)}, bf16[2,24,2432]{2,1,0:T(8,128)(2,1)S(1)}, u32[]{:S(2)}, u32[]{:S(2)}) collective-permute-start(bf16[2,24,2432]{2,1,0:T(8,128)(2,1)S(1)} %broadcast_select_fusion.9), channel_id=1, source_target_pairs={{0,4},{1,5},{2,6},{3,7},{4,0},{5,1},{6,2},{7,3},{8,12},{9,13},{10,... | collective-permute-start | bytes 700424 | tf_op jit(solution)/shard_map/ppermute | solution.py:264
  29.1 13.5 %collective-permute-start.2 = (bf16[2,2,24,2432]{3,2,1,0:T(8,128)(2,1)S(1)}, bf16[2,2,24,2432]{3,2,1,0:T(8,128)(2,1)S(1)}, u32[]{:S(2)}, u32[]{:S(2)}) collective-permute-start(bf16[2,2,24,2432]{3,2,1,0:T(8,128)(2,1)S(1)} %broadcast_select_fusion.7), channel_id=1, source_target_pairs={{0,16},{1,3},{2,18},{3,1},{4,20},{5,7},{6,22},{7,5},{8,24},{9,11},... | collective-permute-start | bytes 1400840 | tf_op jit(solution)/shard_map/ppermute | solution.py:264
  30.4 10.7 %collective-permute-start.4 = (bf16[96,768]{1,0:T(8,128)(2,1)}, bf16[96,768]{1,0:T(8,128)(2,1)S(1)}, u32[]{:S(2)}, u32[]{:S(2)}) collective-permute-start(bf16[96,768]{1,0:T(8,128)(2,1)} %param.18), channel_id=1, source_target_pairs={{0,8},{1,9},{2,10},{3,11},{4,12},{5,13},{6,14},{7,15},{8,0},{9,1},... | collective-permute-start | bytes 442376 | tf_op jit(solution)/shard_map/ppermute | solution.py:264
  42.2 15.2 %collective-permute-start.5 = (bf16[2,96,768]{2,1,0:T(8,128)(2,1)S(1)}, bf16[2,96,768]{2,1,0:T(8,128)(2,1)S(1)}, u32[]{:S(2)}, u32[]{:S(2)}) collective-permute-start(bf16[2,96,768]{2,1,0:T(8,128)(2,1)S(1)} %broadcast_select_fusion.8), channel_id=1, source_target_pairs={{0,4},{1,5},{2,6},{3,7},{4,0},{5,1},{6,2},{7,3},{8,12},{9,13},{10,... | collective-permute-start | bytes 884744 | tf_op jit(solution)/shard_map/ppermute | solution.py:264
  42.9 15.8 %collective-permute-start.3 = (bf16[2,2,2,24,2432]{4,3,0,2,1:T(8,128)(2,1)S(1)}, bf16[2,2,2,24,2432]{4,3,0,2,1:T(8,128)(2,1)S(1)}, u32[]{:S(2)}, u32[]{:S(2)}) collective-permute-start(bf16[2,2,2,24,2432]{4,3,0,2,1:T(8,128)(2,1)S(1)} %broadcast_select_fusion.5), channel_id=1, source_target_pairs={{0,2},{1,17},{2,0},{3,19},{4,6},{5,21},{6,4},{7,23},{8,10},{9,25},... | collective-permute-start | bytes 2801672 | tf_op jit(solution)/shard_map/ppermute | solution.py:264
  61.0 3.1 copy-start.18
  61.0 22.1 %collective-permute-start.6 = (bf16[2,2,2,2,24,2432]{5,4,3,2,1,0:T(8,128)(2,1)}, bf16[2,2,2,2,24,2432]{5,4,3,2,1,0:T(8,128)(2,1)}, u32[]{:S(2)}, u32[]{:S(2)}) collective-permute-start(bf16[2,2,2,2,24,2432]{5,4,3,2,1,0:T(8,128)(2,1)} %select_select_fusion.1), channel_id=1, source_target_pairs={{0,1},{1,0},{2,3},{3,2},{4,5},{5,4},{6,7},{7,6},{8,9},{9,8},{10,11... | collective-permute-start | bytes 5603336 | tf_op jit(solution)/shard_map/ppermute | solution.py:264
  63.8 23.1 %copy-start.2 = (bf16[1,1024,768]{1,2,0:T(8,128)(2,1)}, bf16[1,1024,768]{1,2,0:T(8,128)(2,1)S(1)}, u32[]{:S(2)}) copy-start(bf16[1,1024,768]{1,2,0:T(8,128)(2,1)S(1)} %copy.80) | copy-start | bytes 4718596
  63.8 19.0 %copy-start.19 = (bf16[2,2,96,768]{3,2,1,0:T(8,128)(2,1)S(1)}, bf16[2,2,96,768]{3,2,1,0:T(8,128)(2,1)}, u32[]{:S(2)}) copy-start(bf16[2,2,96,768]{3,2,1,0:T(8,128)(2,1)} %broadcast_select_fusion.6) | copy-start | bytes 1769476
  64.1 18.7 %collective-permute-start.7 = (bf16[2,2,96,768]{3,2,1,0:T(8,128)(2,1)S(1)}, bf16[2,2,96,768]{3,2,1,0:T(8,128)(2,1)S(1)}, u32[]{:S(2)}, u32[]{:S(2)}) collective-permute-start(bf16[2,2,96,768]{3,2,1,0:T(8,128)(2,1)S(1)} %copy-done.18), channel_id=1, source_target_pairs={{0,16},{1,3},{2,18},{3,1},{4,20},{5,7},{6,22},{7,5},{8,24},{9,11},... | collective-permute-start | bytes 1769480 | tf_op jit(solution)/shard_map/ppermute | solution.py:264
  86.1 6.7 %copy-start.16 = (bf16[768,2432]{1,0:T(8,128)(2,1)}, bf16[768,2432]{1,0:T(8,128)(2,1)S(1)}, u32[]{:S(2)}) copy-start(bf16[768,2432]{1,0:T(8,128)(2,1)S(1)} %bitcast_select_fusion.1) | copy-start | bytes 11206660
  92.8 4.9 %copy-start.23 = (s32[1,1024]{1,0:T(1,128)S(1)}, s32[1,1024]{1,0:T(1,128)}, u32[]{:S(2)}) copy-start(s32[1,1024]{1,0:T(1,128)} %seg_ref.1) | copy-start | bytes 12292
  92.8 25.2 %collective-permute-start.8 = (bf16[2,2,2,96,768]{4,3,2,1,0:T(8,128)(2,1)S(1)}, bf16[2,2,2,96,768]{4,3,2,1,0:T(8,128)(2,1)S(1)}, u32[]{:S(2)}, u32[]{:S(2)}) collective-permute-start(bf16[2,2,2,96,768]{4,3,2,1,0:T(8,128)(2,1)S(1)} %broadcast_select_fusion.3), channel_id=1, source_target_pairs={{0,2},{1,17},{2,0},{3,19},{4,6},{5,21},{6,4},{7,23},{8,10},{9,25},... | collective-permute-start | bytes 3538952 | tf_op jit(solution)/shard_map/ppermute | solution.py:264
  124.5 3.2 copy-start.24
  125.4 12.8 %copy-start.21 = (bf16[1024,768]{0,1:T(8,128)(2,1)}, bf16[1024,768]{0,1:T(8,128)(2,1)S(1)}, u32[]{:S(2)}) copy-start(bf16[1024,768]{0,1:T(8,128)(2,1)S(1)} %add_convert_fusion.1) | copy-start | bytes 4718596
  125.4 15.4 %copy-start.8 = (bf16[1,1024,768]{1,2,0:T(8,128)(2,1)S(1)}, bf16[1,1024,768]{1,2,0:T(8,128)(2,1)}, u32[]{:S(2)}) copy-start(bf16[1,1024,768]{1,2,0:T(8,128)(2,1)} %copy.84) | copy-start | bytes 4718596
  125.4 22.3 %collective-permute-start.9 = (bf16[2,2,2,2,96,768]{5,4,3,2,1,0:T(8,128)(2,1)}, bf16[2,2,2,2,96,768]{5,4,3,2,1,0:T(8,128)(2,1)}, u32[]{:S(2)}, u32[]{:S(2)}) collective-permute-start(bf16[2,2,2,2,96,768]{5,4,3,2,1,0:T(8,128)(2,1)} %select_select_fusion), channel_id=1, source_target_pairs={{0,1},{1,0},{2,3},{3,2},{4,5},{5,4},{6,7},{7,6},{8,9},{9,8},{10,11... | collective-permute-start | bytes 7077896 | tf_op jit(solution)/shard_map/ppermute | solution.py:264
  138.3 2.6 copy-start.27
  147.7 3.1 copy-start.9
  147.7 33.6 %slice-start.6 = ((s8[5898240]{0:T(1024)(128)(4,1)}), s8[4194304]{0:T(1024)(128)(4,1)S(1)}, s32[]{:S(2)}) async-start(s8[5898240]{0:T(1024)(128)(4,1)} %bitcast.251), calls=%async_computation.9 | async-start | bytes 8388608
  150.8 18.3 %copy-start.14 = (bf16[3072,768]{1,0:T(8,128)(2,1)}, bf16[3072,768]{1,0:T(8,128)(2,1)S(1)}, u32[]{:S(2)}) copy-start(bf16[3072,768]{1,0:T(8,128)(2,1)S(1)} %bitcast_select_fusion) | copy-start | bytes 14155780
  150.8 18.3 %copy-start.22 = (bf16[1024,768]{0,1:T(8,128)(2,1)S(1)}, bf16[1024,768]{0,1:T(8,128)(2,1)}, u32[]{:S(2)}) copy-start(bf16[1024,768]{0,1:T(8,128)(2,1)} %copy-done.21) | copy-start | bytes 4718596
  150.8 30.5 %slice-start.7 = ((s8[5898240]{0:T(1024)(128)(4,1)}), s8[1703936]{0:T(1024)(128)(4,1)S(1)}, s32[]{:S(2)}) async-start(s8[5898240]{0:T(1024)(128)(4,1)} %bitcast.251), calls=%async_computation.10 | async-start | bytes 3407872
  169.1 12.2 %copy-start.26 = (bf16[1024,3072]{1,0:T(8,128)(2,1)S(1)}, bf16[1024,3072]{1,0:T(8,128)(2,1)}, u32[]{:S(2)}) copy-start(bf16[1024,3072]{1,0:T(8,128)(2,1)} %fusion.6) | copy-start | bytes 18874372
  177.5 2.2 copy-start.15
  181.3 16.4 %collective-permute-start.10 = (bf16[2,2,2,2,24,3072]{5,4,3,2,1,0:T(8,128)(2,1)}, bf16[2,2,2,2,24,3072]{5,4,3,2,1,0:T(8,128)(2,1)}, u32[]{:S(2)}, u32[]{:S(2)}) collective-permute-start(bf16[2,2,2,2,24,3072]{5,4,3,2,1,0:T(8,128)(2,1)} %dynamic-slice_bitcast_fusion), channel_id=1, source_target_pairs={{0,1},{1,0},{2,3},{3,2},{4,5},{5,4},{6,7},{7,6},{8,9},{9,8},{10,11... | collective-permute-start | bytes 7077896 | tf_op jit(solution)/shard_map/ppermute | solution.py:264
  191.6 3.0 copy-start
  191.6 3.3 copy-start.10
  194.9 1.4 copy-start.25
  194.9 2.9 slice-start.4
  196.3 2.2 slice-start.5
  201.0 6.8 %copy-start.5 = (f32[2,2,2,2,24,3072]{5,4,3,2,1,0:T(8,128)}, f32[2,2,2,2,24,3072]{5,4,3,2,1,0:T(8,128)S(1)}, u32[]{:S(2)}) copy-start(f32[2,2,2,2,24,3072]{5,4,3,2,1,0:T(8,128)S(1)} %convert_add_fusion) | copy-start | bytes 14155780
  201.1 6.8 %collective-permute-start.11 = (bf16[2,2,2,2,24,768]{5,4,3,2,1,0:T(8,128)(2,1)S(1)}, bf16[2,2,2,2,24,768]{5,4,3,2,1,0:T(8,128)(2,1)S(1)}, u32[]{:S(2)}, u32[]{:S(2)}) collective-permute-start(bf16[2,2,2,2,24,768]{5,4,3,2,1,0:T(8,128)(2,1)S(1)} %dynamic-slice_bitcast_fusion.2), channel_id=1, source_target_pairs={{0,1},{1,0},{2,3},{3,2},{4,5},{5,4},{6,7},{7,6},{8,9},{9,8},{10,11... | collective-permute-start | bytes 1769480 | tf_op jit(solution)/shard_map/ppermute | solution.py:264
  203.4 38.2 %collective-permute-start.12 = (bf16[2,2,2,24,3072]{4,3,1,2,0:T(8,128)(2,1)}, bf16[2,2,2,24,3072]{4,3,1,2,0:T(8,128)(2,1)}, u32[]{:S(2)}, u32[]{:S(2)}) collective-permute-start(bf16[2,2,2,24,3072]{4,3,1,2,0:T(8,128)(2,1)} %fusion.31), channel_id=1, source_target_pairs={{0,2},{1,17},{2,0},{3,19},{4,6},{5,21},{6,4},{7,23},{8,10},{9,25},... | collective-permute-start | bytes 3538952 | tf_op jit(solution)/shard_map/ppermute | solution.py:264
  209.9 30.2 %collective-permute-start.13 = (bf16[2,2,2,24,768]{4,3,1,2,0:T(8,128)(2,1)}, bf16[2,2,2,24,768]{4,3,1,2,0:T(8,128)(2,1)S(1)}, u32[]{:S(2)}, u32[]{:S(2)}) collective-permute-start(bf16[2,2,2,24,768]{4,3,1,2,0:T(8,128)(2,1)} %fusion.45), channel_id=1, source_target_pairs={{0,2},{1,17},{2,0},{3,19},{4,6},{5,21},{6,4},{7,23},{8,10},{9,25},... | collective-permute-start | bytes 884744 | tf_op jit(solution)/shard_map/ppermute | solution.py:264
  240.1 6.1 %slice-start = ((s8[4718592]{0:T(1024)(128)(4,1)}), s8[4194304]{0:T(1024)(128)(4,1)S(1)}, s32[]{:S(2)}) async-start(s8[4718592]{0:T(1024)(128)(4,1)} %bitcast.228), calls=%async_computation.3 | async-start | bytes 8388608
  241.6 4.6 %slice-start.1 = ((s8[4718592]{0:T(1024)(128)(4,1)}), s8[524288]{0:T(1024)(128)(4,1)S(1)}, s32[]{:S(2)}) async-start(s8[4718592]{0:T(1024)(128)(4,1)} %bitcast.228), calls=%async_computation.4 | async-start | bytes 1048576
  245.2 1.4 copy-start.3
  245.4 13.4 %slice-start.2 = ((s8[4718592]{0:T(1024)(128)(4,1)}), s8[4194304]{0:T(1024)(128)(4,1)S(1)}, s32[]{:S(2)}) async-start(s8[4718592]{0:T(1024)(128)(4,1)} %bitcast.230), calls=%async_computation.5 | async-start | bytes 8388608
  245.5 13.3 %slice-start.3 = ((s8[4718592]{0:T(1024)(128)(4,1)}), s8[524288]{0:T(1024)(128)(4,1)S(1)}, s32[]{:S(2)}) async-start(s8[4718592]{0:T(1024)(128)(4,1)} %bitcast.230), calls=%async_computation.6 | async-start | bytes 1048576
  245.5 11.5 %collective-permute-start.19 = (bf16[2,2,24,3840]{3,2,0,1:T(8,128)(2,1)S(1)}, bf16[2,2,24,3840]{3,2,0,1:T(8,128)(2,1)S(1)}, u32[]{:S(2)}, u32[]{:S(2)}) collective-permute-start(bf16[2,2,24,3840]{3,2,0,1:T(8,128)(2,1)S(1)} %fusion.44), channel_id=1, source_target_pairs={{0,16},{1,3},{2,18},{3,1},{4,20},{5,7},{6,22},{7,5},{8,24},{9,11},... | collective-permute-start | bytes 2211848 | tf_op jit(solution)/shard_map/ppermute | solution.py:264
  251.3 26.6 %collective-permute-start.14 = (bf16[2,2,2,2,24,2304]{5,4,3,2,1,0:T(8,128)(2,1)S(1)}, bf16[2,2,2,2,24,2304]{5,4,3,2,1,0:T(8,128)(2,1)S(1)}, u32[]{:S(2)}, u32[]{:S(2)}) collective-permute-start(bf16[2,2,2,2,24,2304]{5,4,3,2,1,0:T(8,128)(2,1)S(1)} %dynamic-slice_bitcast_fusion.1), channel_id=1, source_target_pairs={{0,1},{1,0},{2,3},{3,2},{4,5},{5,4},{6,7},{7,6},{8,9},{9,8},{10,11... | collective-permute-start | bytes 5308424 | tf_op jit(solution)/shard_map/ppermute | solution.py:264
  257.3 17.8 %collective-permute-start.20 = (bf16[2,24,3840]{2,1,0:T(8,128)(2,1)S(1)}, bf16[2,24,3840]{2,1,0:T(8,128)(2,1)S(1)}, u32[]{:S(2)}, u32[]{:S(2)}) collective-permute-start(bf16[2,24,3840]{2,1,0:T(8,128)(2,1)S(1)} %fusion.48), channel_id=1, source_target_pairs={{0,4},{1,5},{2,6},{3,7},{4,0},{5,1},{6,2},{7,3},{8,12},{9,13},{10,... | collective-permute-start | bytes 1105928 | tf_op jit(solution)/shard_map/ppermute | solution.py:264
  275.1 5.0 %copy-start.20 = (f32[2,24,3840]{2,1,0:T(8,128)}, f32[2,24,3840]{2,1,0:T(8,128)S(1)}, u32[]{:S(2)}) copy-start(f32[2,24,3840]{2,1,0:T(8,128)S(1)} %bitcast_add_fusion.2) | copy-start | bytes 2211844
  275.9 4.2 %copy-start.17 = (bf16[768,2432]{1,0:T(8,128)(2,1)S(1)}, bf16[768,2432]{1,0:T(8,128)(2,1)}, u32[]{:S(2)}) copy-start(bf16[768,2432]{1,0:T(8,128)(2,1)} %copy-done.16) | copy-start | bytes 11206660
  275.9 17.6 %collective-permute-start.21 = (bf16[24,3840]{1,0:T(8,128)(2,1)}, bf16[24,3840]{1,0:T(8,128)(2,1)S(1)}, u32[]{:S(2)}, u32[]{:S(2)}) collective-permute-start(bf16[24,3840]{1,0:T(8,128)(2,1)} %fusion.51), channel_id=1, source_target_pairs={{0,8},{1,9},{2,10},{3,11},{4,12},{5,13},{6,14},{7,15},{8,0},{9,1},... | collective-permute-start | bytes 552968 | tf_op jit(solution)/shard_map/ppermute | solution.py:264
  293.3 18.5 %copy-start.7 = (f32[2,2,2,2,24,2304]{5,4,3,2,1,0:T(8,128)S(1)}, f32[2,2,2,2,24,2304]{5,4,3,2,1,0:T(8,128)}, u32[]{:S(2)}) copy-start(f32[2,2,2,2,24,2304]{5,4,3,2,1,0:T(8,128)} %convert_add_fusion.1) | copy-start | bytes 10616836
  293.4 2.6 collective-permute-start.22
  296.1 4.5 %collective-permute-start.23 = (f32[2,2,2,1,128]{4,2,1,0,3:T(2,128)S(1)}, f32[2,2,2,1,128]{4,2,1,0,3:T(2,128)S(1)}, u32[]{:S(2)}, u32[]{:S(2)}) collective-permute-start(f32[2,2,2,1,128]{4,2,1,0,3:T(2,128)S(1)} %bitcast_select_fusion.9), channel_id=1, source_target_pairs={{0,2},{1,17},{2,0},{3,19},{4,6},{5,21},{6,4},{7,23},{8,10},{9,25},... | collective-permute-start | bytes 12296 | tf_op jit(solution)/shard_map/ppermute | solution.py:264
  296.1 17.3 %copy-start.6 = (f32[1024,768]{0,1:T(8,128)S(1)}, f32[1024,768]{0,1:T(8,128)}, u32[]{:S(2)}) copy-start(f32[1024,768]{0,1:T(8,128)} %copy.97) | copy-start | bytes 9437188
  298.5 13.3 %collective-permute-start.15 = (bf16[2,2,2,24,2304]{4,3,1,2,0:T(8,128)(2,1)S(1)}, bf16[2,2,2,24,2304]{4,3,1,2,0:T(8,128)(2,1)S(1)}, u32[]{:S(2)}, u32[]{:S(2)}) collective-permute-start(bf16[2,2,2,24,2304]{4,3,1,2,0:T(8,128)(2,1)S(1)} %fusion.33), channel_id=1, source_target_pairs={{0,2},{1,17},{2,0},{3,19},{4,6},{5,21},{6,4},{7,23},{8,10},{9,25},... | collective-permute-start | bytes 2654216 | tf_op jit(solution)/shard_map/ppermute | solution.py:264
  300.6 3.7 %collective-permute-start.24 = (f32[2,2,1,128]{3,1,0,2:T(2,128)S(1)}, f32[2,2,1,128]{3,1,0,2:T(2,128)S(1)}, u32[]{:S(2)}, u32[]{:S(2)}) collective-permute-start(f32[2,2,1,128]{3,1,0,2:T(2,128)S(1)} %fusion.58), channel_id=1, source_target_pairs={{0,16},{1,3},{2,18},{3,1},{4,20},{5,7},{6,22},{7,5},{8,24},{9,11},... | collective-permute-start | bytes 6152 | tf_op jit(solution)/shard_map/ppermute | solution.py:264
  304.3 4.7 %collective-permute-start.25 = (f32[2,1,128]{2,1,0:T(1,128)S(1)}, f32[2,1,128]{2,1,0:T(1,128)S(1)}, u32[]{:S(2)}, u32[]{:S(2)}) collective-permute-start(f32[2,1,128]{2,1,0:T(1,128)S(1)} %fusion.61), channel_id=1, source_target_pairs={{0,4},{1,5},{2,6},{3,7},{4,0},{5,1},{6,2},{7,3},{8,12},{9,13},{10,... | collective-permute-start | bytes 3080 | tf_op jit(solution)/shard_map/ppermute | solution.py:264
  309.0 4.5 %copy-start.1 = (f32[1024,768]{0,1:T(8,128)S(1)}, f32[1024,768]{0,1:T(8,128)}, u32[]{:S(2)}) copy-start(f32[1024,768]{0,1:T(8,128)} %copy.87) | copy-start | bytes 9437188
  309.0 4.5 %copy-start.4 = (bf16[1,1024,768]{1,2,0:T(8,128)(2,1)S(1)}, bf16[1,1024,768]{1,2,0:T(8,128)(2,1)}, u32[]{:S(2)}) copy-start(bf16[1,1024,768]{1,2,0:T(8,128)(2,1)} %copy-done.2) | copy-start | bytes 4718596
  309.0 14.2 %collective-permute-start.26 = (f32[1,128]{1,0:T(1,128)S(1)}, f32[1,128]{1,0:T(1,128)S(1)}, u32[]{:S(2)}, u32[]{:S(2)}) collective-permute-start(f32[1,128]{1,0:T(1,128)S(1)} %fusion.64), channel_id=1, source_target_pairs={{0,8},{1,9},{2,10},{3,11},{4,12},{5,13},{6,14},{7,15},{8,0},{9,1},... | collective-permute-start | bytes 1544 | tf_op jit(solution)/shard_map/ppermute | solution.py:264
  312.0 1.4 copy-start.13
  313.0 10.3 %collective-permute-start.16 = (bf16[2,2,24,2304]{3,2,0,1:T(8,128)(2,1)}, bf16[2,2,24,2304]{3,2,0,1:T(8,128)(2,1)}, u32[]{:S(2)}, u32[]{:S(2)}) collective-permute-start(bf16[2,2,24,2304]{3,2,0,1:T(8,128)(2,1)} %fusion.47), channel_id=1, source_target_pairs={{0,16},{1,3},{2,18},{3,1},{4,20},{5,7},{6,22},{7,5},{8,24},{9,11},... | collective-permute-start | bytes 1327112 | tf_op jit(solution)/shard_map/ppermute | solution.py:264
  318.2 2.7 copy-start.11
  324.7 8.4 %collective-permute-start.17 = (bf16[2,24,2304]{2,1,0:T(8,128)(2,1)S(1)}, bf16[2,24,2304]{2,1,0:T(8,128)(2,1)S(1)}, u32[]{:S(2)}, u32[]{:S(2)}) collective-permute-start(bf16[2,24,2304]{2,1,0:T(8,128)(2,1)S(1)} %fusion.50), channel_id=1, source_target_pairs={{0,4},{1,5},{2,6},{3,7},{4,0},{5,1},{6,2},{7,3},{8,12},{9,13},{10,... | collective-permute-start | bytes 663560 | tf_op jit(solution)/shard_map/ppermute | solution.py:264
  333.2 5.8 %collective-permute-start.18 = (bf16[24,2304]{1,0:T(8,128)(2,1)S(1)}, bf16[24,2304]{1,0:T(8,128)(2,1)S(1)}, u32[]{:S(2)}, u32[]{:S(2)}) collective-permute-start(bf16[24,2304]{1,0:T(8,128)(2,1)S(1)} %fusion.53), channel_id=1, source_target_pairs={{0,8},{1,9},{2,10},{3,11},{4,12},{5,13},{6,14},{7,15},{8,0},{9,1},... | collective-permute-start | bytes 331784 | tf_op jit(solution)/shard_map/ppermute | solution.py:264
  (1 other events, 1.1 us)
Sparse Core Ops, SparseCore 0:
  11.5 79.8 all-gather.1
  212.8 111.6 reduce-scatter.1

commit v2 on v1

--- a/solution.py
+++ b/solution.py
@@ -4,6 +4,7 @@
 import jax.numpy as jnp
 from jax import lax
 from jax.experimental import pallas as pl
+from jax.experimental.layout import Layout, with_layout_constraint
 from jax.experimental.pallas import tpu as pltpu
 from jax.sharding import PartitionSpec as P
 
@@ -22,15 +23,6 @@
     inverse = lax.rsqrt(spread + EPSILON)
     unit = center * inverse
     return (unit * gain + shift, unit, inverse)
-
-
-def norm_backward(grad_normed, unit, inverse, gain):
-    grad_unit = grad_normed * gain
-    grad_gain = jnp.sum(grad_normed * unit, axis=0)
-    grad_shift = jnp.sum(grad_normed, axis=0)
-    centered = grad_unit - jnp.mean(grad_unit, axis=-1, keepdims=True)
-    grad_input = inverse * (centered - unit * jnp.mean(grad_unit * unit, axis=-1, keepdims=True))
-    return (grad_input, grad_gain, grad_shift)
 
 
 BLOCK = 128
@@ -140,7 +132,7 @@
         ],
         scratch_shapes=[pltpu.VMEM((length, BLOCK), jnp.float32)],
         cost_estimate=pl.CostEstimate(
-            flops=4 * length * SPAN * width, transcendentals=HEADS * length * SPAN, bytes_accessed=10 * length * width
+            flops=75 * length * SPAN * width, transcendentals=HEADS * length * SPAN, bytes_accessed=10 * length * width
         ),
     )(limit, seg_row[None], project_row)
 
@@ -240,9 +232,55 @@
             pltpu.VMEM((SPAN, BLOCK), jnp.float32),
         ],
         cost_estimate=pl.CostEstimate(
-            flops=10 * length * SPAN * width, transcendentals=HEADS * length * SPAN, bytes_accessed=14 * length * width
+            flops=105 * length * SPAN * width, transcendentals=HEADS * length * SPAN, bytes_accessed=14 * length * width
         ),
     )(project_row, grad_row, lse_row, bias_row)
+
+
+STRIP = 256
+
+
+def norm_back_kernel(grad_ref, weight_ref, value_ref, add_ref, gain_ref, out_ref, *rest):
+    sums_ref = rest[-1]
+
+    @pl.when(pl.program_id(0) == 0)
+    def _():
+        sums_ref[...] = jnp.zeros_like(sums_ref)
+
+    grad = dot_nt(grad_ref[...], weight_ref[...])
+    value = value_ref[...].astype(jnp.float32)
+    center = value - jnp.mean(value, axis=-1, keepdims=True)
+    inverse = lax.rsqrt(jnp.mean(center * center, axis=-1, keepdims=True) + EPSILON)
+    unit = center * inverse
+    sums_ref[0:1, :] += jnp.sum(grad * unit, axis=0, keepdims=True)
+    sums_ref[1:2, :] += jnp.sum(grad, axis=0, keepdims=True)
+    grad_unit = grad * gain_ref[...]
+    centered = grad_unit - jnp.mean(grad_unit, axis=-1, keepdims=True)
+    back = inverse * (centered - unit * jnp.mean(grad_unit * unit, axis=-1, keepdims=True))
+    total = add_ref[...].astype(jnp.float32) + back
+    out_ref[...] = total
+    for low_ref in rest[:-1]:
+        low_ref[...] = total.astype(jnp.bfloat16)
+
+
+def matmul_norm_back(name, grad, weight, value, add, gain, low):
+    rows, depth = grad.shape
+    width = weight.shape[0]
+    strip = lambda size: pl.BlockSpec((STRIP, size), lambda i: (i, 0))
+    whole = lambda *shape: pl.BlockSpec(shape, lambda i: (0, 0), pipeline_mode=pl.Buffered(1))
+    return pl.pallas_call(
+        norm_back_kernel,
+        name=name,
+        grid=(rows // STRIP,),
+        in_specs=[strip(depth), whole(width, depth), strip(width), strip(width), whole(1, width)],
+        out_specs=[strip(width)] * (1 + low) + [pl.BlockSpec((8, width), lambda i: (0, 0))],
+        out_shape=[jax.ShapeDtypeStruct((rows, width), jnp.float32)]
+        + [jax.ShapeDtypeStruct((rows, width), jnp.bfloat16)] * low
+        + [jax.ShapeDtypeStruct((8, width), jnp.float32)],
+        cost_estimate=pl.CostEstimate(
+            flops=2 * rows * width * (depth + 3072), transcendentals=rows, bytes_accessed=2 * rows * depth + 2 * width * depth + 14 * rows * width
+        ),
+    )(grad, weight, value, add, gain[None])
 
 
 BOTH = ("dp", "fsdp")
@@ -273,10 +311,13 @@
     return jnp.where(side_of(shape, at) == bit, jnp.expand_dims(mine, at), jnp.expand_dims(other, at))
 
 
-def gather_far(shard, sizes):
+def far_places(sizes):
+    return list(range(1, bit_count(sizes) - 2))
+
+
+def gather_far(value, sizes, places):
     bits = my_bits(sizes)
-    value = shard
-    for place in range(1, len(bits) - 2):
+    for place in places:
         value = join(value, exchange(value, sizes, (place, place)), place - 1, bits[place])
     return value
 
@@ -288,71 +329,96 @@
     return join(value, other, 0, jnp.where(bits[-1] == 0, bits[0], bits[near]))
 
 
-def gather_next(value, sizes):
+def gather_last(value, beside, other, sizes):
+    bits = my_bits(sizes)
+    last = len(bits) - 1
+    near = last - 1
+
+    def combine(held, received, even):
+        by_first = join(held, received, near, bits[near])
+        by_near = join(
+            jnp.moveaxis(held, 0, near - 1), jnp.moveaxis(received, 0, near - 1), 0, bits[0]
+        )
+        return jnp.where(even, by_first, by_near)
+
+    even = bits[last] == 0
+    other_beside = swap_core(other, sizes)
+    value = join(
+        combine(value, other, even), combine(beside, other_beside, jnp.logical_not(even)), last, bits[last]
+    )
+    return value.reshape((-1,) + value.shape[last + 2 :])
+
+
+def pick(value, at, bit):
+    return lax.dynamic_index_in_dim(value, bit, at, keepdims=False)
+
+
+def add(mine, other):
+    return mine.astype(jnp.float32) + other.astype(jnp.float32)
+
+
+def core_cut(partials, sizes, flip):
+    bits = my_bits(sizes)
+    last = len(bits) - 1
+    shape = (2,) * len(bits)
+    views = [part.reshape(shape + (part.shape[0] >> len(bits),) + part.shape[1:]) for part in partials]
+    return jnp.concatenate([pick(view, last, bits[last] ^ flip) for view in views], axis=-1)
+
+
+def near_cut(value, sizes, flip):
     bits = my_bits(sizes)
     near = len(bits) - 2
-    other = exchange(value, sizes, (near, 0))
-    by_first = join(value, other, near, bits[near])
-    by_near = join(jnp.moveaxis(value, 0, near - 1), jnp.moveaxis(other, 0, near - 1), 0, bits[0])
-    return jnp.where(bits[-1] == 0, by_first, by_near)
-
-
-def gather_core(value, sizes):
+    by_near = pick(value, near, bits[near] ^ flip)
+    by_first = jnp.moveaxis(pick(value, 0, bits[0] ^ flip), near - 1, 0)
+    return jnp.where(bits[-1] == 0, by_near, by_first)
+
+
+def next_cut(value, sizes, flip):
     bits = my_bits(sizes)
-    last = len(bits) - 1
-    value = join(value, exchange(value, sizes, (last, last)), last, bits[last])
-    return value.reshape((-1,) + value.shape[last + 2 :])
-
-
-def pick(value, at, bit):
-    return lax.dynamic_index_in_dim(value, bit, at, keepdims=False)
-
-
-def add_exchange(mine, sent, sizes, places, kind):
-    return mine.astype(jnp.float32) + exchange(sent.astype(kind), sizes, places).astype(jnp.float32)
-
-
-def scatter_core(partial, sizes, kind=jnp.bfloat16):
+    side = jnp.where(bits[-1] == 0, bits[0], bits[len(bits) - 2])
+    return pick(value, 0, side ^ flip)
+
+
+def swap_core(sent, sizes):
+    last = bit_count(sizes) - 1
+    return exchange(sent, sizes, (last, last))
+
+
+def swap_near(sent, sizes):
+    return exchange(sent, sizes, (bit_count(sizes) - 2, 0))
+
+
+def swap_next(sent, sizes):
+    return exchange(sent, sizes, (0, bit_count(sizes) - 2))
+
+
+def far_cut(value, sizes, places, flip):
+    place = places[-1]
+    return pick(value, place - 1, my_bits(sizes)[place] ^ flip)
+
+
+def swap_last(value, sizes):
+    return exchange(value, sizes, (bit_count(sizes) - 2, 0))
+
+
+def swap_far(sent, sizes, places):
+    return exchange(sent, sizes, (places[-1], places[-1]))
+
+
+def finish_far(value, other, sizes, places, kind=jnp.bfloat16):
+    return scatter_far(add(far_cut(value, sizes, places, 0), other), sizes, places[:-1], kind)
+
+
+def scatter_far(value, sizes, places, kind=jnp.bfloat16):
     bits = my_bits(sizes)
-    last = len(bits) - 1
-    shape = (2,) * len(bits) + (partial.shape[0] >> len(bits),) + partial.shape[1:]
-    view = partial.reshape(shape)
-    return add_exchange(
-        pick(view, last, bits[last]), pick(view, last, 1 - bits[last]), sizes, (last, last), kind
-    )
-
-
-def scatter_near(value, sizes, kind=jnp.bfloat16):
-    bits = my_bits(sizes)
-    near = len(bits) - 2
-    even = bits[-1] == 0
-
-    def cut(flip):
-        by_near = pick(value, near, bits[near] ^ flip)
-        by_first = jnp.moveaxis(pick(value, 0, bits[0] ^ flip), near - 1, 0)
-        return jnp.where(even, by_near, by_first)
-
-    return add_exchange(cut(0), cut(1), sizes, (near, 0), kind)
-
-
-def scatter_next(value, sizes, kind=jnp.bfloat16):
-    bits = my_bits(sizes)
-    near = len(bits) - 2
-    side = jnp.where(bits[-1] == 0, bits[0], bits[near])
-    return add_exchange(pick(value, 0, side), pick(value, 0, 1 - side), sizes, (0, near), kind)
-
-
-def scatter_far(value, sizes, kind=jnp.bfloat16):
-    bits = my_bits(sizes)
-    for place in reversed(range(1, len(bits) - 2)):
-        value = add_exchange(
-            pick(value, place - 1, bits[place]),
-            pick(value, place - 1, 1 - bits[place]),
-            sizes,
-            (place, place),
-            kind,
-        )
+    for place in reversed(places):
+        sent = pick(value, place - 1, 1 - bits[place]).astype(kind)
+        value = add(pick(value, place - 1, bits[place]), exchange(sent, sizes, (place, place)))
     return value
+
+
+def row_major(value):
+    return with_layout_constraint(value, Layout(major_to_minor=(0, 1)))
 
 
 def tie(*values):
@@ -380,69 +446,91 @@
     small = jnp.stack([attn_gain, attn_shift, mlp_gain, mlp_shift], axis=1)
     small = jnp.pad(small, ((0, 0), (0, 128 - 4)))
     wide = up_weight.shape[1]
-    second = lax.all_gather(
-        jnp.concatenate([up_weight, out_weight], axis=1), BOTH, axis=0, tiled=True
-    )
-    up_full, out_full = (second[:, :wide], second[:, wide:])
-    first = gather_far(jnp.concatenate([qkv_weight, small], axis=1), sizes)
-    first, down_weight = tie(first, down_weight)
-    down_full = gather_far(down_weight, sizes)
-    first = gather_next(gather_near(first, sizes), sizes)
-    first, down_full = tie(first, down_full)
-    first = gather_core(first, sizes)
-    down_full = gather_near(down_full, sizes)
+    far = far_places(sizes)
+    low = jnp.bfloat16
+    first = gather_far(jnp.concatenate([qkv_weight, small], axis=1), sizes, far)
+    first, up_weight, out_weight = tie(first, up_weight, out_weight)
+    first = gather_near(first, sizes)
+    second = gather_far(jnp.concatenate([up_weight, out_weight], axis=1), sizes, far[:1])
+    first, second = tie(first, second)
+    other = swap_last(first, sizes)
+    beside = swap_core(first, sizes)
+    second = gather_far(second, sizes, far[1:])
+    first = row_major(gather_last(first, beside, other, sizes))
+    first, second, down_weight = tie(first, second, down_weight)
+    second = gather_near(second, sizes)
+    down_full = gather_far(down_weight, sizes, far[:1])
     qkv_full = first[:, : 3 * width]
-    small = first[:, 3 * width : 3 * width + 4].astype(jnp.float32).T
+    small = row_major(first[:, 3 * width :])
+    small = small[:, :4].astype(jnp.float32).T
     gain_one, shift_one, gain_two, shift_two = (small[0], small[1], small[2], small[3])
     flat = tokens.astype(jnp.float32).reshape(rows_here * length, width)
     normed_float, unit_one, inverse_one = norm_forward(flat, gain_one, shift_one)
     normed = normed_float.astype(jnp.bfloat16)
     project = jnp.dot(normed, qkv_full, preferred_element_type=jnp.float32).astype(jnp.bfloat16)
-    project, down_full = tie(project, down_full)
-    down_full = gather_next(down_full, sizes)
+    project, second, down_full = tie(project, second, down_full)
+    other = swap_last(second, sizes)
+    beside = swap_core(second, sizes)
+    down_full = gather_far(down_full, sizes, far[1:])
     project_rows = project.reshape(rows_here, length, 3 * width)
     forward = [
         attend_row(project_rows[row], segments[row], thresholds[row : row + 1])
         for row in range(rows_here)
     ]
     mixed_flat = jnp.concatenate([item[0] for item in forward], axis=0)
+    mixed_flat, other, beside, down_full = tie(mixed_flat, other, beside, down_full)
+    second = row_major(gather_last(second, beside, other, sizes))
+    up_full, out_full = (second[:, :wide], second[:, wide:])
+    down_full = gather_near(down_full, sizes)
     soft = sum(jnp.sum(item[3][0]) for item in forward)
     pairs = sum(jnp.sum(item[3][1]) for item in forward)
     middle = flat + jnp.dot(mixed_flat, out_full, preferred_element_type=jnp.float32)
     normed_two_float, unit_two, inverse_two = norm_forward(middle, gain_two, shift_two)
-    normed_two, down_full = tie(normed_two_float.astype(jnp.bfloat16), down_full)
-    down_full = gather_core(down_full, sizes)
+    normed_two, down_full = tie(normed_two_float.astype(low), down_full)
+    other = swap_last(down_full, sizes)
+    beside = swap_core(down_full, sizes)
     hidden = jnp.dot(normed_two, up_full, preferred_element_type=jnp.float32)
-    active = jax.nn.gelu(hidden, approximate=True).astype(jnp.bfloat16)
+    squared = hidden * hidden
+    curve = jnp.tanh(0.7978845608 * hidden * (1.0 + 0.044715 * squared))
+    active = (0.5 * hidden * (1.0 + curve)).astype(low)
+    slope = 0.5 * (1.0 + curve) + hidden * (1.0 - curve * curve) * (
+        0.3989422804 + 0.0535161226 * squared
+    )
+    slope = slope.astype(low)
+    active, slope, other, beside = tie(active, slope, other, beside)
+    down_full = gather_last(down_full, beside, other, sizes)
     grad_seed = jnp.where(
         (segments >= 0)[:, :, None], cotangent, jnp.zeros_like(cotangent)
     ).reshape(rows_here * length, width)
     grad_down = jnp.dot(active.T, grad_seed, preferred_element_type=jnp.float32)
-    down_full, grad_down = tie(down_full, grad_down)
-    grad_down = lax.psum_scatter(
-        grad_down.astype(jnp.bfloat16), BOTH, scatter_dimension=0, tiled=True
-    ).astype(jnp.float32)
+    grad_down = grad_down.astype(low)
+    sent, grad_seed = tie(core_cut((grad_down,), sizes, 1), grad_seed)
+    other_down = swap_core(sent, sizes)
     grad_active = jnp.dot(grad_seed, down_full.T, preferred_element_type=jnp.float32)
-    unused_value, gelu_pull = jax.vjp(lambda values: jax.nn.gelu(values, approximate=True), hidden)
-    grad_hidden = gelu_pull(grad_active)[0].astype(jnp.bfloat16)
+    grad_hidden = (grad_active * slope.astype(jnp.float32)).astype(low)
+    grad_down, grad_hidden = tie(grad_down, grad_hidden)
+    grad_down = add(core_cut((grad_down,), sizes, 0), other_down)
+    sent, grad_hidden = tie(near_cut(grad_down, sizes, 1).astype(low), grad_hidden)
+    other_down = swap_near(sent, sizes)
     grad_up = jnp.dot(normed_two.T, grad_hidden, preferred_element_type=jnp.float32)
-    grad_hidden, grad_up = tie(grad_hidden, grad_up.astype(jnp.bfloat16))
-    grad_up = scatter_core(grad_up, sizes)
-    grad_normed_two = jnp.dot(grad_hidden, up_full.T, preferred_element_type=jnp.float32)
-    grad_middle_part, grad_gain_two, grad_shift_two = norm_backward(
-        grad_normed_two, unit_two, inverse_two, gain_two
-    )
-    grad_middle = grad_seed.astype(jnp.float32) + grad_middle_part
-    grad_branch = grad_middle.astype(jnp.bfloat16)
-    grad_out = jnp.dot(mixed_flat.T, grad_branch, preferred_element_type=jnp.float32)
-    grad_branch, grad_out, grad_up = tie(grad_branch, grad_out.astype(jnp.bfloat16), grad_up)
-    grad_up = scatter_near(grad_up, sizes)
-    grad_out = scatter_core(grad_out, sizes)
-    grad_mixed = jnp.dot(grad_branch, out_full.T, preferred_element_type=jnp.float32).astype(
-        jnp.bfloat16
-    )
-    grad_mixed, grad_out = tie(grad_mixed.reshape(rows_here, length, width), grad_out)
-    grad_out = scatter_near(grad_out, sizes)
+    grad_hidden, grad_up = tie(grad_hidden, grad_up.astype(low))
+    grad_middle, grad_branch, sums_two = matmul_norm_back(
+        "mlp_norm_backward", grad_hidden, second, middle, grad_seed, gain_two, 1
+    )
+    grad_out = jnp.dot(mixed_flat.T, grad_branch, preferred_element_type=jnp.float32).astype(low)
+    grad_down, grad_out, other_down = tie(grad_down, grad_out, other_down)
+    grad_down = add(near_cut(grad_down, sizes, 0), other_down)
+    sent, sent_down, grad_branch = tie(
+        core_cut((grad_up, grad_out), sizes, 1), next_cut(grad_down, sizes, 1).astype(low), grad_branch
+    )
+    other = swap_core(sent, sizes)
+    other_down = swap_next(sent_down, sizes)
+    grad_mixed = jnp.dot(grad_branch, out_full.T, preferred_element_type=jnp.float32).astype(low)
+    grad_up, grad_out, grad_mixed = tie(grad_up, grad_out, grad_mixed)
+    upper = add(core_cut((grad_up, grad_out), sizes, 0), other)
+    grad_mixed = grad_mixed.reshape(rows_here, length, width)
+    sent, grad_mixed = tie(near_cut(upper, sizes, 1).astype(low), grad_mixed)
+    other = swap_near(sent, sizes)
     grad_project = jnp.concatenate(
         [
             row_back(project_rows[row], grad_mixed[row], forward[row][1], forward[row][2])
@@ -450,29 +538,88 @@
         ],
         axis=0,
     )
-    grad_project, grad_up, grad_out = tie(grad_project, grad_up, grad_out)
-    upper = scatter_next(jnp.concatenate([grad_up, grad_out], axis=-1), sizes)
-    grad_qkv = jnp.dot(normed.T, grad_project, preferred_element_type=jnp.float32)
-    grad_qkv, active = tie(grad_qkv.astype(jnp.bfloat16), active)
-    grad_qkv = scatter_core(grad_qkv, sizes)
-    result = middle + jnp.dot(active, down_full, preferred_element_type=jnp.float32)
-    output = result.astype(jnp.bfloat16).reshape(rows_here, length, width)
-    grad_project, grad_qkv, output = tie(grad_project, grad_qkv, output)
-    upper = scatter_far(upper, sizes)
-    grad_up, grad_out = (upper[:, :wide], upper[:, wide:])
-    grad_qkv = scatter_far(scatter_next(scatter_near(grad_qkv, sizes), sizes), sizes)
-    grad_normed = jnp.dot(grad_project, qkv_full.T, preferred_element_type=jnp.float32)
-    grad_input_part, grad_gain_one, grad_shift_one = norm_backward(
-        grad_normed, unit_one, inverse_one, gain_one
-    )
-    grad_tokens = (grad_middle + grad_input_part).reshape(rows_here, length, width)
+    near_far, far_far = (far[1:], far[:1])
+    upper, grad_down, grad_project, other, other_down = tie(
+        upper, grad_down, grad_project, other, other_down
+    )
+    grad_qkv = jnp.dot(normed.T, grad_project, preferred_element_type=jnp.float32).astype(low)
+    sent, upper, grad_down, grad_project = tie(
+        core_cut((grad_qkv,), sizes, 1), upper, grad_down, grad_project
+    )
+    other_qkv = swap_core(sent, sizes)
+    upper = add(near_cut(upper, sizes, 0), other)
+    grad_down = add(next_cut(grad_down, sizes, 0), other_down)
+    grad_qkv, sent, sent_down = tie(
+        grad_qkv,
+        next_cut(upper, sizes, 1).astype(low),
+        far_cut(grad_down, sizes, near_far, 1).astype(low),
+    )
+    other = swap_next(sent, sizes)
+    other_down = swap_far(sent_down, sizes, near_far)
+    grad_qkv = add(core_cut((grad_qkv,), sizes, 0), other_qkv)
+    sent, grad_project = tie(near_cut(grad_qkv, sizes, 1).astype(low), grad_project)
+    other_qkv = swap_near(sent, sizes)
+    grad_tokens, sums_one = matmul_norm_back(
+        "attention_norm_backward",
+        grad_project,
+        first,
+        tokens.reshape(rows_here * length, width),
+        grad_middle,
+        gain_one,
+        0,
+    )
+    grad_tokens = grad_tokens.reshape(rows_here, length, width)
+    grad_qkv, sums_one, other_qkv, other, other_down = tie(
+        grad_qkv, sums_one, other_qkv, other, other_down
+    )
+    grad_qkv = add(near_cut(grad_qkv, sizes, 0), other_qkv)
+    sent, sums_one, upper, grad_down = tie(
+        next_cut(grad_qkv, sizes, 1).astype(low), sums_one, upper, grad_down
+    )
+    other_qkv = swap_next(sent, sizes)
+    upper = add(next_cut(upper, sizes, 0), other)
+    grad_down = finish_far(grad_down, other_down, sizes, near_far)
+    grad_gain_one, grad_shift_one, grad_gain_two, grad_shift_two = (
+        sums_one[0],
+        sums_one[1],
+        sums_two[0],
+        sums_two[1],
+    )
     small = jnp.stack([grad_gain_one, grad_shift_one, grad_gain_two, grad_shift_two])
     small = small.reshape(4, shards, piece).transpose(1, 0, 2).reshape(shards, 4 * piece)
     totals = jnp.broadcast_to(jnp.stack([soft, pairs]), (shards, 2))
     small = jnp.concatenate([small, totals], axis=1)
     small = jnp.pad(small, ((0, 0), (0, 128 - small.shape[1])))
-    small = scatter_near(scatter_core(small, sizes, jnp.float32), sizes, jnp.float32)
-    small = scatter_far(scatter_next(small, sizes, jnp.float32), sizes, jnp.float32)[0]
+    sent_small, sent, sent_down, active = tie(
+        core_cut((small,), sizes, 1),
+        far_cut(upper, sizes, near_far, 1).astype(low),
+        far_cut(grad_down, sizes, far_far, 1).astype(low),
+        active,
+    )
+    other_small = swap_core(sent_small, sizes)
+    other = swap_far(sent, sizes, near_far)
+    other_down = swap_far(sent_down, sizes, far_far)
+    result = middle + jnp.dot(active, down_full, preferred_element_type=jnp.float32)
+    output = result.astype(low).reshape(rows_here, length, width)
+    grad_qkv, output, other_qkv, other, other_down, other_small = tie(
+        grad_qkv, output, other_qkv, other, other_down, other_small
+    )
+    grad_qkv = add(next_cut(grad_qkv, sizes, 0), other_qkv)
+    sent, upper, grad_down, small = tie(
+        far_cut(grad_qkv, sizes, near_far, 1).astype(low), upper, grad_down, small
+    )
+    other_qkv = swap_far(sent, sizes, near_far)
+    small = add(core_cut((small,), sizes, 0), other_small)
+    other_small = swap_near(near_cut(small, sizes, 1), sizes)
+    upper = finish_far(upper, other, sizes, near_far)
+    grad_down = finish_far(grad_down, other_down, sizes, far_far)
+    upper = scatter_far(upper, sizes, far_far)
+    grad_up, grad_out = (upper[:, :wide], upper[:, wide:])
+    grad_qkv = finish_far(grad_qkv, other_qkv, sizes, near_far)
+    small = add(near_cut(small, sizes, 0), other_small)
+    grad_qkv = scatter_far(grad_qkv, sizes, far_far)
+    small = add(next_cut(small, sizes, 0), swap_next(next_cut(small, sizes, 1), sizes))
+    small = scatter_far(scatter_far(small, sizes, near_far, jnp.float32), sizes, far_far, jnp.float32)[0]
     fraction = small[4 * piece] / small[4 * piece + 1]
     return (
         output,

time: 352 us -> 327 us (0.929)
  Pallas kernels: 46.1 us -> 67.7 us
  between operations: 18.1 us -> 4.84 us
  local copies, waits for them, and re-layouts: 35.7 us -> 23.4 us
  matrix products: 85 us -> 73.6 us
  waiting for transfers between devices: 73.5 us -> 64.4 us
    pallas_call x0 -> x2, Pallas kernels: none -> 21.9 us  [matmul_norm_back(): pl.pallas_call(norm_back_kernel, name=name, grid=(rows // STRIP,), in_spe...]
    dot_general x2 -> x0, matrix products: 12.2 us -> none  [the longest x1 6.73 us: body(): jnp.dot(grad_hidden, up_full.T, preferred_element_type=jnp.float32)]
    ppermute x27 -> x38, waiting for transfers between devices: 73.4 us -> 64.4 us  [exchange(): lax.ppermute(value, BOTH, [(i, i ^ masks[i & 1]) for i in range(2 ** coun...]
    unnamed x78 -> x79, local copies, waits for them, and re-layouts: 20.6 us -> 11.6 us
    dot_general x1, matrix products: 18.3 us -> 9.39 us  [body(): jnp.dot(grad_seed, down_full.T, preferred_element_type=jnp.float32)]
    dot_general x2 -> x0, local copies, waits for them, and re-layouts: 7.21 us -> none  [the longest x1 3.68 us: body(): jnp.dot(grad_project, qkv_full.T, preferred_element_type=jnp.float32)]
    reduce_sum x2 -> x0, other arithmetic: 6.69 us -> none  [norm_backward(): grad_gain = jnp.sum(grad_normed * unit, axis=0)]
    select_n x3 -> x4, other arithmetic: 5.04 us -> 11 us  [the longest x3 11 us: combine(): return jnp.where(even, by_first, by_near)]
  transfers between devices with their start and end apart: 29 -> 38, of which waited for: 12 -> 16; matrix products, arithmetic and copies ran while one was open for 36% -> 31% of each run, Pallas kernels for 13% -> 21%
where the time goes in v2:
time: 327 us; the launch traced here: 323 us
  matrix products  73.6 us (23%)
  Pallas kernels  67.7 us (21%)
  waiting for transfers between devices  64.4 us (20%)
  other arithmetic  54 us (17%)
  starting transfers between devices  35.5 us (11%)
  local copies, waits for them, and re-layouts  23.4 us (7%)
  between operations  4.84 us (1%)
    ppermute x38, waiting for transfers between devices, exchange(): lax.ppermute(value, BOTH, [(i, i ^ masks[i & 1]) for i in range(2 ** coun...  64.4 us
    ppermute x38, starting transfers between devices, exchange(): lax.ppermute(value, BOTH, [(i, i ^ masks[i & 1]) for i in range(2 ** coun...  35.5 us
    pallas_call x1, Pallas kernels, row_back(): pl.pallas_call(attend_back_kernel, name='attend_backward', grid=(blocks,)...  27 us
    pallas_call x2, Pallas kernels, matmul_norm_back(): pl.pallas_call(norm_back_kernel, name=name, grid=(rows // STRIP,), in_spe...  21.9 us
    pallas_call x1, Pallas kernels, attend_row(): pl.pallas_call(attend_kernel, name='attend_forward', grid=(blocks,), in_s...  18.9 us
    add x20, other arithmetic, add(): return mine.astype(jnp.float32) + other.astype(jnp.float32)  16.2 us
    dot_general x1, matrix products, body(): hidden = jnp.dot(normed_two, up_full, preferred_element_type=jnp.float32)  12.9 us
    select_n x12, other arithmetic, join(): jnp.where(side_of(shape, at) == bit, jnp.expand_dims(mine, at), jnp.expan...  12.6 us
  transfers between devices with their start and end apart: 38, of which 16 were waited for; matrix products, arithmetic and copies ran while one was open for 31% of the time, Pallas kernels for 21%

profile of v2, /device:TPU:0, one launch (start us, length us, event | category | flops | bytes accessed | tf_op | source)
XLA Modules:
  0.0 323.5 jit_solution(12284361930242078859)
XLA Ops:
  2.5 4.1 %collective-permute-start = (bf16[24,2432]{1,0:T(8,128)(2,1)S(1)}, bf16[24,2432]{1,0:T(8,128)(2,1)S(1)}, u32[]{:S(2)}, u32[]{:S(2)}) collective-permute-start(bf16[24,2432]{1,0:T(8,128)(2,1)S(1)} %fusion.30), channel_id=1, source_target_pairs={{0,8},{1,9},{2,10},{3,11},{4,12},{5,13},{6,14},{7,15},{8,0},{9,1},... | collective-permute-start | bytes 350216 | tf_op jit(solution)/shard_map/ppermute | solution.py:302
  6.6 5.7 %collective-permute-done = bf16[24,2432]{1,0:T(8,128)(2,1)S(1)} collective-permute-done((bf16[24,2432]{1,0:T(8,128)(2,1)S(1)}, bf16[24,2432]{1,0:T(8,128)(2,1)S(1)}, u32[]{:S(2)}, u32[]{:S(2)}) %collective-permute-start) | collective-permute-done | bytes 116768 | tf_op jit(solution)/shard_map/ppermute | solution.py:302
  13.3 6.1 %collective-permute-done.1 = bf16[2,24,2432]{2,1,0:T(8,128)(2,1)S(1)} collective-permute-done((bf16[2,24,2432]{2,1,0:T(8,128)(2,1)S(1)}, bf16[2,24,2432]{2,1,0:T(8,128)(2,1)S(1)}, u32[]{:S(2)}, u32[]{:S(2)}) %collective-permute-start.1) | collective-permute-done | bytes 233504 | tf_op jit(solution)/shard_map/ppermute | solution.py:302
  21.3 3.1 collective-permute-start.3
  24.4 1.5 collective-permute-start.2
  25.9 6.7 %collective-permute-done.3 = bf16[24,3840]{1,0:T(8,128)(2,1)S(1)} collective-permute-done((bf16[24,3840]{1,0:T(8,128)(2,1)S(1)}, bf16[24,3840]{1,0:T(8,128)(2,1)S(1)}, u32[]{:S(2)}, u32[]{:S(2)}) %collective-permute-start.3) | collective-permute-done | bytes 184352 | tf_op jit(solution)/shard_map/ppermute | solution.py:302
  33.8 1.6 collective-permute-start.4
  36.3 1.3 collective-permute-start.7
  38.6 8.8 %collective-permute-done.4 = bf16[2,2,2,24,2432]{4,3,0,2,1:T(8,128)(2,1)S(1)} collective-permute-done((bf16[2,2,2,24,2432]{4,3,0,2,1:T(8,128)(2,1)S(1)}, bf16[2,2,2,24,2432]{4,3,0,2,1:T(8,128)(2,1)S(1)}, u32[]{:S(2)}, u32[]{:S(2)}) %collective-permute-start.4) | collective-permute-done | bytes 933920 | tf_op jit(solution)/shard_map/ppermute | solution.py:302
  47.4 2.1 broadcast_select_fusion.3
  49.9 2.0 select_select_fusion.5
  52.8 1.5 collective-permute-start.9
  55.4 1.6 collective-permute-start.8
  57.0 7.9 %convolution_convert_fusion.project_ref = bf16[1024,2304]{1,0:T(8,128)(2,1)} fusion(bf16[768,2432]{1,0:T(8,128)(2,1)} %copy-done.12, bf16[1,1024,768]{2,1,0:T(8,128)(2,1)S(1)} %copy-done.7, f32[768]{0:T(1024)S(1)} %get-tuple-element.193, f32[768]{0:T(1024)S(1)} %get-tuple-element.195, f32[1024]{0:T(1024)S(1)} %add_rsqrt_fusion.1, ...), kind=kOutput, calls=%fused_computation.7 | convolution fusion | flops 3630956544 | bytes 9844736 | tf_op jit(solution)/shard_map/dot_general | solution.py:470
  65.0 1.9 collective-permute-done.8
  67.2 1.6 collective-permute-start.10
  68.8 2.4 collective-permute-start.12
  71.2 18.9 %attend_forward.1 = (bf16[1024,768]{1,0:T(8,128)(2,1)}, f32[16,1024]{1,0:T(8,128)}, f32[8,384,128]{2,1,0:T(8,128)}, f32[8,128]{1,0:T(8,128)}) custom-call(f32[1]{0:T(128)S(6)} %copy.153.limit_ref, s32[1,1024]{1,0:T(1,128)} %seg_ref.1, bf16[1024,2304]{1,0:T(8,128)(2,1)} %convolution_convert_fusion.project_ref), custom_call_target="tpu_custom_call" | custom-call | flops 22649241600 | bytes 7864320 | tf_op jit(solution)/shard_map/attend_forward/pallas_call | solution.py:112
  90.1 1.9 broadcast_select_fusion.4
  92.0 1.6 collective-permute-start.14
  93.7 2.8 select_bitcast_fusion.add_ref
  96.5 5.8 %collective-permute-done.14 = bf16[2,2,96,768]{3,2,1,0:T(8,128)(2,1)} collective-permute-done((bf16[2,2,96,768]{3,2,1,0:T(8,128)(2,1)}, bf16[2,2,96,768]{3,2,1,0:T(8,128)(2,1)}, u32[]{:S(2)}, u32[]{:S(2)}) %collective-permute-start.14) | collective-permute-done | bytes 589856 | tf_op jit(solution)/shard_map/ppermute | solution.py:302
  102.3 2.5 broadcast_select_fusion.1
  104.7 6.2 %select_select_fusion.1 = (bf16[2,2,2,2,24,3840]{5,4,3,2,1,0:T(8,128)(2,1)S(1)}, bf16[2,2,2,2,24,3840]{5,4,3,2,1,0:T(8,128)(2,1)S(1)}) fusion(pred[2]{0:T(512)(128)(4,1)S(1)} %get-tuple-element.215, pred[2]{0:T(512)(128)(4,1)S(1)} %get-tuple-element.216, pred[]{:T(512)S(6)} %eq.44, bf16[2,2,2,24,3840]{4,3,2,1,0:T(8,128)(2,1)} %bitcast.13, ...), kind=kLoop, calls=%fused_computation.39 | loop fusion | flops 8847360 | bytes 17694726 | tf_op jit(solution)/shard_map/jit(_where)/select_n | solution.py:342
  110.9 3.0 bitcast_select_fusion.weight_ref
  113.8 3.3 %fusion.47 = (f32[1024]{0:T(1024)S(1)}, f32[1024,768]{1,0:T(8,128)S(1)}) fusion(bf16[1024,768]{1,0:T(8,128)(2,1)} %get-tuple-element.109, bf16[768,3840]{1,0:T(8,128)(2,1)} %bitcast_select_fusion.weight_ref, bf16[1,1024,768]{2,1,0:T(8,128)(2,1)S(1)} %copy-done.7), kind=kOutput, calls=%fused_computation.166 | convolution fusion | flops 1210317824 | bytes 7475200 | tf_op jit(solution)/shard_map/dot_general | solution.py:487
  118.8 1.6 copy-done.5
  120.4 1.3 collective-permute-start.15
  121.6 12.9 %add_convert_fusion = (bf16[1024,3072]{1,0:T(8,128)(2,1)}, bf16[1024,3072]{1,0:T(8,128)(2,1)}) fusion(bf16[1024,768]{1,0:T(8,128)(2,1)S(1)} %add_convert_fusion.2, bf16[768,3840]{1,0:T(8,128)(2,1)S(1)} %copy-done.8), kind=kOutput, calls=%fused_computation.1 | convolution fusion | flops 4888461312 | bytes 18874368 | tf_op jit(solution)/shard_map/dot_general | solution.py:492
  134.6 2.0 collective-permute-done.15
  136.6 8.5 %convolution_convert_fusion.2 = bf16[3072,768]{1,0:T(8,128)(2,1)S(1)} fusion(bf16[1024,3072]{1,0:T(8,128)(2,1)} %get-tuple-element.167, bf16[1024,768]{1,0:T(8,128)(2,1)S(1)} %copy-done.17), kind=kOutput, calls=%fused_computation.9 | convolution fusion | flops 4834197504 | bytes 12582912 | tf_op jit(solution)/shard_map/dot_general | solution.py:505
  145.9 2.9 select_select_fusion.3
  149.4 9.4 %multiply_convert_fusion.grad_ref = bf16[1024,3072]{1,0:T(8,128)(2,1)S(1)} fusion(bf16[1024,3072]{1,0:T(8,128)(2,1)} %get-tuple-element.119, bf16[1024,768]{1,0:T(8,128)(2,1)} %select_bitcast_fusion.add_ref, bf16[3072,768]{1,0:T(8,128)(2,1)S(1)} %bitcast_select_fusion.1), kind=kOutput, calls=%fused_computation | convolution fusion | flops 4841275392 | bytes 18874368 | tf_op jit(solution)/shard_map/dot_general | solution.py:509
  158.8 4.0 %convert_add_fusion.1 = f32[2,2,2,2,96,768]{5,4,3,2,1,0:T(8,128)S(1)} fusion(bf16[2,2,2,2,96,768]{5,4,3,2,1,0:T(8,128)(2,1)} %collective-permute-done.18, bf16[2,2,2,2,2,96,768]{6,5,4,3,2,1,0:T(8,128)(2,1)S(1)} %bitcast.259, s32[]{:T(128)S(6)} %select_n.421), kind=kLoop, calls=%fused_computation.13 | loop fusion | flops 3538944 | bytes 9437188 | tf_op jit(solution)/shard_map/add | solution.py:357
  163.1 1.4 collective-permute-start.19
  165.4 7.2 %convolution_convert_fusion.1 = bf16[768,3072]{1,0:T(8,128)(2,1)} fusion(bf16[1024,768]{1,0:T(8,128)(2,1)S(1)} %copy-done.19, bf16[1024,3072]{1,0:T(8,128)(2,1)S(1)} %multiply_convert_fusion.grad_ref), kind=kOutput, calls=%fused_computation.8 | convolution fusion | flops 4834197504 | bytes 12582912 | tf_op jit(solution)/shard_map/dot_general | solution.py:515
  172.6 12.0 %mlp_norm_backward.1 = (f32[1024,768]{1,0:T(8,128)}, bf16[1024,768]{1,0:T(8,128)(2,1)}, f32[8,768]{1,0:T(8,128)}) custom-call(bf16[1024,3072]{1,0:T(8,128)(2,1)} %copy-done.33, bf16[768,3840]{1,0:T(8,128)(2,1)} %bitcast_select_fusion.weight_ref, f32[1024,768]{1,0:T(8,128)} %copy-done.3, bf16[1024,768]{1,0:T(8,128)(2,1)} %select_bitcast_fusion.add_ref, ...), custom_call_target="tpu_custom_call" | custom-call | flops 9663676416 | bytes 22020096 | tf_op jit(solution)/shard_map/mlp_norm_backward/pallas_call | solution.py:271
  184.6 3.5 %convolution_convert_fusion.5 = bf16[768,768]{1,0:T(8,128)(2,1)S(1)} fusion(bf16[1024,768]{1,0:T(8,128)(2,1)} %get-tuple-element.109, bf16[1024,768]{1,0:T(8,128)(2,1)} %get-tuple-element.131), kind=kOutput, calls=%fused_computation.58 | convolution fusion | flops 1208549376 | bytes 4325376 | tf_op jit(solution)/shard_map/dot_general | solution.py:520
  188.1 2.3 dynamic-slice_bitcast_fusion.3
  190.9 1.8 pad_maximum_fusion
  192.8 1.5 slice_reduce_fusion.3
  194.3 4.4 %convolution_convert_fusion.4 = bf16[1024,768]{1,0:T(8,128)(2,1)} fusion(bf16[1024,768]{1,0:T(8,128)(2,1)} %get-tuple-element.131, bf16[768,3840]{1,0:T(8,128)(2,1)} %bitcast_select_fusion.weight_ref), kind=kOutput, calls=%fused_computation.56 | convolution fusion | flops 1208745984 | bytes 4325376 | tf_op jit(solution)/shard_map/dot_general | solution.py:528
  198.7 1.5 collective-permute-start.22
  200.5 2.6 convert_add_fusion
  203.2 2.5 copy-done
  205.7 1.5 fusion.13
  207.6 27.0 %attend_backward.1.grad_ref = bf16[1024,2304]{1,0:T(8,128)(2,1)} custom-call(bf16[1024,2304]{1,0:T(8,128)(2,1)} %convolution_convert_fusion.project_ref, bf16[1024,768]{1,0:T(8,128)(2,1)} %convolution_convert_fusion.4, f32[16,1024]{1,0:T(8,128)} %get-tuple-element.137.lse_ref, f32[8,384,128]{2,1,0:T(8,128)} %get-tuple-element.138.bias_ref), custom_call_target="tpu_custom_call" | custom-call | flops 31708938240 | bytes 11010048 | tf_op jit(solution)/shard_map/attend_backward/pallas_call | solution.py:216
  234.6 7.0 %convolution_convert_fusion.3 = bf16[768,2304]{1,0:T(8,128)(2,1)S(1)} fusion(bf16[1024,2304]{1,0:T(8,128)(2,1)} %attend_backward.1.grad_ref, bf16[1,1024,768]{2,1,0:T(8,128)(2,1)} %param.12, f32[768]{0:T(1024)S(1)} %copy-done.27, f32[768]{0:T(1024)S(1)} %copy-done.29, f32[1024]{0:T(1024)S(1)} %copy-done.32, f32[1024]{0:T(1024)S(1)} %copy-done.25), kind=kOutput, calls=%fused_computation.10 | convolution fusion | flops 3630366720 | bytes 9844736 | tf_op jit(solution)/shard_map/dot_general | solution.py:545
  244.8 1.8 fusion.12
  249.7 1.7 collective-permute-start.24
  251.4 1.4 pad_maximum_fusion.4
  254.1 9.9 %attention_norm_backward.1 = (f32[1024,768]{1,0:T(8,128)}, f32[8,768]{1,0:T(8,128)}) custom-call(bf16[1024,2304]{1,0:T(8,128)(2,1)} %attend_backward.1.grad_ref, bf16[768,2432]{1,0:T(8,128)(2,1)} %copy-done.12, bf16[1024,768]{1,0:T(8,128)(2,1)} %bitcast.253, f32[1024,768]{1,0:T(8,128)} %get-tuple-element.152.add_ref, f32[1,768]{1,0:T(1,128)} %get-tuple-element.191.gain_ref), custom_call_target="tpu_custom_call" | custom-call | flops 8455716864 | bytes 19267584 | tf_op jit(solution)/shard_map/attention_norm_backward/pallas_call | solution.py:271
  264.0 5.9 %collective-permute-done.25 = bf16[2,2,24,3840]{3,2,1,0:T(8,128)(2,1)} collective-permute-done((bf16[2,2,24,3840]{3,2,1,0:T(8,128)(2,1)}, bf16[2,2,24,3840]{3,2,1,0:T(8,128)(2,1)}, u32[]{:S(2)}, u32[]{:S(2)}) %collective-permute-start.25) | collective-permute-done | bytes 737312 | tf_op jit(solution)/shard_map/ppermute | solution.py:302
  270.5 1.4 fusion.16
  275.0 1.9 collective-permute-start.27
  276.9 1.7 bitcast_add_fusion
  279.8 1.8 collective-permute-start.29
  281.6 9.4 %fusion.18 = bf16[1,1024,768]{2,1,0:T(8,128)(2,1)} fusion(f32[1024,768]{1,0:T(8,128)S(1)} %copy-done.4, bf16[1024,3072]{1,0:T(8,128)(2,1)} %get-tuple-element.167, bf16[3072,768]{1,0:T(8,128)(2,1)} %copy-done.11), kind=kOutput, calls=%fused_computation.59 | convolution fusion | flops 4833411072 | bytes 15728640 | tf_op jit(solution)/shard_map/dot_general | solution.py:602
  291.1 4.3 %collective-permute-done.28 = bf16[2,24,3840]{2,1,0:T(8,128)(2,1)S(1)} collective-permute-done((bf16[2,24,3840]{2,1,0:T(8,128)(2,1)S(1)}, bf16[2,24,3840]{2,1,0:T(8,128)(2,1)S(1)}, u32[]{:S(2)}, u32[]{:S(2)}) %collective-permute-start.28) | collective-permute-done | bytes 368672 | tf_op jit(solution)/shard_map/ppermute | solution.py:302
  297.7 2.3 collective-permute-done.34
  301.7 2.0 collective-permute-done.35
  304.7 2.7 collective-permute-done.36
  308.2 4.8 %collective-permute-done.37 = f32[1,128]{1,0:T(1,128)S(1)} collective-permute-done((f32[1,128]{1,0:T(1,128)S(1)}, f32[1,128]{1,0:T(1,128)S(1)}, u32[]{:S(2)}, u32[]{:S(2)}) %collective-permute-start.37) | collective-permute-done | bytes 544 | tf_op jit(solution)/shard_map/ppermute | solution.py:302
  317.1 4.3 %collective-permute-done.32 = bf16[24,2304]{1,0:T(8,128)(2,1)S(1)} collective-permute-done((bf16[24,2304]{1,0:T(8,128)(2,1)S(1)}, bf16[24,2304]{1,0:T(8,128)(2,1)S(1)}, u32[]{:S(2)}, u32[]{:S(2)}) %collective-permute-start.32) | collective-permute-done | bytes 110624 | tf_op jit(solution)/shard_map/ppermute | solution.py:302
  (207 shorter events, 36.9 us)
Async XLA Ops:
  0.6 34.7 %copy-start.7 = (bf16[1,1024,768]{2,1,0:T(8,128)(2,1)S(1)}, bf16[1,1024,768]{2,1,0:T(8,128)(2,1)}, u32[]{:S(2)}) copy-start(bf16[1,1024,768]{2,1,0:T(8,128)(2,1)} %param.12) | copy-start | bytes 4718596
  2.5 9.8 %collective-permute-start = (bf16[24,2432]{1,0:T(8,128)(2,1)S(1)}, bf16[24,2432]{1,0:T(8,128)(2,1)S(1)}, u32[]{:S(2)}, u32[]{:S(2)}) collective-permute-start(bf16[24,2432]{1,0:T(8,128)(2,1)S(1)} %fusion.30), channel_id=1, source_target_pairs={{0,8},{1,9},{2,10},{3,11},{4,12},{5,13},{6,14},{7,15},{8,0},{9,1},... | collective-permute-start | bytes 350216 | tf_op jit(solution)/shard_map/ppermute | solution.py:302
  12.5 6.9 %collective-permute-start.1 = (bf16[2,24,2432]{2,1,0:T(8,128)(2,1)S(1)}, bf16[2,24,2432]{2,1,0:T(8,128)(2,1)S(1)}, u32[]{:S(2)}, u32[]{:S(2)}) collective-permute-start(bf16[2,24,2432]{2,1,0:T(8,128)(2,1)S(1)} %broadcast_select_fusion.8), channel_id=1, source_target_pairs={{0,4},{1,5},{2,6},{3,7},{4,0},{5,1},{6,2},{7,3},{8,12},{9,13},{10,... | collective-permute-start | bytes 700424 | tf_op jit(solution)/shard_map/ppermute | solution.py:302
  21.3 11.3 %collective-permute-start.3 = (bf16[24,3840]{1,0:T(8,128)(2,1)S(1)}, bf16[24,3840]{1,0:T(8,128)(2,1)S(1)}, u32[]{:S(2)}, u32[]{:S(2)}) collective-permute-start(bf16[24,3840]{1,0:T(8,128)(2,1)S(1)} %constant_dynamic-update-slice_fusion), channel_id=1, source_target_pairs={{0,8},{1,9},{2,10},{3,11},{4,12},{5,13},{6,14},{7,15},{8,0},{9,1},... | collective-permute-start | bytes 552968 | tf_op jit(solution)/shard_map/ppermute | solution.py:302
  24.4 9.0 %collective-permute-start.2 = (bf16[2,2,24,2432]{3,2,1,0:T(8,128)(2,1)S(1)}, bf16[2,2,24,2432]{3,2,1,0:T(8,128)(2,1)S(1)}, u32[]{:S(2)}, u32[]{:S(2)}) collective-permute-start(bf16[2,2,24,2432]{3,2,1,0:T(8,128)(2,1)S(1)} %broadcast_select_fusion.5), channel_id=1, source_target_pairs={{0,16},{1,3},{2,18},{3,1},{4,20},{5,7},{6,22},{7,5},{8,24},{9,11},... | collective-permute-start | bytes 1400840 | tf_op jit(solution)/shard_map/ppermute | solution.py:302
  33.8 13.6 %collective-permute-start.4 = (bf16[2,2,2,24,2432]{4,3,0,2,1:T(8,128)(2,1)S(1)}, bf16[2,2,2,24,2432]{4,3,0,2,1:T(8,128)(2,1)S(1)}, u32[]{:S(2)}, u32[]{:S(2)}) collective-permute-start(bf16[2,2,2,24,2432]{4,3,0,2,1:T(8,128)(2,1)S(1)} %broadcast_select_fusion.2), channel_id=1, source_target_pairs={{0,2},{1,17},{2,0},{3,19},{4,6},{5,21},{6,4},{7,23},{8,10},{9,25},... | collective-permute-start | bytes 2801672 | tf_op jit(solution)/shard_map/ppermute | solution.py:302
  35.6 21.3 %copy-start.24 = (f32[1024]{0:T(1024)}, f32[1024]{0:T(1024)S(1)}, u32[]{:S(2)}) copy-start(f32[1024]{0:T(1024)S(1)} %broadcast_multiply_fusion.1) | copy-start | bytes 12292
  36.3 11.1 %collective-permute-start.7 = (bf16[2,24,3840]{2,1,0:T(8,128)(2,1)}, bf16[2,24,3840]{2,1,0:T(8,128)(2,1)}, u32[]{:S(2)}, u32[]{:S(2)}) collective-permute-start(bf16[2,24,3840]{2,1,0:T(8,128)(2,1)} %broadcast_select_fusion.6), channel_id=1, source_target_pairs={{0,4},{1,5},{2,6},{3,7},{4,0},{5,1},{6,2},{7,3},{8,12},{9,13},{10,... | collective-permute-start | bytes 1105928 | tf_op jit(solution)/shard_map/ppermute | solution.py:302
  38.5 18.5 %copy-start.31 = (f32[1024]{0:T(1024)}, f32[1024]{0:T(1024)S(1)}, u32[]{:S(2)}) copy-start(f32[1024]{0:T(1024)S(1)} %add_rsqrt_fusion.1) | copy-start | bytes 12292
  38.5 11.0 %collective-permute-start.5 = (bf16[2,2,2,24,2432]{4,3,0,2,1:T(8,128)(2,1)S(1)}, bf16[2,2,2,24,2432]{4,3,0,2,1:T(8,128)(2,1)S(1)}, u32[]{:S(2)}, u32[]{:S(2)}) collective-permute-start(bf16[2,2,2,24,2432]{4,3,0,2,1:T(8,128)(2,1)S(1)} %broadcast_select_fusion.2), channel_id=1, source_target_pairs={{0,1},{1,0},{2,3},{3,2},{4,5},{5,4},{6,7},{7,6},{8,9},{9,8},{10,11... | collective-permute-start | bytes 2801672 | tf_op jit(solution)/shard_map/ppermute | solution.py:302
  47.4 2.5 collective-permute-start.6
  51.9 3.5 %copy-start.15 = (bf16[2,2,24,3840]{3,2,1,0:T(8,128)(2,1)S(1)}, bf16[2,2,24,3840]{3,2,1,0:T(8,128)(2,1)}, u32[]{:S(2)}) copy-start(bf16[2,2,24,3840]{3,2,1,0:T(8,128)(2,1)} %broadcast_select_fusion.3) | copy-start | bytes 2211844
  52.8 12.1 %collective-permute-start.9 = (bf16[96,768]{1,0:T(8,128)(2,1)S(1)}, bf16[96,768]{1,0:T(8,128)(2,1)S(1)}, u32[]{:S(2)}, u32[]{:S(2)}) collective-permute-start(bf16[96,768]{1,0:T(8,128)(2,1)S(1)} %copy-done.23), channel_id=1, source_target_pairs={{0,8},{1,9},{2,10},{3,11},{4,12},{5,13},{6,14},{7,15},{8,0},{9,1},... | collective-permute-start | bytes 442376 | tf_op jit(solution)/shard_map/ppermute | solution.py:302
  55.4 9.5 %copy-start.26 = (f32[768]{0:T(1024)}, f32[768]{0:T(1024)S(1)}, u32[]{:S(2)}) copy-start(f32[768]{0:T(1024)S(1)} %get-tuple-element.193) | copy-start | bytes 9220
  55.4 9.5 %copy-start.28 = (f32[768]{0:T(1024)}, f32[768]{0:T(1024)S(1)}, u32[]{:S(2)}) copy-start(f32[768]{0:T(1024)S(1)} %get-tuple-element.195) | copy-start | bytes 9220
  55.4 11.5 %collective-permute-start.8 = (bf16[2,2,24,3840]{3,2,1,0:T(8,128)(2,1)S(1)}, bf16[2,2,24,3840]{3,2,1,0:T(8,128)(2,1)S(1)}, u32[]{:S(2)}, u32[]{:S(2)}) collective-permute-start(bf16[2,2,24,3840]{3,2,1,0:T(8,128)(2,1)S(1)} %copy-done.15), channel_id=1, source_target_pairs={{0,16},{1,3},{2,18},{3,1},{4,20},{5,7},{6,22},{7,5},{8,24},{9,11},... | collective-permute-start | bytes 2211848 | tf_op jit(solution)/shard_map/ppermute | solution.py:302
  57.0 10.0 %copy-start.16 = (bf16[2,2,24,3840]{3,2,1,0:T(8,128)(2,1)S(1)}, bf16[2,2,24,3840]{3,2,1,0:T(8,128)(2,1)}, u32[]{:S(2)}) copy-start(bf16[2,2,24,3840]{3,2,1,0:T(8,128)(2,1)} %broadcast_select_fusion.3) | copy-start | bytes 2211844
  67.1 26.6 %copy-start.30 = (s32[1,1024]{1,0:T(1,128)S(1)}, s32[1,1024]{1,0:T(1,128)}, u32[]{:S(2)}) copy-start(s32[1,1024]{1,0:T(1,128)} %seg_ref.1) | copy-start | bytes 12292
  67.2 24.8 %collective-permute-start.11 = (bf16[2,2,2,24,3840]{4,3,0,2,1:T(8,128)(2,1)S(1)}, bf16[2,2,2,24,3840]{4,3,0,2,1:T(8,128)(2,1)}, u32[]{:S(2)}, u32[]{:S(2)}) collective-permute-start(bf16[2,2,2,24,3840]{4,3,0,2,1:T(8,128)(2,1)S(1)} %broadcast_select_fusion), channel_id=1, source_target_pairs={{0,1},{1,0},{2,3},{3,2},{4,5},{5,4},{6,7},{7,6},{8,9},{9,8},{10,11... | collective-permute-start | bytes 4423688 | tf_op jit(solution)/shard_map/ppermute | solution.py:302
  67.2 24.7 %collective-permute-start.10 = (bf16[2,2,2,24,3840]{4,3,0,2,1:T(8,128)(2,1)S(1)}, bf16[2,2,2,24,3840]{4,3,0,2,1:T(8,128)(2,1)}, u32[]{:S(2)}, u32[]{:S(2)}) collective-permute-start(bf16[2,2,2,24,3840]{4,3,0,2,1:T(8,128)(2,1)S(1)} %broadcast_select_fusion), channel_id=1, source_target_pairs={{0,2},{1,17},{2,0},{3,19},{4,6},{5,21},{6,4},{7,23},{8,10},{9,25},... | collective-permute-start | bytes 4423688 | tf_op jit(solution)/shard_map/ppermute | solution.py:302
  68.8 21.3 %collective-permute-start.12 = (bf16[2,96,768]{2,1,0:T(8,128)(2,1)S(1)}, bf16[2,96,768]{2,1,0:T(8,128)(2,1)}, u32[]{:S(2)}, u32[]{:S(2)}) collective-permute-start(bf16[2,96,768]{2,1,0:T(8,128)(2,1)S(1)} %broadcast_select_fusion.7), channel_id=1, source_target_pairs={{0,4},{1,5},{2,6},{3,7},{4,0},{5,1},{6,2},{7,3},{8,12},{9,13},{10,... | collective-permute-start | bytes 884744 | tf_op jit(solution)/shard_map/ppermute | solution.py:302
  92.0 12.7 %collective-permute-start.13 = (bf16[2,2,2,24,3840]{4,3,0,2,1:T(8,128)(2,1)}, bf16[2,2,2,24,3840]{4,3,0,2,1:T(8,128)(2,1)}, u32[]{:S(2)}, u32[]{:S(2)}) collective-permute-start(bf16[2,2,2,24,3840]{4,3,0,2,1:T(8,128)(2,1)} %collective-permute-done.10), channel_id=1, source_target_pairs={{0,1},{1,0},{2,3},{3,2},{4,5},{5,4},{6,7},{7,6},{8,9},{9,8},{10,11... | collective-permute-start | bytes 4423688 | tf_op jit(solution)/shard_map/ppermute | solution.py:302
  92.0 10.3 %collective-permute-start.14 = (bf16[2,2,96,768]{3,2,1,0:T(8,128)(2,1)}, bf16[2,2,96,768]{3,2,1,0:T(8,128)(2,1)}, u32[]{:S(2)}, u32[]{:S(2)}) collective-permute-start(bf16[2,2,96,768]{3,2,1,0:T(8,128)(2,1)} %broadcast_select_fusion.4), channel_id=1, source_target_pairs={{0,16},{1,3},{2,18},{3,1},{4,20},{5,7},{6,22},{7,5},{8,24},{9,11},... | collective-permute-start | bytes 1769480 | tf_op jit(solution)/shard_map/ppermute | solution.py:302
  117.2 4.5 %copy-start.8 = (bf16[768,3840]{1,0:T(8,128)(2,1)S(1)}, bf16[768,3840]{1,0:T(8,128)(2,1)}, u32[]{:S(2)}) copy-start(bf16[768,3840]{1,0:T(8,128)(2,1)} %bitcast_select_fusion.weight_ref) | copy-start | bytes 17694724
  120.3 14.2 %copy-start.18 = (bf16[1024,768]{1,0:T(8,128)(2,1)}, bf16[1024,768]{1,0:T(8,128)(2,1)S(1)}, u32[]{:S(2)}) copy-start(bf16[1024,768]{1,0:T(8,128)(2,1)S(1)} %add_convert_fusion.2) | copy-start | bytes 4718596
  120.4 16.2 %copy-start.17 = (bf16[1024,768]{1,0:T(8,128)(2,1)S(1)}, bf16[1024,768]{1,0:T(8,128)(2,1)}, u32[]{:S(2)}) copy-start(bf16[1024,768]{1,0:T(8,128)(2,1)} %select_bitcast_fusion.add_ref) | copy-start | bytes 4718596
  120.4 14.2 %collective-permute-start.16 = (bf16[2,2,2,96,768]{4,3,2,1,0:T(8,128)(2,1)S(1)}, bf16[2,2,2,96,768]{4,3,2,1,0:T(8,128)(2,1)S(1)}, u32[]{:S(2)}, u32[]{:S(2)}) collective-permute-start(bf16[2,2,2,96,768]{4,3,2,1,0:T(8,128)(2,1)S(1)} %copy-done.5), channel_id=1, source_target_pairs={{0,1},{1,0},{2,3},{3,2},{4,5},{5,4},{6,7},{7,6},{8,9},{9,8},{10,11... | collective-permute-start | bytes 3538952 | tf_op jit(solution)/shard_map/ppermute | solution.py:302
  120.4 16.2 %collective-permute-start.15 = (bf16[2,2,2,96,768]{4,3,2,1,0:T(8,128)(2,1)S(1)}, bf16[2,2,2,96,768]{4,3,2,1,0:T(8,128)(2,1)S(1)}, u32[]{:S(2)}, u32[]{:S(2)}) collective-permute-start(bf16[2,2,2,96,768]{4,3,2,1,0:T(8,128)(2,1)S(1)} %copy-done.5), channel_id=1, source_target_pairs={{0,2},{1,17},{2,0},{3,19},{4,6},{5,21},{6,4},{7,23},{8,10},{9,25},... | collective-permute-start | bytes 3538952 | tf_op jit(solution)/shard_map/ppermute | solution.py:302
  136.6 9.3 %collective-permute-start.17 = (bf16[2,2,2,96,768]{4,3,2,1,0:T(8,128)(2,1)S(1)}, bf16[2,2,2,96,768]{4,3,2,1,0:T(8,128)(2,1)S(1)}, u32[]{:S(2)}, u32[]{:S(2)}) collective-permute-start(bf16[2,2,2,96,768]{4,3,2,1,0:T(8,128)(2,1)S(1)} %collective-permute-done.15), channel_id=1, source_target_pairs={{0,1},{1,0},{2,3},{3,2},{4,5},{5,4},{6,7},{7,6},{8,9},{9,8},{10,11... | collective-permute-start | bytes 3538952 | tf_op jit(solution)/shard_map/ppermute | solution.py:302
  145.3 13.5 %collective-permute-start.18 = (bf16[2,2,2,2,96,768]{5,4,3,2,1,0:T(8,128)(2,1)S(1)}, bf16[2,2,2,2,96,768]{5,4,3,2,1,0:T(8,128)(2,1)}, u32[]{:S(2)}, u32[]{:S(2)}) collective-permute-start(bf16[2,2,2,2,96,768]{5,4,3,2,1,0:T(8,128)(2,1)S(1)} %dynamic-slice_bitcast_fusion.4), channel_id=1, source_target_pairs={{0,1},{1,0},{2,3},{3,2},{4,5},{5,4},{6,7},{7,6},{8,9},{9,8},{10,11... | collective-permute-start | bytes 7077896 | tf_op jit(solution)/shard_map/ppermute | solution.py:302
  149.3 9.4 %copy-start.11 = (bf16[3072,768]{1,0:T(8,128)(2,1)}, bf16[3072,768]{1,0:T(8,128)(2,1)S(1)}, u32[]{:S(2)}) copy-start(bf16[3072,768]{1,0:T(8,128)(2,1)S(1)} %bitcast_select_fusion.1) | copy-start | bytes 14155780
  158.8 5.7 %copy-start.33 = (bf16[1024,3072]{1,0:T(8,128)(2,1)}, bf16[1024,3072]{1,0:T(8,128)(2,1)S(1)}, u32[]{:S(2)}) copy-start(bf16[1024,3072]{1,0:T(8,128)(2,1)S(1)} %multiply_convert_fusion.grad_ref) | copy-start | bytes 18874372
  162.8 9.8 %copy-start.2 = (f32[2,2,2,2,96,768]{5,4,3,2,1,0:T(8,128)}, f32[2,2,2,2,96,768]{5,4,3,2,1,0:T(8,128)S(1)}, u32[]{:S(2)}) copy-start(f32[2,2,2,2,96,768]{5,4,3,2,1,0:T(8,128)S(1)} %convert_add_fusion.1) | copy-start | bytes 14155780
  163.1 27.3 %collective-permute-start.19 = (bf16[2,2,2,96,768]{4,3,1,2,0:T(8,128)(2,1)S(1)}, bf16[2,2,2,96,768]{4,3,1,2,0:T(8,128)(2,1)S(1)}, u32[]{:S(2)}, u32[]{:S(2)}) collective-permute-start(bf16[2,2,2,96,768]{4,3,1,2,0:T(8,128)(2,1)S(1)} %fusion.15), channel_id=1, source_target_pairs={{0,2},{1,17},{2,0},{3,19},{4,6},{5,21},{6,4},{7,23},{8,10},{9,25},... | collective-permute-start | bytes 3538952 | tf_op jit(solution)/shard_map/ppermute | solution.py:302
  184.6 5.8 %slice-start = ((s8[4718592]{0:T(1024)(128)(4,1)}), s8[4194304]{0:T(1024)(128)(4,1)S(1)}, s32[]{:S(2)}) async-start(s8[4718592]{0:T(1024)(128)(4,1)} %bitcast.249), calls=%async_computation | async-start | bytes 8388608
  184.6 5.8 %slice-start.1 = ((s8[4718592]{0:T(1024)(128)(4,1)}), s8[524288]{0:T(1024)(128)(4,1)S(1)}, s32[]{:S(2)}) async-start(s8[4718592]{0:T(1024)(128)(4,1)} %bitcast.249), calls=%async_computation.1 | async-start | bytes 1048576
  192.7 7.8 %collective-permute-start.20 = (bf16[2,2,2,2,24,3840]{5,4,3,2,1,0:T(8,128)(2,1)}, bf16[2,2,2,2,24,3840]{5,4,3,2,1,0:T(8,128)(2,1)}, u32[]{:S(2)}, u32[]{:S(2)}) collective-permute-start(bf16[2,2,2,2,24,3840]{5,4,3,2,1,0:T(8,128)(2,1)} %pad_maximum_fusion), channel_id=1, source_target_pairs={{0,1},{1,0},{2,3},{3,2},{4,5},{5,4},{6,7},{7,6},{8,9},{9,8},{10,11... | collective-permute-start | bytes 8847368 | tf_op jit(solution)/shard_map/ppermute | solution.py:302
  192.8 7.4 %slice-start.2 = ((s8[4718592]{0:T(1024)(128)(4,1)}), s8[4194304]{0:T(1024)(128)(4,1)S(1)}, s32[]{:S(2)}) async-start(s8[4718592]{0:T(1024)(128)(4,1)} %bitcast.255), calls=%async_computation.2 | async-start | bytes 8388608
  194.3 5.9 %copy-start.21 = (bf16[768,768]{1,0:T(8,128)(2,1)S(1)}, bf16[768,768]{1,0:T(8,128)(2,1)}, u32[]{:S(2)}) copy-start(bf16[768,768]{1,0:T(8,128)(2,1)} %copy-done.20) | copy-start | bytes 3538948
  194.3 6.0 %slice-start.3 = ((s8[4718592]{0:T(1024)(128)(4,1)}), s8[524288]{0:T(1024)(128)(4,1)S(1)}, s32[]{:S(2)}) async-start(s8[4718592]{0:T(1024)(128)(4,1)} %bitcast.255), calls=%async_computation.3 | async-start | bytes 1048576
  198.7 35.9 %collective-permute-start.22 = (bf16[2,2,96,768]{3,2,0,1:T(8,128)(2,1)S(1)}, bf16[2,2,96,768]{3,2,0,1:T(8,128)(2,1)S(1)}, u32[]{:S(2)}, u32[]{:S(2)}) collective-permute-start(bf16[2,2,96,768]{3,2,0,1:T(8,128)(2,1)S(1)} %fusion.22), channel_id=1, source_target_pairs={{0,16},{1,3},{2,18},{3,1},{4,20},{5,7},{6,22},{7,5},{8,24},{9,11},... | collective-permute-start | bytes 1769480 | tf_op jit(solution)/shard_map/ppermute | solution.py:302
  207.2 27.4 %collective-permute-start.21 = (bf16[2,2,2,24,3840]{4,3,2,1,0:T(8,128)(2,1)}, bf16[2,2,2,24,3840]{4,3,2,1,0:T(8,128)(2,1)}, u32[]{:S(2)}, u32[]{:S(2)}) collective-permute-start(bf16[2,2,2,24,3840]{4,3,2,1,0:T(8,128)(2,1)} %fusion.13), channel_id=1, source_target_pairs={{0,2},{1,17},{2,0},{3,19},{4,6},{5,21},{6,4},{7,23},{8,10},{9,25},... | collective-permute-start | bytes 4423688 | tf_op jit(solution)/shard_map/ppermute | solution.py:302
  207.6 27.0 %copy-start.25 = (f32[1024]{0:T(1024)S(1)}, f32[1024]{0:T(1024)}, u32[]{:S(2)}) copy-start(f32[1024]{0:T(1024)} %copy-done.24) | copy-start | bytes 12292
  207.6 27.0 %copy-start.27 = (f32[768]{0:T(1024)S(1)}, f32[768]{0:T(1024)}, u32[]{:S(2)}) copy-start(f32[768]{0:T(1024)} %copy-done.26) | copy-start | bytes 9220
  207.6 27.0 %copy-start.29 = (f32[768]{0:T(1024)S(1)}, f32[768]{0:T(1024)}, u32[]{:S(2)}) copy-start(f32[768]{0:T(1024)} %copy-done.28) | copy-start | bytes 9220
  207.6 27.1 %copy-start.32 = (f32[1024]{0:T(1024)S(1)}, f32[1024]{0:T(1024)}, u32[]{:S(2)}) copy-start(f32[1024]{0:T(1024)} %copy-done.31) | copy-start | bytes 12292
  241.7 6.0 %collective-permute-start.23 = (bf16[2,2,2,2,24,2304]{5,4,3,2,1,0:T(8,128)(2,1)S(1)}, bf16[2,2,2,2,24,2304]{5,4,3,2,1,0:T(8,128)(2,1)S(1)}, u32[]{:S(2)}, u32[]{:S(2)}) collective-permute-start(bf16[2,2,2,2,24,2304]{5,4,3,2,1,0:T(8,128)(2,1)S(1)} %dynamic-slice_bitcast_fusion.5), channel_id=1, source_target_pairs={{0,1},{1,0},{2,3},{3,2},{4,5},{5,4},{6,7},{7,6},{8,9},{9,8},{10,11... | collective-permute-start | bytes 5308424 | tf_op jit(solution)/shard_map/ppermute | solution.py:302
  249.7 20.7 %collective-permute-start.24 = (bf16[2,2,2,24,2304]{4,3,1,2,0:T(8,128)(2,1)}, bf16[2,2,2,24,2304]{4,3,1,2,0:T(8,128)(2,1)}, u32[]{:S(2)}, u32[]{:S(2)}) collective-permute-start(bf16[2,2,2,24,2304]{4,3,1,2,0:T(8,128)(2,1)} %fusion.17), channel_id=1, source_target_pairs={{0,2},{1,17},{2,0},{3,19},{4,6},{5,21},{6,4},{7,23},{8,10},{9,25},... | collective-permute-start | bytes 2654216 | tf_op jit(solution)/shard_map/ppermute | solution.py:302
  253.5 10.5 %collective-permute-start.26 = (bf16[2,96,768]{2,1,0:T(8,128)(2,1)}, bf16[2,96,768]{2,1,0:T(8,128)(2,1)}, u32[]{:S(2)}, u32[]{:S(2)}) collective-permute-start(bf16[2,96,768]{2,1,0:T(8,128)(2,1)} %fusion.25), channel_id=1, source_target_pairs={{0,4},{1,5},{2,6},{3,7},{4,0},{5,1},{6,2},{7,3},{8,12},{9,13},{10,... | collective-permute-start | bytes 884744 | tf_op jit(solution)/shard_map/ppermute | solution.py:302
  253.5 16.4 %collective-permute-start.25 = (bf16[2,2,24,3840]{3,2,1,0:T(8,128)(2,1)}, bf16[2,2,24,3840]{3,2,1,0:T(8,128)(2,1)}, u32[]{:S(2)}, u32[]{:S(2)}) collective-permute-start(bf16[2,2,24,3840]{3,2,1,0:T(8,128)(2,1)} %fusion.21), channel_id=1, source_target_pairs={{0,16},{1,3},{2,18},{3,1},{4,20},{5,7},{6,22},{7,5},{8,24},{9,11},... | collective-permute-start | bytes 2211848 | tf_op jit(solution)/shard_map/ppermute | solution.py:302
  274.8 3.9 %copy-start.14 = (f32[2,2,96,768]{3,2,0,1:T(8,128)S(1)}, f32[2,2,96,768]{3,2,0,1:T(8,128)}, u32[]{:S(2)}) copy-start(f32[2,2,96,768]{3,2,0,1:T(8,128)} %copy-done.13) | copy-start | bytes 3538948
  275.0 6.7 %copy-start.4 = (f32[1024,768]{1,0:T(8,128)S(1)}, f32[1024,768]{1,0:T(8,128)}, u32[]{:S(2)}) copy-start(f32[1024,768]{1,0:T(8,128)} %copy-done.3) | copy-start | bytes 9437188
  275.0 21.1 %collective-permute-start.27 = (bf16[2,2,24,2304]{3,2,0,1:T(8,128)(2,1)}, bf16[2,2,24,2304]{3,2,0,1:T(8,128)(2,1)S(1)}, u32[]{:S(2)}, u32[]{:S(2)}) collective-permute-start(bf16[2,2,24,2304]{3,2,0,1:T(8,128)(2,1)} %fusion.23), channel_id=1, source_target_pairs={{0,16},{1,3},{2,18},{3,1},{4,20},{5,7},{6,22},{7,5},{8,24},{9,11},... | collective-permute-start | bytes 1327112 | tf_op jit(solution)/shard_map/ppermute | solution.py:302
  279.7 16.4 %copy-start.10 = (f32[2,2,2,24,2304]{4,3,1,2,0:T(8,128)S(1)}, f32[2,2,2,24,2304]{4,3,1,2,0:T(8,128)}, u32[]{:S(2)}) copy-start(f32[2,2,2,24,2304]{4,3,1,2,0:T(8,128)} %copy-done.9) | copy-start | bytes 5308420
  279.8 11.3 %collective-permute-start.30 = (f32[2,2,2,2,1,128]{5,3,2,1,4,0:T(2,128)S(1)}, f32[2,2,2,2,1,128]{5,3,2,1,4,0:T(2,128)S(1)}, u32[]{:S(2)}, u32[]{:S(2)}) collective-permute-start(f32[2,2,2,2,1,128]{5,3,2,1,4,0:T(2,128)S(1)} %bitcast.274), channel_id=1, source_target_pairs={{0,1},{1,0},{2,3},{3,2},{4,5},{5,4},{6,7},{7,6},{8,9},{9,8},{10,11... | collective-permute-start | bytes 24584 | tf_op jit(solution)/shard_map/ppermute | solution.py:302
  279.8 11.2 %collective-permute-start.29 = (bf16[96,768]{1,0:T(8,128)(2,1)S(1)}, bf16[96,768]{1,0:T(8,128)(2,1)S(1)}, u32[]{:S(2)}, u32[]{:S(2)}) collective-permute-start(bf16[96,768]{1,0:T(8,128)(2,1)S(1)} %fusion.29), channel_id=1, source_target_pairs={{0,8},{1,9},{2,10},{3,11},{4,12},{5,13},{6,14},{7,15},{8,0},{9,1},... | collective-permute-start | bytes 442376 | tf_op jit(solution)/shard_map/ppermute | solution.py:302
  281.6 13.8 %collective-permute-start.28 = (bf16[2,24,3840]{2,1,0:T(8,128)(2,1)S(1)}, bf16[2,24,3840]{2,1,0:T(8,128)(2,1)S(1)}, u32[]{:S(2)}, u32[]{:S(2)}) collective-permute-start(bf16[2,24,3840]{2,1,0:T(8,128)(2,1)S(1)} %fusion.24), channel_id=1, source_target_pairs={{0,4},{1,5},{2,6},{3,7},{4,0},{5,1},{6,2},{7,3},{8,12},{9,13},{10,... | collective-permute-start | bytes 1105928 | tf_op jit(solution)/shard_map/ppermute | solution.py:302
  296.3 3.7 %collective-permute-start.34 = (f32[2,2,2,1,128]{4,2,1,0,3:T(2,128)S(1)}, f32[2,2,2,1,128]{4,2,1,0,3:T(2,128)S(1)}, u32[]{:S(2)}, u32[]{:S(2)}) collective-permute-start(f32[2,2,2,1,128]{4,2,1,0,3:T(2,128)S(1)} %bitcast_select_fusion.10), channel_id=1, source_target_pairs={{0,2},{1,17},{2,0},{3,19},{4,6},{5,21},{6,4},{7,23},{8,10},{9,25},... | collective-permute-start | bytes 12296 | tf_op jit(solution)/shard_map/ppermute | solution.py:302
  297.3 18.2 %collective-permute-start.31 = (bf16[2,24,2304]{2,1,0:T(8,128)(2,1)S(1)}, bf16[2,24,2304]{2,1,0:T(8,128)(2,1)S(1)}, u32[]{:S(2)}, u32[]{:S(2)}) collective-permute-start(bf16[2,24,2304]{2,1,0:T(8,128)(2,1)S(1)} %fusion.27), channel_id=1, source_target_pairs={{0,4},{1,5},{2,6},{3,7},{4,0},{5,1},{6,2},{7,3},{8,12},{9,13},{10,... | collective-permute-start | bytes 663560 | tf_op jit(solution)/shard_map/ppermute | solution.py:302
  300.0 3.6 %collective-permute-start.35 = (f32[2,2,1,128]{3,1,0,2:T(2,128)S(1)}, f32[2,2,1,128]{3,1,0,2:T(2,128)S(1)}, u32[]{:S(2)}, u32[]{:S(2)}) collective-permute-start(f32[2,2,1,128]{3,1,0,2:T(2,128)S(1)} %fusion.36), channel_id=1, source_target_pairs={{0,16},{1,3},{2,18},{3,1},{4,20},{5,7},{6,22},{7,5},{8,24},{9,11},... | collective-permute-start | bytes 6152 | tf_op jit(solution)/shard_map/ppermute | solution.py:302
  303.7 3.6 %collective-permute-start.36 = (f32[2,1,128]{2,1,0:T(1,128)S(1)}, f32[2,1,128]{2,1,0:T(1,128)S(1)}, u32[]{:S(2)}, u32[]{:S(2)}) collective-permute-start(f32[2,1,128]{2,1,0:T(1,128)S(1)} %fusion.39), channel_id=1, source_target_pairs={{0,4},{1,5},{2,6},{3,7},{4,0},{5,1},{6,2},{7,3},{8,12},{9,13},{10,... | collective-permute-start | bytes 3080 | tf_op jit(solution)/shard_map/ppermute | solution.py:302
  304.1 11.5 %collective-permute-start.33 = (bf16[24,3840]{1,0:T(8,128)(2,1)S(1)}, bf16[24,3840]{1,0:T(8,128)(2,1)S(1)}, u32[]{:S(2)}, u32[]{:S(2)}) collective-permute-start(bf16[24,3840]{1,0:T(8,128)(2,1)S(1)} %fusion.28), channel_id=1, source_target_pairs={{0,8},{1,9},{2,10},{3,11},{4,12},{5,13},{6,14},{7,15},{8,0},{9,1},... | collective-permute-start | bytes 552968 | tf_op jit(solution)/shard_map/ppermute | solution.py:302
  307.3 5.7 %collective-permute-start.37 = (f32[1,128]{1,0:T(1,128)S(1)}, f32[1,128]{1,0:T(1,128)S(1)}, u32[]{:S(2)}, u32[]{:S(2)}) collective-permute-start(f32[1,128]{1,0:T(1,128)S(1)} %fusion.42), channel_id=1, source_target_pairs={{0,8},{1,9},{2,10},{3,11},{4,12},{5,13},{6,14},{7,15},{8,0},{9,1},... | collective-permute-start | bytes 1544 | tf_op jit(solution)/shard_map/ppermute | solution.py:302
  315.6 5.8 %collective-permute-start.32 = (bf16[24,2304]{1,0:T(8,128)(2,1)S(1)}, bf16[24,2304]{1,0:T(8,128)(2,1)S(1)}, u32[]{:S(2)}, u32[]{:S(2)}) collective-permute-start(bf16[24,2304]{1,0:T(8,128)(2,1)S(1)} %fusion.31), channel_id=1, source_target_pairs={{0,8},{1,9},{2,10},{3,11},{4,12},{5,13},{6,14},{7,15},{8,0},{9,1},... | collective-permute-start | bytes 331784 | tf_op jit(solution)/shard_map/ppermute | solution.py:302
  (12 other events, 22.4 us)

commit v3 on v2

--- a/solution.py
+++ b/solution.py
@@ -542,19 +542,16 @@
     upper, grad_down, grad_project, other, other_down = tie(
         upper, grad_down, grad_project, other, other_down
     )
+    upper = add(near_cut(upper, sizes, 0), other)
+    sent, grad_project = tie(next_cut(upper, sizes, 1).astype(low), grad_project)
+    other = swap_next(sent, sizes)
     grad_qkv = jnp.dot(normed.T, grad_project, preferred_element_type=jnp.float32).astype(low)
-    sent, upper, grad_down, grad_project = tie(
-        core_cut((grad_qkv,), sizes, 1), upper, grad_down, grad_project
+    sent, grad_down, grad_project, other = tie(
+        core_cut((grad_qkv,), sizes, 1), grad_down, grad_project, other
     )
     other_qkv = swap_core(sent, sizes)
-    upper = add(near_cut(upper, sizes, 0), other)
     grad_down = add(next_cut(grad_down, sizes, 0), other_down)
-    grad_qkv, sent, sent_down = tie(
-        grad_qkv,
-        next_cut(upper, sizes, 1).astype(low),
-        far_cut(grad_down, sizes, near_far, 1).astype(low),
-    )
-    other = swap_next(sent, sizes)
+    grad_qkv, sent_down = tie(grad_qkv, far_cut(grad_down, sizes, near_far, 1).astype(low))
     other_down = swap_far(sent_down, sizes, near_far)
     grad_qkv = add(core_cut((grad_qkv,), sizes, 0), other_qkv)
     sent, grad_project = tie(near_cut(grad_qkv, sizes, 1).astype(low), grad_project)

time: 327 us -> 324 us (level)
  waiting for transfers between devices: 64.4 us -> 53.9 us
  starting transfers between devices: 35.5 us -> 43.9 us
    ppermute x38, waiting for transfers between devices: 64.4 us -> 53.9 us  [exchange(): lax.ppermute(value, BOTH, [(i, i ^ masks[i & 1]) for i in range(2 ** coun...]
    ppermute x38, starting transfers between devices: 35.5 us -> 43.9 us  [exchange(): lax.ppermute(value, BOTH, [(i, i ^ masks[i & 1]) for i in range(2 ** coun...]
    unnamed x79 -> x85, local copies, waits for them, and re-layouts: 11.6 us -> 13.3 us
  transfers between devices with their start and end apart: 38 -> 38, of which waited for: 16 -> 15; matrix products, arithmetic and copies ran while one was open for 31% -> 31% of each run, Pallas kernels for 21% -> 21%
where the time goes in v3:
time: 324 us; the launch traced here: 321 us
  matrix products  70.7 us (22%)
  Pallas kernels  67.8 us (21%)
  other arithmetic  54.4 us (17%)
  waiting for transfers between devices  53.9 us (17%)
  starting transfers between devices  43.9 us (14%)
  local copies, waits for them, and re-layouts  24.9 us (8%)
  between operations  4.94 us (2%)
    ppermute x38, waiting for transfers between devices, exchange(): lax.ppermute(value, BOTH, [(i, i ^ masks[i & 1]) for i in range(2 ** coun...  53.9 us
    ppermute x38, starting transfers between devices, exchange(): lax.ppermute(value, BOTH, [(i, i ^ masks[i & 1]) for i in range(2 ** coun...  43.9 us
    pallas_call x1, Pallas kernels, row_back(): pl.pallas_call(attend_back_kernel, name='attend_backward', grid=(blocks,)...  27 us
    pallas_call x2, Pallas kernels, matmul_norm_back(): pl.pallas_call(norm_back_kernel, name=name, grid=(rows // STRIP,), in_spe...  21.9 us
    pallas_call x1, Pallas kernels, attend_row(): pl.pallas_call(attend_kernel, name='attend_forward', grid=(blocks,), in_s...  18.9 us
    add x20, other arithmetic, add(): return mine.astype(jnp.float32) + other.astype(jnp.float32)  17.7 us
    unnamed x85, local copies, waits for them, and re-layouts  13.3 us
    dot_general x1, matrix products, body(): hidden = jnp.dot(normed_two, up_full, preferred_element_type=jnp.float32)  12.9 us
  transfers between devices with their start and end apart: 38, of which 15 were waited for; matrix products, arithmetic and copies ran while one was open for 31% of the time, Pallas kernels for 21%

profile of v3, /device:TPU:0, one launch (start us, length us, event | category | flops | bytes accessed | tf_op | source)
XLA Modules:
  0.0 320.6 jit_solution(14219872240602913855)
XLA Ops:
  2.5 4.1 %collective-permute-start = (bf16[24,2432]{1,0:T(8,128)(2,1)S(1)}, bf16[24,2432]{1,0:T(8,128)(2,1)S(1)}, u32[]{:S(2)}, u32[]{:S(2)}) collective-permute-start(bf16[24,2432]{1,0:T(8,128)(2,1)S(1)} %fusion.30), channel_id=1, source_target_pairs={{0,8},{1,9},{2,10},{3,11},{4,12},{5,13},{6,14},{7,15},{8,0},{9,1},... | collective-permute-start | bytes 350216 | tf_op jit(solution)/shard_map/ppermute | solution.py:302
  6.6 5.7 %collective-permute-done = bf16[24,2432]{1,0:T(8,128)(2,1)S(1)} collective-permute-done((bf16[24,2432]{1,0:T(8,128)(2,1)S(1)}, bf16[24,2432]{1,0:T(8,128)(2,1)S(1)}, u32[]{:S(2)}, u32[]{:S(2)}) %collective-permute-start) | collective-permute-done | bytes 116768 | tf_op jit(solution)/shard_map/ppermute | solution.py:302
  13.3 6.1 %collective-permute-done.1 = bf16[2,24,2432]{2,1,0:T(8,128)(2,1)S(1)} collective-permute-done((bf16[2,24,2432]{2,1,0:T(8,128)(2,1)S(1)}, bf16[2,24,2432]{2,1,0:T(8,128)(2,1)S(1)}, u32[]{:S(2)}, u32[]{:S(2)}) %collective-permute-start.1) | collective-permute-done | bytes 233504 | tf_op jit(solution)/shard_map/ppermute | solution.py:302
  21.3 3.1 collective-permute-start.3
  24.4 1.5 collective-permute-start.2
  25.9 6.7 %collective-permute-done.3 = bf16[24,3840]{1,0:T(8,128)(2,1)S(1)} collective-permute-done((bf16[24,3840]{1,0:T(8,128)(2,1)S(1)}, bf16[24,3840]{1,0:T(8,128)(2,1)S(1)}, u32[]{:S(2)}, u32[]{:S(2)}) %collective-permute-start.3) | collective-permute-done | bytes 184352 | tf_op jit(solution)/shard_map/ppermute | solution.py:302
  33.8 1.6 collective-permute-start.4
  38.6 8.8 %collective-permute-done.4 = bf16[2,2,2,24,2432]{4,3,0,2,1:T(8,128)(2,1)S(1)} collective-permute-done((bf16[2,2,2,24,2432]{4,3,0,2,1:T(8,128)(2,1)S(1)}, bf16[2,2,2,24,2432]{4,3,0,2,1:T(8,128)(2,1)S(1)}, u32[]{:S(2)}, u32[]{:S(2)}) %collective-permute-start.4) | collective-permute-done | bytes 933920 | tf_op jit(solution)/shard_map/ppermute | solution.py:302
  47.4 2.1 broadcast_select_fusion.3
  49.9 2.3 select_select_fusion.5
  53.2 1.5 collective-permute-start.9
  55.8 1.6 collective-permute-start.8
  57.4 7.9 %convolution_convert_fusion.project_ref = bf16[1024,2304]{1,0:T(8,128)(2,1)} fusion(bf16[768,2432]{1,0:T(8,128)(2,1)} %copy-done.12, bf16[1,1024,768]{2,1,0:T(8,128)(2,1)S(1)} %copy-done.6, f32[768]{0:T(1024)S(1)} %get-tuple-element.195, f32[768]{0:T(1024)S(1)} %get-tuple-element.197, f32[1024]{0:T(1024)S(1)} %add_rsqrt_fusion.1, ...), kind=kOutput, calls=%fused_computation.7 | convolution fusion | flops 3630956544 | bytes 9844736 | tf_op jit(solution)/shard_map/dot_general | solution.py:470
  65.4 1.9 collective-permute-done.8
  67.6 1.6 collective-permute-start.10
  69.2 2.4 collective-permute-start.12
  71.6 18.9 %attend_forward.1 = (bf16[1024,768]{1,0:T(8,128)(2,1)}, f32[16,1024]{1,0:T(8,128)}, f32[8,384,128]{2,1,0:T(8,128)}, f32[8,128]{1,0:T(8,128)}) custom-call(f32[1]{0:T(128)S(6)} %copy.153.limit_ref, s32[1,1024]{1,0:T(1,128)} %seg_ref.1, bf16[1024,2304]{1,0:T(8,128)(2,1)} %convolution_convert_fusion.project_ref), custom_call_target="tpu_custom_call" | custom-call | flops 22649241600 | bytes 7864320 | tf_op jit(solution)/shard_map/attend_forward/pallas_call | solution.py:112
  90.4 1.9 broadcast_select_fusion.4
  92.4 1.6 collective-permute-start.14
  94.1 2.8 select_bitcast_fusion.add_ref
  96.9 5.7 %collective-permute-done.14 = bf16[2,2,96,768]{3,2,1,0:T(8,128)(2,1)} collective-permute-done((bf16[2,2,96,768]{3,2,1,0:T(8,128)(2,1)}, bf16[2,2,96,768]{3,2,1,0:T(8,128)(2,1)}, u32[]{:S(2)}, u32[]{:S(2)}) %collective-permute-start.14) | collective-permute-done | bytes 589856 | tf_op jit(solution)/shard_map/ppermute | solution.py:302
  102.6 2.5 broadcast_select_fusion.1
  105.1 6.2 %select_select_fusion.1 = (bf16[2,2,2,2,24,3840]{5,4,3,2,1,0:T(8,128)(2,1)S(1)}, bf16[2,2,2,2,24,3840]{5,4,3,2,1,0:T(8,128)(2,1)S(1)}) fusion(pred[2]{0:T(512)(128)(4,1)S(1)} %get-tuple-element.217, pred[2]{0:T(512)(128)(4,1)S(1)} %get-tuple-element.218, pred[]{:T(512)S(6)} %eq.44, bf16[2,2,2,24,3840]{4,3,2,1,0:T(8,128)(2,1)} %bitcast.13, ...), kind=kLoop, calls=%fused_computation.39 | loop fusion | flops 8847360 | bytes 17694726 | tf_op jit(solution)/shard_map/jit(_where)/select_n | solution.py:342
  111.3 2.9 bitcast_select_fusion.weight_ref
  114.3 3.3 %fusion.47 = (f32[1024]{0:T(1024)S(1)}, f32[1024,768]{1,0:T(8,128)S(1)}) fusion(bf16[1024,768]{1,0:T(8,128)(2,1)} %get-tuple-element.110, bf16[768,3840]{1,0:T(8,128)(2,1)} %bitcast_select_fusion.weight_ref, bf16[1,1024,768]{2,1,0:T(8,128)(2,1)S(1)} %copy-done.6), kind=kOutput, calls=%fused_computation.166 | convolution fusion | flops 1210317824 | bytes 7475200 | tf_op jit(solution)/shard_map/dot_general | solution.py:487
  119.2 1.6 copy-done.4
  122.1 12.9 %add_convert_fusion = (bf16[1024,3072]{1,0:T(8,128)(2,1)}, bf16[1024,3072]{1,0:T(8,128)(2,1)}) fusion(bf16[1024,768]{1,0:T(8,128)(2,1)S(1)} %add_convert_fusion.2, bf16[768,3840]{1,0:T(8,128)(2,1)S(1)} %copy-done.8), kind=kOutput, calls=%fused_computation.1 | convolution fusion | flops 4888461312 | bytes 18874368 | tf_op jit(solution)/shard_map/dot_general | solution.py:492
  135.0 2.0 collective-permute-done.15
  137.0 8.5 %convolution_convert_fusion.2 = bf16[3072,768]{1,0:T(8,128)(2,1)S(1)} fusion(bf16[1024,3072]{1,0:T(8,128)(2,1)} %get-tuple-element.169, bf16[1024,768]{1,0:T(8,128)(2,1)S(1)} %copy-done.19), kind=kOutput, calls=%fused_computation.9 | convolution fusion | flops 4834197504 | bytes 12582912 | tf_op jit(solution)/shard_map/dot_general | solution.py:505
  146.3 2.9 select_select_fusion.3
  149.8 9.4 %multiply_convert_fusion.grad_ref = bf16[1024,3072]{1,0:T(8,128)(2,1)S(1)} fusion(bf16[1024,3072]{1,0:T(8,128)(2,1)} %get-tuple-element.120, bf16[1024,768]{1,0:T(8,128)(2,1)} %select_bitcast_fusion.add_ref, bf16[3072,768]{1,0:T(8,128)(2,1)S(1)} %bitcast_select_fusion.1), kind=kOutput, calls=%fused_computation | convolution fusion | flops 4841275392 | bytes 18874368 | tf_op jit(solution)/shard_map/dot_general | solution.py:509
  159.2 4.0 %convert_add_fusion.1 = f32[2,2,2,2,96,768]{5,4,3,2,1,0:T(8,128)S(1)} fusion(bf16[2,2,2,2,96,768]{5,4,3,2,1,0:T(8,128)(2,1)} %collective-permute-done.18, bf16[2,2,2,2,2,96,768]{6,5,4,3,2,1,0:T(8,128)(2,1)S(1)} %bitcast.259, s32[]{:T(128)S(6)} %select_n.422), kind=kLoop, calls=%fused_computation.13 | loop fusion | flops 3538944 | bytes 9437188 | tf_op jit(solution)/shard_map/add | solution.py:357
  165.8 7.0 %convolution_convert_fusion.1 = bf16[768,3072]{1,0:T(8,128)(2,1)} fusion(bf16[1024,768]{1,0:T(8,128)(2,1)S(1)} %copy-done.21, bf16[1024,3072]{1,0:T(8,128)(2,1)S(1)} %multiply_convert_fusion.grad_ref), kind=kOutput, calls=%fused_computation.8 | convolution fusion | flops 4834197504 | bytes 12582912 | tf_op jit(solution)/shard_map/dot_general | solution.py:515
  172.8 12.0 %mlp_norm_backward.1 = (f32[1024,768]{1,0:T(8,128)}, bf16[1024,768]{1,0:T(8,128)(2,1)}, f32[8,768]{1,0:T(8,128)}) custom-call(bf16[1024,3072]{1,0:T(8,128)(2,1)} %copy-done.35, bf16[768,3840]{1,0:T(8,128)(2,1)} %bitcast_select_fusion.weight_ref, f32[1024,768]{1,0:T(8,128)} %copy-done.2, bf16[1024,768]{1,0:T(8,128)(2,1)} %select_bitcast_fusion.add_ref, ...), custom_call_target="tpu_custom_call" | custom-call | flops 9663676416 | bytes 22020096 | tf_op jit(solution)/shard_map/mlp_norm_backward/pallas_call | solution.py:271
  184.8 3.5 %convolution_convert_fusion.5 = bf16[768,768]{1,0:T(8,128)(2,1)S(1)} fusion(bf16[1024,768]{1,0:T(8,128)(2,1)} %get-tuple-element.110, bf16[1024,768]{1,0:T(8,128)(2,1)} %get-tuple-element.132), kind=kOutput, calls=%fused_computation.58 | convolution fusion | flops 1208549376 | bytes 4325376 | tf_op jit(solution)/shard_map/dot_general | solution.py:520
  188.3 1.8 dynamic-slice_bitcast_fusion.3
  192.1 4.3 %convolution_convert_fusion.4 = bf16[1024,768]{1,0:T(8,128)(2,1)} fusion(bf16[1024,768]{1,0:T(8,128)(2,1)S(1)} %copy-done.36, bf16[768,3840]{1,0:T(8,128)(2,1)} %bitcast_select_fusion.weight_ref), kind=kOutput, calls=%fused_computation.56 | convolution fusion | flops 1208745984 | bytes 4325376 | tf_op jit(solution)/shard_map/dot_general | solution.py:528
  196.4 1.5 collective-permute-start.22
  198.8 2.5 copy-done
  201.4 1.6 fusion.13
  203.3 27.0 %attend_backward.1.grad_ref = bf16[1024,2304]{1,0:T(8,128)(2,1)} custom-call(bf16[1024,2304]{1,0:T(8,128)(2,1)} %convolution_convert_fusion.project_ref, bf16[1024,768]{1,0:T(8,128)(2,1)} %convolution_convert_fusion.4, f32[16,1024]{1,0:T(8,128)} %get-tuple-element.138.lse_ref, f32[8,384,128]{2,1,0:T(8,128)} %get-tuple-element.139.bias_ref), custom_call_target="tpu_custom_call" | custom-call | flops 31708938240 | bytes 11010048 | tf_op jit(solution)/shard_map/attend_backward/pallas_call | solution.py:216
  230.4 3.7 %fusion.12 = f32[2,2,2,24,3840]{4,3,2,1,0:T(8,128)S(1)} fusion(bf16[2,2,2,24,3840]{4,3,2,1,0:T(8,128)(2,1)} %collective-permute-done.21, f32[2,2,2,2,24,3840]{5,4,3,2,1,0:T(8,128)} %copy-done, s32[]{:T(128)S(6)} %select_n.426, pred[]{:T(512)S(6)} %eq.44, s32[]{:T(128)S(6)} %select_n.427), kind=kLoop, calls=%fused_computation.33 | loop fusion | flops 2211840 | bytes 10321929 | tf_op jit(solution)/shard_map/add | solution.py:357
  234.2 1.4 collective-permute-start.23
  235.9 4.5 %convolution_convert_fusion.3 = bf16[768,2304]{1,0:T(8,128)(2,1)S(1)} fusion(bf16[1024,2304]{1,0:T(8,128)(2,1)S(1)} %copy-done.34, bf16[1,1024,768]{2,1,0:T(8,128)(2,1)S(1)} %copy-done.7, f32[768]{0:T(1024)S(1)} %copy-done.28, f32[768]{0:T(1024)S(1)} %copy-done.30, f32[1024]{0:T(1024)S(1)} %copy-done.33, f32[1024]{0:T(1024)S(1)} %copy-done.26), kind=kOutput, calls=%fused_computation.10 | convolution fusion | flops 3630366720 | bytes 9844736 | tf_op jit(solution)/shard_map/dot_general | solution.py:548
  240.4 1.9 copy-done.15
  243.6 2.2 collective-permute-done.23
  246.7 1.5 slice_reduce_fusion.3
  249.1 1.6 collective-permute-done.24
  250.7 2.0 convert_add_fusion.2
  253.9 1.6 collective-permute-start.25
  255.5 1.4 pad_maximum_fusion.4
  257.6 9.9 %attention_norm_backward.1 = (f32[1024,768]{1,0:T(8,128)}, f32[8,768]{1,0:T(8,128)}) custom-call(bf16[1024,2304]{1,0:T(8,128)(2,1)} %attend_backward.1.grad_ref, bf16[768,2432]{1,0:T(8,128)(2,1)} %copy-done.12, bf16[1024,768]{1,0:T(8,128)(2,1)} %bitcast.253, f32[1024,768]{1,0:T(8,128)} %get-tuple-element.154.add_ref, f32[1,768]{1,0:T(1,128)} %get-tuple-element.193.gain_ref), custom_call_target="tpu_custom_call" | custom-call | flops 8455716864 | bytes 19267584 | tf_op jit(solution)/shard_map/attention_norm_backward/pallas_call | solution.py:271
  267.5 1.4 fusion.16
  273.3 1.7 bitcast_add_fusion
  276.2 1.8 collective-permute-start.29
  278.0 1.8 collective-permute-start.28
  279.9 9.4 %fusion.18 = bf16[1,1024,768]{2,1,0:T(8,128)(2,1)} fusion(f32[1024,768]{1,0:T(8,128)S(1)} %copy-done.3, bf16[1024,3072]{1,0:T(8,128)(2,1)} %get-tuple-element.169, bf16[3072,768]{1,0:T(8,128)(2,1)} %copy-done.11), kind=kOutput, calls=%fused_computation.59 | convolution fusion | flops 4833411072 | bytes 15728640 | tf_op jit(solution)/shard_map/dot_general | solution.py:599
  289.3 2.0 collective-permute-done.28
  292.2 1.4 collective-permute-start.34
  298.0 1.5 collective-permute-done.35
  300.5 2.8 collective-permute-start.33
  303.3 1.8 collective-permute-start.37
  305.9 3.4 %collective-permute-done.37 = f32[1,128]{1,0:T(1,128)S(1)} collective-permute-done((f32[1,128]{1,0:T(1,128)S(1)}, f32[1,128]{1,0:T(1,128)S(1)}, u32[]{:S(2)}, u32[]{:S(2)}) %collective-permute-start.37) | collective-permute-done | bytes 544 | tf_op jit(solution)/shard_map/ppermute | solution.py:302
  314.0 4.4 %collective-permute-done.32 = bf16[24,2304]{1,0:T(8,128)(2,1)S(1)} collective-permute-done((bf16[24,2304]{1,0:T(8,128)(2,1)S(1)}, bf16[24,2304]{1,0:T(8,128)(2,1)S(1)}, u32[]{:S(2)}, u32[]{:S(2)}) %collective-permute-start.32) | collective-permute-done | bytes 110624 | tf_op jit(solution)/shard_map/ppermute | solution.py:302
  (213 shorter events, 43.5 us)
Async XLA Ops:
  0.6 34.7 %copy-start.6 = (bf16[1,1024,768]{2,1,0:T(8,128)(2,1)S(1)}, bf16[1,1024,768]{2,1,0:T(8,128)(2,1)}, u32[]{:S(2)}) copy-start(bf16[1,1024,768]{2,1,0:T(8,128)(2,1)} %param.12) | copy-start | bytes 4718596
  2.5 9.8 %collective-permute-start = (bf16[24,2432]{1,0:T(8,128)(2,1)S(1)}, bf16[24,2432]{1,0:T(8,128)(2,1)S(1)}, u32[]{:S(2)}, u32[]{:S(2)}) collective-permute-start(bf16[24,2432]{1,0:T(8,128)(2,1)S(1)} %fusion.30), channel_id=1, source_target_pairs={{0,8},{1,9},{2,10},{3,11},{4,12},{5,13},{6,14},{7,15},{8,0},{9,1},... | collective-permute-start | bytes 350216 | tf_op jit(solution)/shard_map/ppermute | solution.py:302
  12.5 6.9 %collective-permute-start.1 = (bf16[2,24,2432]{2,1,0:T(8,128)(2,1)S(1)}, bf16[2,24,2432]{2,1,0:T(8,128)(2,1)S(1)}, u32[]{:S(2)}, u32[]{:S(2)}) collective-permute-start(bf16[2,24,2432]{2,1,0:T(8,128)(2,1)S(1)} %broadcast_select_fusion.8), channel_id=1, source_target_pairs={{0,4},{1,5},{2,6},{3,7},{4,0},{5,1},{6,2},{7,3},{8,12},{9,13},{10,... | collective-permute-start | bytes 700424 | tf_op jit(solution)/shard_map/ppermute | solution.py:302
  21.3 11.3 %collective-permute-start.3 = (bf16[24,3840]{1,0:T(8,128)(2,1)S(1)}, bf16[24,3840]{1,0:T(8,128)(2,1)S(1)}, u32[]{:S(2)}, u32[]{:S(2)}) collective-permute-start(bf16[24,3840]{1,0:T(8,128)(2,1)S(1)} %constant_dynamic-update-slice_fusion), channel_id=1, source_target_pairs={{0,8},{1,9},{2,10},{3,11},{4,12},{5,13},{6,14},{7,15},{8,0},{9,1},... | collective-permute-start | bytes 552968 | tf_op jit(solution)/shard_map/ppermute | solution.py:302
  24.4 9.0 %collective-permute-start.2 = (bf16[2,2,24,2432]{3,2,1,0:T(8,128)(2,1)S(1)}, bf16[2,2,24,2432]{3,2,1,0:T(8,128)(2,1)S(1)}, u32[]{:S(2)}, u32[]{:S(2)}) collective-permute-start(bf16[2,2,24,2432]{3,2,1,0:T(8,128)(2,1)S(1)} %broadcast_select_fusion.5), channel_id=1, source_target_pairs={{0,16},{1,3},{2,18},{3,1},{4,20},{5,7},{6,22},{7,5},{8,24},{9,11},... | collective-permute-start | bytes 1400840 | tf_op jit(solution)/shard_map/ppermute | solution.py:302
  33.8 13.6 %collective-permute-start.4 = (bf16[2,2,2,24,2432]{4,3,0,2,1:T(8,128)(2,1)S(1)}, bf16[2,2,2,24,2432]{4,3,0,2,1:T(8,128)(2,1)S(1)}, u32[]{:S(2)}, u32[]{:S(2)}) collective-permute-start(bf16[2,2,2,24,2432]{4,3,0,2,1:T(8,128)(2,1)S(1)} %broadcast_select_fusion.2), channel_id=1, source_target_pairs={{0,2},{1,17},{2,0},{3,19},{4,6},{5,21},{6,4},{7,23},{8,10},{9,25},... | collective-permute-start | bytes 2801672 | tf_op jit(solution)/shard_map/ppermute | solution.py:302
  35.6 21.7 %copy-start.25 = (f32[1024]{0:T(1024)}, f32[1024]{0:T(1024)S(1)}, u32[]{:S(2)}) copy-start(f32[1024]{0:T(1024)S(1)} %broadcast_multiply_fusion.1) | copy-start | bytes 12292
  36.3 11.1 %collective-permute-start.7 = (bf16[2,24,3840]{2,1,0:T(8,128)(2,1)}, bf16[2,24,3840]{2,1,0:T(8,128)(2,1)}, u32[]{:S(2)}, u32[]{:S(2)}) collective-permute-start(bf16[2,24,3840]{2,1,0:T(8,128)(2,1)} %broadcast_select_fusion.6), channel_id=1, source_target_pairs={{0,4},{1,5},{2,6},{3,7},{4,0},{5,1},{6,2},{7,3},{8,12},{9,13},{10,... | collective-permute-start | bytes 1105928 | tf_op jit(solution)/shard_map/ppermute | solution.py:302
  38.5 18.9 %copy-start.32 = (f32[1024]{0:T(1024)}, f32[1024]{0:T(1024)S(1)}, u32[]{:S(2)}) copy-start(f32[1024]{0:T(1024)S(1)} %add_rsqrt_fusion.1) | copy-start | bytes 12292
  38.5 11.0 %collective-permute-start.5 = (bf16[2,2,2,24,2432]{4,3,0,2,1:T(8,128)(2,1)S(1)}, bf16[2,2,2,24,2432]{4,3,0,2,1:T(8,128)(2,1)S(1)}, u32[]{:S(2)}, u32[]{:S(2)}) collective-permute-start(bf16[2,2,2,24,2432]{4,3,0,2,1:T(8,128)(2,1)S(1)} %broadcast_select_fusion.2), channel_id=1, source_target_pairs={{0,1},{1,0},{2,3},{3,2},{4,5},{5,4},{6,7},{7,6},{8,9},{9,8},{10,11... | collective-permute-start | bytes 2801672 | tf_op jit(solution)/shard_map/ppermute | solution.py:302
  47.4 2.5 collective-permute-start.6
  53.2 12.1 %collective-permute-start.9 = (bf16[96,768]{1,0:T(8,128)(2,1)S(1)}, bf16[96,768]{1,0:T(8,128)(2,1)S(1)}, u32[]{:S(2)}, u32[]{:S(2)}) collective-permute-start(bf16[96,768]{1,0:T(8,128)(2,1)S(1)} %copy-done.24), channel_id=1, source_target_pairs={{0,8},{1,9},{2,10},{3,11},{4,12},{5,13},{6,14},{7,15},{8,0},{9,1},... | collective-permute-start | bytes 442376 | tf_op jit(solution)/shard_map/ppermute | solution.py:302
  55.8 9.5 %copy-start.27 = (f32[768]{0:T(1024)}, f32[768]{0:T(1024)S(1)}, u32[]{:S(2)}) copy-start(f32[768]{0:T(1024)S(1)} %get-tuple-element.195) | copy-start | bytes 9220
  55.8 9.5 %copy-start.29 = (f32[768]{0:T(1024)}, f32[768]{0:T(1024)S(1)}, u32[]{:S(2)}) copy-start(f32[768]{0:T(1024)S(1)} %get-tuple-element.197) | copy-start | bytes 9220
  55.8 11.5 %collective-permute-start.8 = (bf16[2,2,24,3840]{3,2,1,0:T(8,128)(2,1)S(1)}, bf16[2,2,24,3840]{3,2,1,0:T(8,128)(2,1)S(1)}, u32[]{:S(2)}, u32[]{:S(2)}) collective-permute-start(bf16[2,2,24,3840]{3,2,1,0:T(8,128)(2,1)S(1)} %copy-done.17), channel_id=1, source_target_pairs={{0,16},{1,3},{2,18},{3,1},{4,20},{5,7},{6,22},{7,5},{8,24},{9,11},... | collective-permute-start | bytes 2211848 | tf_op jit(solution)/shard_map/ppermute | solution.py:302
  57.4 10.0 %copy-start.18 = (bf16[2,2,24,3840]{3,2,1,0:T(8,128)(2,1)S(1)}, bf16[2,2,24,3840]{3,2,1,0:T(8,128)(2,1)}, u32[]{:S(2)}) copy-start(bf16[2,2,24,3840]{3,2,1,0:T(8,128)(2,1)} %broadcast_select_fusion.3) | copy-start | bytes 2211844
  67.5 26.6 %copy-start.31 = (s32[1,1024]{1,0:T(1,128)S(1)}, s32[1,1024]{1,0:T(1,128)}, u32[]{:S(2)}) copy-start(s32[1,1024]{1,0:T(1,128)} %seg_ref.1) | copy-start | bytes 12292
  67.5 24.8 %collective-permute-start.11 = (bf16[2,2,2,24,3840]{4,3,0,2,1:T(8,128)(2,1)S(1)}, bf16[2,2,2,24,3840]{4,3,0,2,1:T(8,128)(2,1)}, u32[]{:S(2)}, u32[]{:S(2)}) collective-permute-start(bf16[2,2,2,24,3840]{4,3,0,2,1:T(8,128)(2,1)S(1)} %broadcast_select_fusion), channel_id=1, source_target_pairs={{0,1},{1,0},{2,3},{3,2},{4,5},{5,4},{6,7},{7,6},{8,9},{9,8},{10,11... | collective-permute-start | bytes 4423688 | tf_op jit(solution)/shard_map/ppermute | solution.py:302
  67.6 24.7 %collective-permute-start.10 = (bf16[2,2,2,24,3840]{4,3,0,2,1:T(8,128)(2,1)S(1)}, bf16[2,2,2,24,3840]{4,3,0,2,1:T(8,128)(2,1)}, u32[]{:S(2)}, u32[]{:S(2)}) collective-permute-start(bf16[2,2,2,24,3840]{4,3,0,2,1:T(8,128)(2,1)S(1)} %broadcast_select_fusion), channel_id=1, source_target_pairs={{0,2},{1,17},{2,0},{3,19},{4,6},{5,21},{6,4},{7,23},{8,10},{9,25},... | collective-permute-start | bytes 4423688 | tf_op jit(solution)/shard_map/ppermute | solution.py:302
  69.2 21.2 %collective-permute-start.12 = (bf16[2,96,768]{2,1,0:T(8,128)(2,1)S(1)}, bf16[2,96,768]{2,1,0:T(8,128)(2,1)}, u32[]{:S(2)}, u32[]{:S(2)}) collective-permute-start(bf16[2,96,768]{2,1,0:T(8,128)(2,1)S(1)} %broadcast_select_fusion.7), channel_id=1, source_target_pairs={{0,4},{1,5},{2,6},{3,7},{4,0},{5,1},{6,2},{7,3},{8,12},{9,13},{10,... | collective-permute-start | bytes 884744 | tf_op jit(solution)/shard_map/ppermute | solution.py:302
  92.4 12.7 %collective-permute-start.13 = (bf16[2,2,2,24,3840]{4,3,0,2,1:T(8,128)(2,1)}, bf16[2,2,2,24,3840]{4,3,0,2,1:T(8,128)(2,1)}, u32[]{:S(2)}, u32[]{:S(2)}) collective-permute-start(bf16[2,2,2,24,3840]{4,3,0,2,1:T(8,128)(2,1)} %collective-permute-done.10), channel_id=1, source_target_pairs={{0,1},{1,0},{2,3},{3,2},{4,5},{5,4},{6,7},{7,6},{8,9},{9,8},{10,11... | collective-permute-start | bytes 4423688 | tf_op jit(solution)/shard_map/ppermute | solution.py:302
  92.4 10.3 %collective-permute-start.14 = (bf16[2,2,96,768]{3,2,1,0:T(8,128)(2,1)}, bf16[2,2,96,768]{3,2,1,0:T(8,128)(2,1)}, u32[]{:S(2)}, u32[]{:S(2)}) collective-permute-start(bf16[2,2,96,768]{3,2,1,0:T(8,128)(2,1)} %broadcast_select_fusion.4), channel_id=1, source_target_pairs={{0,16},{1,3},{2,18},{3,1},{4,20},{5,7},{6,22},{7,5},{8,24},{9,11},... | collective-permute-start | bytes 1769480 | tf_op jit(solution)/shard_map/ppermute | solution.py:302
  117.6 4.5 %copy-start.8 = (bf16[768,3840]{1,0:T(8,128)(2,1)S(1)}, bf16[768,3840]{1,0:T(8,128)(2,1)}, u32[]{:S(2)}) copy-start(bf16[768,3840]{1,0:T(8,128)(2,1)} %bitcast_select_fusion.weight_ref) | copy-start | bytes 17694724
  120.8 14.2 %copy-start.20 = (bf16[1024,768]{1,0:T(8,128)(2,1)}, bf16[1024,768]{1,0:T(8,128)(2,1)S(1)}, u32[]{:S(2)}) copy-start(bf16[1024,768]{1,0:T(8,128)(2,1)S(1)} %add_convert_fusion.2) | copy-start | bytes 4718596
  120.8 16.2 %copy-start.19 = (bf16[1024,768]{1,0:T(8,128)(2,1)S(1)}, bf16[1024,768]{1,0:T(8,128)(2,1)}, u32[]{:S(2)}) copy-start(bf16[1024,768]{1,0:T(8,128)(2,1)} %select_bitcast_fusion.add_ref) | copy-start | bytes 4718596
  120.8 14.2 %collective-permute-start.16 = (bf16[2,2,2,96,768]{4,3,2,1,0:T(8,128)(2,1)S(1)}, bf16[2,2,2,96,768]{4,3,2,1,0:T(8,128)(2,1)S(1)}, u32[]{:S(2)}, u32[]{:S(2)}) collective-permute-start(bf16[2,2,2,96,768]{4,3,2,1,0:T(8,128)(2,1)S(1)} %copy-done.4), channel_id=1, source_target_pairs={{0,1},{1,0},{2,3},{3,2},{4,5},{5,4},{6,7},{7,6},{8,9},{9,8},{10,11... | collective-permute-start | bytes 3538952 | tf_op jit(solution)/shard_map/ppermute | solution.py:302
  120.8 16.2 %collective-permute-start.15 = (bf16[2,2,2,96,768]{4,3,2,1,0:T(8,128)(2,1)S(1)}, bf16[2,2,2,96,768]{4,3,2,1,0:T(8,128)(2,1)S(1)}, u32[]{:S(2)}, u32[]{:S(2)}) collective-permute-start(bf16[2,2,2,96,768]{4,3,2,1,0:T(8,128)(2,1)S(1)} %copy-done.4), channel_id=1, source_target_pairs={{0,2},{1,17},{2,0},{3,19},{4,6},{5,21},{6,4},{7,23},{8,10},{9,25},... | collective-permute-start | bytes 3538952 | tf_op jit(solution)/shard_map/ppermute | solution.py:302
  137.0 9.3 %collective-permute-start.17 = (bf16[2,2,2,96,768]{4,3,2,1,0:T(8,128)(2,1)S(1)}, bf16[2,2,2,96,768]{4,3,2,1,0:T(8,128)(2,1)S(1)}, u32[]{:S(2)}, u32[]{:S(2)}) collective-permute-start(bf16[2,2,2,96,768]{4,3,2,1,0:T(8,128)(2,1)S(1)} %collective-permute-done.15), channel_id=1, source_target_pairs={{0,1},{1,0},{2,3},{3,2},{4,5},{5,4},{6,7},{7,6},{8,9},{9,8},{10,11... | collective-permute-start | bytes 3538952 | tf_op jit(solution)/shard_map/ppermute | solution.py:302
  145.7 13.5 %collective-permute-start.18 = (bf16[2,2,2,2,96,768]{5,4,3,2,1,0:T(8,128)(2,1)S(1)}, bf16[2,2,2,2,96,768]{5,4,3,2,1,0:T(8,128)(2,1)}, u32[]{:S(2)}, u32[]{:S(2)}) collective-permute-start(bf16[2,2,2,2,96,768]{5,4,3,2,1,0:T(8,128)(2,1)S(1)} %dynamic-slice_bitcast_fusion.4), channel_id=1, source_target_pairs={{0,1},{1,0},{2,3},{3,2},{4,5},{5,4},{6,7},{7,6},{8,9},{9,8},{10,11... | collective-permute-start | bytes 7077896 | tf_op jit(solution)/shard_map/ppermute | solution.py:302
  149.8 9.4 %copy-start.11 = (bf16[3072,768]{1,0:T(8,128)(2,1)}, bf16[3072,768]{1,0:T(8,128)(2,1)S(1)}, u32[]{:S(2)}) copy-start(bf16[3072,768]{1,0:T(8,128)(2,1)S(1)} %bitcast_select_fusion.1) | copy-start | bytes 14155780
  159.2 5.7 %copy-start.35 = (bf16[1024,3072]{1,0:T(8,128)(2,1)}, bf16[1024,3072]{1,0:T(8,128)(2,1)S(1)}, u32[]{:S(2)}) copy-start(bf16[1024,3072]{1,0:T(8,128)(2,1)S(1)} %multiply_convert_fusion.grad_ref) | copy-start | bytes 18874372
  163.2 9.6 %copy-start.1 = (f32[2,2,2,2,96,768]{5,4,3,2,1,0:T(8,128)}, f32[2,2,2,2,96,768]{5,4,3,2,1,0:T(8,128)S(1)}, u32[]{:S(2)}) copy-start(f32[2,2,2,2,96,768]{5,4,3,2,1,0:T(8,128)S(1)} %convert_add_fusion.1) | copy-start | bytes 14155780
  163.5 26.6 %collective-permute-start.19 = (bf16[2,2,2,96,768]{4,3,1,2,0:T(8,128)(2,1)S(1)}, bf16[2,2,2,96,768]{4,3,1,2,0:T(8,128)(2,1)S(1)}, u32[]{:S(2)}, u32[]{:S(2)}) collective-permute-start(bf16[2,2,2,96,768]{4,3,1,2,0:T(8,128)(2,1)S(1)} %fusion.15), channel_id=1, source_target_pairs={{0,2},{1,17},{2,0},{3,19},{4,6},{5,21},{6,4},{7,23},{8,10},{9,25},... | collective-permute-start | bytes 3538952 | tf_op jit(solution)/shard_map/ppermute | solution.py:302
  184.8 5.4 %slice-start = ((s8[4718592]{0:T(1024)(128)(4,1)}), s8[4194304]{0:T(1024)(128)(4,1)S(1)}, s32[]{:S(2)}) async-start(s8[4718592]{0:T(1024)(128)(4,1)} %bitcast.249), calls=%async_computation | async-start | bytes 8388608
  184.8 5.4 %slice-start.1 = ((s8[4718592]{0:T(1024)(128)(4,1)}), s8[524288]{0:T(1024)(128)(4,1)S(1)}, s32[]{:S(2)}) async-start(s8[4718592]{0:T(1024)(128)(4,1)} %bitcast.249), calls=%async_computation.1 | async-start | bytes 1048576
  190.7 7.2 %slice-start.2 = ((s8[4718592]{0:T(1024)(128)(4,1)}), s8[524288]{0:T(1024)(128)(4,1)S(1)}, s32[]{:S(2)}) async-start(s8[4718592]{0:T(1024)(128)(4,1)} %bitcast.255), calls=%async_computation.2 | async-start | bytes 1048576
  190.9 7.0 %slice-start.3 = ((s8[4718592]{0:T(1024)(128)(4,1)}), s8[4194304]{0:T(1024)(128)(4,1)S(1)}, s32[]{:S(2)}) async-start(s8[4718592]{0:T(1024)(128)(4,1)} %bitcast.255), calls=%async_computation.3 | async-start | bytes 8388608
  190.9 7.2 %collective-permute-start.20 = (bf16[2,2,2,2,24,3840]{5,4,3,2,1,0:T(8,128)(2,1)S(1)}, bf16[2,2,2,2,24,3840]{5,4,3,2,1,0:T(8,128)(2,1)S(1)}, u32[]{:S(2)}, u32[]{:S(2)}) collective-permute-start(bf16[2,2,2,2,24,3840]{5,4,3,2,1,0:T(8,128)(2,1)S(1)} %pad_maximum_fusion), channel_id=1, source_target_pairs={{0,1},{1,0},{2,3},{3,2},{4,5},{5,4},{6,7},{7,6},{8,9},{9,8},{10,11... | collective-permute-start | bytes 8847368 | tf_op jit(solution)/shard_map/ppermute | solution.py:302
  196.4 34.1 %collective-permute-start.22 = (bf16[2,2,96,768]{3,2,0,1:T(8,128)(2,1)S(1)}, bf16[2,2,96,768]{3,2,0,1:T(8,128)(2,1)S(1)}, u32[]{:S(2)}, u32[]{:S(2)}) collective-permute-start(bf16[2,2,96,768]{3,2,0,1:T(8,128)(2,1)S(1)} %fusion.22), channel_id=1, source_target_pairs={{0,16},{1,3},{2,18},{3,1},{4,20},{5,7},{6,22},{7,5},{8,24},{9,11},... | collective-permute-start | bytes 1769480 | tf_op jit(solution)/shard_map/ppermute | solution.py:302
  202.9 27.5 %collective-permute-start.21 = (bf16[2,2,2,24,3840]{4,3,2,1,0:T(8,128)(2,1)}, bf16[2,2,2,24,3840]{4,3,2,1,0:T(8,128)(2,1)}, u32[]{:S(2)}, u32[]{:S(2)}) collective-permute-start(bf16[2,2,2,24,3840]{4,3,2,1,0:T(8,128)(2,1)} %fusion.13), channel_id=1, source_target_pairs={{0,2},{1,17},{2,0},{3,19},{4,6},{5,21},{6,4},{7,23},{8,10},{9,25},... | collective-permute-start | bytes 4423688 | tf_op jit(solution)/shard_map/ppermute | solution.py:302
  230.4 5.3 %copy-start.7 = (bf16[1,1024,768]{2,1,0:T(8,128)(2,1)S(1)}, bf16[1,1024,768]{2,1,0:T(8,128)(2,1)}, u32[]{:S(2)}) copy-start(bf16[1,1024,768]{2,1,0:T(8,128)(2,1)} %param.12) | copy-start | bytes 4718596
  230.4 5.3 %copy-start.26 = (f32[1024]{0:T(1024)S(1)}, f32[1024]{0:T(1024)}, u32[]{:S(2)}) copy-start(f32[1024]{0:T(1024)} %copy-done.25) | copy-start | bytes 12292
  230.4 5.3 %copy-start.28 = (f32[768]{0:T(1024)S(1)}, f32[768]{0:T(1024)}, u32[]{:S(2)}) copy-start(f32[768]{0:T(1024)} %copy-done.27) | copy-start | bytes 9220
  230.4 5.3 %copy-start.30 = (f32[768]{0:T(1024)S(1)}, f32[768]{0:T(1024)}, u32[]{:S(2)}) copy-start(f32[768]{0:T(1024)} %copy-done.29) | copy-start | bytes 9220
  230.4 5.3 %copy-start.33 = (f32[1024]{0:T(1024)S(1)}, f32[1024]{0:T(1024)}, u32[]{:S(2)}) copy-start(f32[1024]{0:T(1024)} %copy-done.32) | copy-start | bytes 12292
  230.4 5.5 %copy-start.34 = (bf16[1024,2304]{1,0:T(8,128)(2,1)S(1)}, bf16[1024,2304]{1,0:T(8,128)(2,1)}, u32[]{:S(2)}) copy-start(bf16[1024,2304]{1,0:T(8,128)(2,1)} %attend_backward.1.grad_ref) | copy-start | bytes 14155780
  234.1 6.3 %copy-start.5 = (f32[2,2,2,24,3840]{4,3,2,1,0:T(8,128)}, f32[2,2,2,24,3840]{4,3,2,1,0:T(8,128)S(1)}, u32[]{:S(2)}) copy-start(f32[2,2,2,24,3840]{4,3,2,1,0:T(8,128)S(1)} %fusion.12) | copy-start | bytes 8847364
  234.2 11.5 %collective-permute-start.23 = (bf16[2,2,24,3840]{3,2,1,0:T(8,128)(2,1)S(1)}, bf16[2,2,24,3840]{3,2,1,0:T(8,128)(2,1)S(1)}, u32[]{:S(2)}, u32[]{:S(2)}) collective-permute-start(bf16[2,2,24,3840]{3,2,1,0:T(8,128)(2,1)S(1)} %fusion.21), channel_id=1, source_target_pairs={{0,16},{1,3},{2,18},{3,1},{4,20},{5,7},{6,22},{7,5},{8,24},{9,11},... | collective-permute-start | bytes 2211848 | tf_op jit(solution)/shard_map/ppermute | solution.py:302
  246.7 4.0 %collective-permute-start.24 = (bf16[2,2,2,2,24,2304]{5,4,3,2,1,0:T(8,128)(2,1)}, bf16[2,2,2,2,24,2304]{5,4,3,2,1,0:T(8,128)(2,1)}, u32[]{:S(2)}, u32[]{:S(2)}) collective-permute-start(bf16[2,2,2,2,24,2304]{5,4,3,2,1,0:T(8,128)(2,1)} %dynamic-slice_bitcast_fusion.5), channel_id=1, source_target_pairs={{0,1},{1,0},{2,3},{3,2},{4,5},{5,4},{6,7},{7,6},{8,9},{9,8},{10,11... | collective-permute-start | bytes 5308424 | tf_op jit(solution)/shard_map/ppermute | solution.py:302
  253.9 13.6 %collective-permute-start.25 = (bf16[2,2,2,24,2304]{4,3,1,2,0:T(8,128)(2,1)}, bf16[2,2,2,24,2304]{4,3,1,2,0:T(8,128)(2,1)}, u32[]{:S(2)}, u32[]{:S(2)}) collective-permute-start(bf16[2,2,2,24,2304]{4,3,1,2,0:T(8,128)(2,1)} %fusion.17), channel_id=1, source_target_pairs={{0,2},{1,17},{2,0},{3,19},{4,6},{5,21},{6,4},{7,23},{8,10},{9,25},... | collective-permute-start | bytes 2654216 | tf_op jit(solution)/shard_map/ppermute | solution.py:302
  257.6 9.9 %collective-permute-start.26 = (bf16[2,96,768]{2,1,0:T(8,128)(2,1)}, bf16[2,96,768]{2,1,0:T(8,128)(2,1)}, u32[]{:S(2)}, u32[]{:S(2)}) collective-permute-start(bf16[2,96,768]{2,1,0:T(8,128)(2,1)} %fusion.25), channel_id=1, source_target_pairs={{0,4},{1,5},{2,6},{3,7},{4,0},{5,1},{6,2},{7,3},{8,12},{9,13},{10,... | collective-permute-start | bytes 884744 | tf_op jit(solution)/shard_map/ppermute | solution.py:302
  272.1 7.8 %copy-start.3 = (f32[1024,768]{1,0:T(8,128)S(1)}, f32[1024,768]{1,0:T(8,128)}, u32[]{:S(2)}) copy-start(f32[1024,768]{1,0:T(8,128)} %copy-done.2) | copy-start | bytes 9437188
  272.1 19.9 %collective-permute-start.27 = (bf16[2,2,24,2304]{3,2,0,1:T(8,128)(2,1)}, bf16[2,2,24,2304]{3,2,0,1:T(8,128)(2,1)S(1)}, u32[]{:S(2)}, u32[]{:S(2)}) collective-permute-start(bf16[2,2,24,2304]{3,2,0,1:T(8,128)(2,1)} %fusion.23), channel_id=1, source_target_pairs={{0,16},{1,3},{2,18},{3,1},{4,20},{5,7},{6,22},{7,5},{8,24},{9,11},... | collective-permute-start | bytes 1327112 | tf_op jit(solution)/shard_map/ppermute | solution.py:302
  276.1 15.9 %copy-start.10 = (f32[2,2,2,24,2304]{4,3,1,2,0:T(8,128)S(1)}, f32[2,2,2,24,2304]{4,3,1,2,0:T(8,128)}, u32[]{:S(2)}) copy-start(f32[2,2,2,24,2304]{4,3,1,2,0:T(8,128)} %copy-done.9) | copy-start | bytes 5308420
  276.1 13.1 %collective-permute-start.30 = (f32[2,2,2,2,1,128]{5,3,2,1,4,0:T(2,128)S(1)}, f32[2,2,2,2,1,128]{5,3,2,1,4,0:T(2,128)S(1)}, u32[]{:S(2)}, u32[]{:S(2)}) collective-permute-start(f32[2,2,2,2,1,128]{5,3,2,1,4,0:T(2,128)S(1)} %bitcast.274), channel_id=1, source_target_pairs={{0,1},{1,0},{2,3},{3,2},{4,5},{5,4},{6,7},{7,6},{8,9},{9,8},{10,11... | collective-permute-start | bytes 24584 | tf_op jit(solution)/shard_map/ppermute | solution.py:302
  276.2 13.1 %collective-permute-start.29 = (bf16[96,768]{1,0:T(8,128)(2,1)S(1)}, bf16[96,768]{1,0:T(8,128)(2,1)S(1)}, u32[]{:S(2)}, u32[]{:S(2)}) collective-permute-start(bf16[96,768]{1,0:T(8,128)(2,1)S(1)} %fusion.29), channel_id=1, source_target_pairs={{0,8},{1,9},{2,10},{3,11},{4,12},{5,13},{6,14},{7,15},{8,0},{9,1},... | collective-permute-start | bytes 442376 | tf_op jit(solution)/shard_map/ppermute | solution.py:302
  278.0 13.2 %collective-permute-start.28 = (bf16[2,24,3840]{2,1,0:T(8,128)(2,1)S(1)}, bf16[2,24,3840]{2,1,0:T(8,128)(2,1)S(1)}, u32[]{:S(2)}, u32[]{:S(2)}) collective-permute-start(bf16[2,24,3840]{2,1,0:T(8,128)(2,1)S(1)} %fusion.24), channel_id=1, source_target_pairs={{0,4},{1,5},{2,6},{3,7},{4,0},{5,1},{6,2},{7,3},{8,12},{9,13},{10,... | collective-permute-start | bytes 1105928 | tf_op jit(solution)/shard_map/ppermute | solution.py:302
  292.2 3.7 %collective-permute-start.34 = (f32[2,2,2,1,128]{4,2,1,0,3:T(2,128)S(1)}, f32[2,2,2,1,128]{4,2,1,0,3:T(2,128)S(1)}, u32[]{:S(2)}, u32[]{:S(2)}) collective-permute-start(f32[2,2,2,1,128]{4,2,1,0,3:T(2,128)S(1)} %bitcast_select_fusion.10), channel_id=1, source_target_pairs={{0,2},{1,17},{2,0},{3,19},{4,6},{5,21},{6,4},{7,23},{8,10},{9,25},... | collective-permute-start | bytes 12296 | tf_op jit(solution)/shard_map/ppermute | solution.py:302
  293.7 18.2 %collective-permute-start.31 = (bf16[2,24,2304]{2,1,0:T(8,128)(2,1)S(1)}, bf16[2,24,2304]{2,1,0:T(8,128)(2,1)S(1)}, u32[]{:S(2)}, u32[]{:S(2)}) collective-permute-start(bf16[2,24,2304]{2,1,0:T(8,128)(2,1)S(1)} %fusion.27), channel_id=1, source_target_pairs={{0,4},{1,5},{2,6},{3,7},{4,0},{5,1},{6,2},{7,3},{8,12},{9,13},{10,... | collective-permute-start | bytes 663560 | tf_op jit(solution)/shard_map/ppermute | solution.py:302
  295.9 3.6 %collective-permute-start.35 = (f32[2,2,1,128]{3,1,0,2:T(2,128)S(1)}, f32[2,2,1,128]{3,1,0,2:T(2,128)S(1)}, u32[]{:S(2)}, u32[]{:S(2)}) collective-permute-start(f32[2,2,1,128]{3,1,0,2:T(2,128)S(1)} %fusion.36), channel_id=1, source_target_pairs={{0,16},{1,3},{2,18},{3,1},{4,20},{5,7},{6,22},{7,5},{8,24},{9,11},... | collective-permute-start | bytes 6152 | tf_op jit(solution)/shard_map/ppermute | solution.py:302
  299.6 3.8 %collective-permute-start.36 = (f32[2,1,128]{2,1,0:T(1,128)S(1)}, f32[2,1,128]{2,1,0:T(1,128)S(1)}, u32[]{:S(2)}, u32[]{:S(2)}) collective-permute-start(f32[2,1,128]{2,1,0:T(1,128)S(1)} %fusion.39), channel_id=1, source_target_pairs={{0,4},{1,5},{2,6},{3,7},{4,0},{5,1},{6,2},{7,3},{8,12},{9,13},{10,... | collective-permute-start | bytes 3080 | tf_op jit(solution)/shard_map/ppermute | solution.py:302
  300.5 12.1 %collective-permute-start.33 = (bf16[24,3840]{1,0:T(8,128)(2,1)S(1)}, bf16[24,3840]{1,0:T(8,128)(2,1)S(1)}, u32[]{:S(2)}, u32[]{:S(2)}) collective-permute-start(bf16[24,3840]{1,0:T(8,128)(2,1)S(1)} %fusion.28), channel_id=1, source_target_pairs={{0,8},{1,9},{2,10},{3,11},{4,12},{5,13},{6,14},{7,15},{8,0},{9,1},... | collective-permute-start | bytes 552968 | tf_op jit(solution)/shard_map/ppermute | solution.py:302
  303.3 5.9 %collective-permute-start.37 = (f32[1,128]{1,0:T(1,128)S(1)}, f32[1,128]{1,0:T(1,128)S(1)}, u32[]{:S(2)}, u32[]{:S(2)}) collective-permute-start(f32[1,128]{1,0:T(1,128)S(1)} %fusion.42), channel_id=1, source_target_pairs={{0,8},{1,9},{2,10},{3,11},{4,12},{5,13},{6,14},{7,15},{8,0},{9,1},... | collective-permute-start | bytes 1544 | tf_op jit(solution)/shard_map/ppermute | solution.py:302
  311.9 6.6 %collective-permute-start.32 = (bf16[24,2304]{1,0:T(8,128)(2,1)S(1)}, bf16[24,2304]{1,0:T(8,128)(2,1)S(1)}, u32[]{:S(2)}, u32[]{:S(2)}) collective-permute-start(bf16[24,2304]{1,0:T(8,128)(2,1)S(1)} %fusion.31), channel_id=1, source_target_pairs={{0,8},{1,9},{2,10},{3,11},{4,12},{5,13},{6,14},{7,15},{8,0},{9,1},... | collective-permute-start | bytes 331784 | tf_op jit(solution)/shard_map/ppermute | solution.py:302
  (15 other events, 31.5 us)
